TPU v7x, 512 devices: a whole 4x4x16 slice. The times are simulated.
512 devices in a mesh: ctx: 64 (over z, y), head: 8 (over x, core).
Axes of the slice: x: 4, y: 4, z: 16, core: 2. Of those that a mesh axis runs over, the one named last changes fastest.
Arguments:
- query: bfloat16 [65536, 1024], P(('ctx', 'head')), may hold values from -40 to 40
- key_in: bfloat16 [65536, 1024], P(('ctx', 'head')), may hold values from -9 to 9
- value_in: bfloat16 [65536, 1024], P(('ctx', 'head')), may hold values from -6 to 6
- grad_out: bfloat16 [65536, 1024], P(('ctx', 'head')), may hold values from -6 to 6
- random_blocks: int32 [1024, 8, 3], P('ctx', 'head'), may hold values from 0 to 1023, as said below
- universal_segment_indices: int32 [2], replicated, may hold values from 0 to 1023, as said below
Outputs:
- head_results: bfloat16 [65536, 1024], P('ctx', 'head')
- asker_derivative: bfloat16 [65536, 1024], P('ctx', 'head')
- grad_key: bfloat16 [65536, 1024], P('ctx', 'head')
- grad_value: bfloat16 [65536, 1024], P('ctx', 'head')
Inputs may be any that keep to these rules, and one draw needn't show every extreme that they name: `random_blocks`: within one device's share of the lists (16 query blocks, 1 head) at most 2 entries name blocks of one index c of ctx (blocks c * 16 to c * 16 + 15), and in every share some index gets exactly 2. `universal_segment_indices`: the global blocks are different, and one of them is the last block 1023.
All inputs are finite; a program needn't handle non-finite values.
Results may differ from a plain program's by a relative error of at most 0.0075.
Values may be sent and summed in bfloat16 or wider, within the bound.
No kernel may reach another device: no remote copies, remote signals or barrier semaphores. Data moves between devices by JAX's collectives and lax.ppermute only.
A program may use at most 128 MiB of HBM per device.

v0:
```python
import jax
import jax.numpy as jnp
from jax import lax
from jax.sharding import Mesh
from jax.sharding import PartitionSpec as P

FEATURE_LENGTH = 128
SPAN_TOKENS = 64
RANDOM = 3
WORLDWIDE_COUNT = 2
CTX = ("ctx_0", "ctx_1")
CTX_HEAD = ("ctx_0", "ctx_1", "head")


def extended(cells, sides, width):
    for axis, dim in sides:
        count = lax.axis_size(axis)
        ends = count - 1
        head = lax.slice_in_dim(cells, 0, width, axis=dim)
        tail = lax.slice_in_dim(cells, cells.shape[dim] - width, cells.shape[dim], axis=dim)
        cells = jnp.concatenate(
            [
                lax.ppermute(tail, axis, [(i, (i + 1) % count) for i in range(ends)]),
                cells,
                lax.ppermute(head, axis, [((i + 1) % count, i) for i in range(ends)]),
            ],
            axis=dim,
        )
    return cells


def spread(array, axes, root):
    array = jnp.where(lax.axis_index(axes) == root, array, jnp.zeros_like(array))
    for axis in axes:
        array = lax.psum(array, axis)
    return array


def one_axis_at_a_time(array, axes):
    for axis in axes:
        array = lax.pmax(array, axis)
    return array


def over_axes(array, axes):
    for axis in axes:
        array = lax.psum(array, axis)
    return array


def from_behind(array, axis, by):
    devices = lax.axis_size(axis)
    pairs = [(i, i + by) for i in range(devices) if 0 <= i + by < devices]
    return lax.ppermute(array, axis, pairs)


def list_masks(listed, block_total):
    inside = (listed >= 0) & (listed < block_total)
    kept = []
    for slot_pos in range(listed.shape[-1]):
        seen = jnp.zeros(listed.shape[:-1], dtype=jnp.bool_)
        for prior_pos in range(slot_pos):
            seen = seen | inside[..., prior_pos] & (listed[..., prior_pos] == listed[..., slot_pos])
        kept.append(inside[..., slot_pos] & jnp.logical_not(seen))
    return jnp.stack(kept, -1)


def slot_ranks(owners, ctx_count):
    onehot = (owners[..., None] == jnp.arange(ctx_count, dtype=jnp.int32)).astype(jnp.int32)
    before = jnp.cumsum(onehot, axis=-2) - onehot
    return jnp.sum(before * onehot, axis=-1)


def body(query, key_in, value_in, grad_out, random_blocks, universal_segment_indices):
    query, key_in, value_in, grad_out = (
        lax.all_to_all(query, "head", split_axis=1, concat_axis=0, tiled=True),
        lax.all_to_all(key_in, "head", split_axis=1, concat_axis=0, tiled=True),
        lax.all_to_all(value_in, "head", split_axis=1, concat_axis=0, tiled=True),
        lax.all_to_all(grad_out, "head", split_axis=1, concat_axis=0, tiled=True),
    )
    ctx_count = lax.axis_size(CTX)
    ctx_place = lax.axis_index(CTX)
    token_count = query.shape[0]
    head_count = query.shape[1] // FEATURE_LENGTH
    block_count = token_count // SPAN_TOKENS
    block_total = ctx_count * block_count
    request_count = block_count * head_count * RANDOM
    slot_cap = max(2, (5 * request_count + 4 * ctx_count - 1) // (4 * ctx_count))
    inverse_root_dimension = FEATURE_LENGTH ** (-0.5)
    list_width = 3 + RANDOM + WORLDWIDE_COUNT

    def by_head(matrix):
        return matrix.reshape(block_count, SPAN_TOKENS, head_count, FEATURE_LENGTH).transpose(
            0, 2, 1, 3
        )

    def from_head(blocks):
        return blocks.transpose(0, 2, 1, 3).reshape(token_count, head_count * FEATURE_LENGTH)

    query_heads = by_head(query)
    dout_heads = by_head(grad_out)
    paired = jnp.concatenate(
        [
            key_in.reshape(token_count, head_count, FEATURE_LENGTH),
            value_in.reshape(token_count, head_count, FEATURE_LENGTH),
        ],
        2,
    ).reshape(token_count, head_count * 2 * FEATURE_LENGTH)
    padded = extended(paired, ((CTX, 0),), SPAN_TOKENS)
    table_all = padded.reshape(
        block_count + 2, SPAN_TOKENS, head_count, 2 * FEATURE_LENGTH
    ).transpose(0, 2, 1, 3)
    window_sets = jnp.stack(
        [table_all[:block_count], table_all[1 : block_count + 1], table_all[2:]], 2
    )
    local_table = table_all[1 : block_count + 1].reshape(
        block_count * head_count, SPAN_TOKENS, 2 * FEATURE_LENGTH
    )
    head_iota = jnp.arange(head_count, dtype=jnp.int32)[None, :, None]
    owners = (random_blocks // block_count).reshape(-1)
    items = (random_blocks % block_count * head_count + head_iota).reshape(-1)
    slots = owners * slot_cap + slot_ranks(owners, ctx_count)
    requests = (
        jnp.zeros((ctx_count * slot_cap,), jnp.int32)
        .at[slots]
        .set(items)
        .reshape(ctx_count, slot_cap)
    )
    received = lax.all_to_all(requests, CTX, split_axis=0, concat_axis=0, tiled=True)
    fetched = lax.all_to_all(local_table[received], CTX, split_axis=0, concat_axis=0, tiled=True)
    random_sets = fetched.reshape(ctx_count * slot_cap, SPAN_TOKENS, 2 * FEATURE_LENGTH)[
        slots
    ].reshape(block_count, head_count, RANDOM, SPAN_TOKENS, 2 * FEATURE_LENGTH)
    shared_rows = []
    for global_pos in range(WORLDWIDE_COUNT):
        block_id = universal_segment_indices[global_pos]
        start_row = block_id % block_count * SPAN_TOKENS
        piece = jnp.concatenate(
            [
                lax.dynamic_slice_in_dim(matrix, start_row, SPAN_TOKENS, 0)
                for matrix in (query, key_in, value_in, grad_out)
            ],
            1,
        )
        shared_rows.append(spread(piece, CTX, block_id // block_count))
    shared = (
        jnp.stack(shared_rows, 0)
        .reshape(WORLDWIDE_COUNT, SPAN_TOKENS, 4, head_count, FEATURE_LENGTH)
        .transpose(2, 3, 0, 1, 4)
    )
    global_query = shared[0].reshape(head_count, WORLDWIDE_COUNT * SPAN_TOKENS, FEATURE_LENGTH)
    global_dout = shared[3].reshape(head_count, WORLDWIDE_COUNT * SPAN_TOKENS, FEATURE_LENGTH)
    global_pairs = jnp.concatenate([shared[1], shared[2]], -1)
    pair_sets = jnp.concatenate(
        [
            window_sets,
            random_sets,
            jnp.broadcast_to(
                global_pairs[None],
                (block_count, head_count, WORLDWIDE_COUNT, SPAN_TOKENS, 2 * FEATURE_LENGTH),
            ),
        ],
        2,
    )
    collected_lookup_segments = pair_sets[..., :FEATURE_LENGTH]
    collected_content_segments = pair_sets[..., FEATURE_LENGTH:]
    own_ids = ctx_place * block_count + jnp.arange(block_count, dtype=jnp.int32)
    window_ids = jnp.stack([own_ids - 1, own_ids, own_ids + 1], 1)[:, None, :]
    global_cols = jnp.broadcast_to(
        universal_segment_indices[None, None, :], (block_count, head_count, WORLDWIDE_COUNT)
    )
    listed = jnp.concatenate([window_ids, random_blocks, global_cols], 2)
    kept = list_masks(listed, block_total)
    raw_affinities = (
        jnp.einsum(
            "bhqd,bhskd->bhqsk",
            query_heads,
            collected_lookup_segments,
            preferred_element_type=jnp.float32,
        )
        * inverse_root_dimension
    )
    live = kept[:, :, None, :, None]
    row_max = jnp.max(jnp.where(live, raw_affinities, -jnp.inf), axis=(3, 4), keepdims=True)
    normalized_affinities = jnp.where(live, jnp.exp(raw_affinities - row_max), 0.0)
    normalizer_totals = jnp.sum(normalized_affinities, axis=(3, 4))
    sparse_mixture = (
        jnp.einsum(
            "bhqsk,bhskd->bhqd",
            normalized_affinities.astype(jnp.bfloat16),
            collected_content_segments,
            preferred_element_type=jnp.float32,
        )
        / normalizer_totals[..., None]
    ).astype(jnp.bfloat16)
    key_heads = key_in.reshape(token_count, head_count, FEATURE_LENGTH).transpose(1, 0, 2)
    value_heads = value_in.reshape(token_count, head_count, FEATURE_LENGTH).transpose(1, 0, 2)
    global_scores = (
        jnp.einsum("hqd,hkd->hqk", global_query, key_heads, preferred_element_type=jnp.float32)
        * inverse_root_dimension
    )
    global_max = one_axis_at_a_time(jnp.max(global_scores, axis=-1), CTX)
    global_weights = jnp.exp(global_scores - global_max[..., None])
    partial_acc = jnp.einsum(
        "hqk,hkd->hqd",
        global_weights.astype(jnp.bfloat16),
        value_heads,
        preferred_element_type=jnp.float32,
    )
    global_acc, global_total = (
        over_axes(partial_acc, CTX),
        over_axes(jnp.sum(global_weights, axis=-1), CTX),
    )
    universal_mixture = (global_acc / global_total[..., None]).astype(jnp.bfloat16)
    global_blocks = universal_mixture.reshape(
        head_count, WORLDWIDE_COUNT, SPAN_TOKENS, FEATURE_LENGTH
    )
    hits = [
        own_ids == universal_segment_indices[global_pos] for global_pos in range(WORLDWIDE_COUNT)
    ]
    mixed_segments = sparse_mixture
    for global_pos in range(WORLDWIDE_COUNT):
        mixed_segments = jnp.where(
            hits[global_pos][:, None, None, None],
            global_blocks[None, :, global_pos],
            mixed_segments,
        )
    is_global = jnp.any(own_ids[:, None] == universal_segment_indices[None, :], axis=1)
    filtered_upstream = jnp.where(
        is_global[:, None, None, None], jnp.zeros((), jnp.bfloat16), dout_heads
    )
    rowwise_correction = jnp.sum(
        filtered_upstream.astype(jnp.float32) * sparse_mixture.astype(jnp.float32), axis=-1
    )
    probabilities = normalized_affinities / normalizer_totals[..., None, None]
    prob_half = probabilities.astype(jnp.bfloat16)
    affinity_derivative = jnp.einsum(
        "bhqd,bhskd->bhqsk",
        filtered_upstream,
        collected_content_segments,
        preferred_element_type=jnp.float32,
    )
    raw_affinity_derivative = (
        probabilities * (affinity_derivative - rowwise_correction[..., None, None])
    ).astype(jnp.bfloat16)
    grad_q = (
        jnp.einsum(
            "bhqsk,bhskd->bhqd",
            raw_affinity_derivative,
            collected_lookup_segments,
            preferred_element_type=jnp.float32,
        )
        * inverse_root_dimension
    )
    pair_grads = []
    for slot_pos in range(list_width):
        key_part = (
            jnp.einsum(
                "bhqk,bhqd->bhkd",
                raw_affinity_derivative[:, :, :, slot_pos],
                query_heads,
                preferred_element_type=jnp.float32,
            )
            * inverse_root_dimension
        )
        value_part = jnp.einsum(
            "bhqk,bhqd->bhkd",
            prob_half[:, :, :, slot_pos],
            filtered_upstream,
            preferred_element_type=jnp.float32,
        )
        pair_grads.append(jnp.concatenate([key_part, value_part], -1))
    grad_pairs = pair_grads[1]
    grad_pairs = grad_pairs.at[:-1].add(pair_grads[0][1:])
    grad_pairs = grad_pairs.at[1:].add(pair_grads[2][:-1])
    from_next = from_behind(pair_grads[0][0].astype(jnp.bfloat16), CTX, -1).astype(jnp.float32)
    from_prev = from_behind(pair_grads[2][-1].astype(jnp.bfloat16), CTX, 1).astype(jnp.float32)
    grad_pairs = grad_pairs.at[-1].add(from_next).at[0].add(from_prev)
    random_terms = (
        jnp.stack(pair_grads[3 : 3 + RANDOM], 2)
        .astype(jnp.bfloat16)
        .reshape(request_count, SPAN_TOKENS, 2 * FEATURE_LENGTH)
    )
    outgoing = (
        jnp.zeros((ctx_count * slot_cap, SPAN_TOKENS, 2 * FEATURE_LENGTH), jnp.bfloat16)
        .at[slots]
        .set(random_terms)
    )
    returned = lax.all_to_all(
        outgoing.reshape(ctx_count, slot_cap, SPAN_TOKENS, 2 * FEATURE_LENGTH),
        CTX,
        split_axis=0,
        concat_axis=0,
        tiled=True,
    )
    table_grads = (
        jnp.zeros((block_count * head_count, SPAN_TOKENS, 2 * FEATURE_LENGTH), jnp.float32)
        .at[received.reshape(-1)]
        .add(
            returned.reshape(ctx_count * slot_cap, SPAN_TOKENS, 2 * FEATURE_LENGTH).astype(
                jnp.float32
            )
        )
    )
    grad_pairs = grad_pairs + table_grads.reshape(
        block_count, head_count, SPAN_TOKENS, 2 * FEATURE_LENGTH
    )
    global_terms = jnp.stack(
        [
            jnp.sum(pair_grads[3 + RANDOM + global_pos], axis=0)
            for global_pos in range(WORLDWIDE_COUNT)
        ],
        0,
    )
    global_delta = jnp.sum(
        global_dout.astype(jnp.float32) * universal_mixture.astype(jnp.float32), axis=-1
    )
    global_prob = global_weights / global_total[..., None]
    value_local = jnp.einsum(
        "hqk,hqd->hkd",
        global_prob.astype(jnp.bfloat16),
        global_dout,
        preferred_element_type=jnp.float32,
    )
    global_dprob = jnp.einsum(
        "hqd,hkd->hqk", global_dout, value_heads, preferred_element_type=jnp.float32
    )
    global_dscore = (global_prob * (global_dprob - global_delta[..., None])).astype(jnp.bfloat16)
    key_local = (
        jnp.einsum("hqk,hqd->hkd", global_dscore, global_query, preferred_element_type=jnp.float32)
        * inverse_root_dimension
    )
    query_partial = (
        jnp.einsum("hqk,hkd->hqd", global_dscore, key_heads, preferred_element_type=jnp.float32)
        * inverse_root_dimension
    )
    global_terms, universal_asker_derivative = (
        over_axes(global_terms, CTX),
        over_axes(query_partial, CTX),
    )
    local_pairs = jnp.concatenate([key_local, value_local], -1).reshape(
        head_count, block_count, SPAN_TOKENS, 2 * FEATURE_LENGTH
    )
    grad_pairs = grad_pairs + local_pairs.transpose(1, 0, 2, 3)
    global_dq_blocks = universal_asker_derivative.reshape(
        head_count, WORLDWIDE_COUNT, SPAN_TOKENS, FEATURE_LENGTH
    )
    for global_pos in range(WORLDWIDE_COUNT):
        hit_mask = hits[global_pos][:, None, None, None]
        grad_pairs = grad_pairs + jnp.where(hit_mask, global_terms[global_pos][None], 0.0)
        grad_q = jnp.where(hit_mask, global_dq_blocks[None, :, global_pos], grad_q)
    return (
        from_head(mixed_segments),
        from_head(grad_q).astype(jnp.bfloat16),
        from_head(grad_pairs[..., :FEATURE_LENGTH]).astype(jnp.bfloat16),
        from_head(grad_pairs[..., FEATURE_LENGTH:]).astype(jnp.bfloat16),
    )


def solution(mesh):
    torus = Mesh(mesh.devices.reshape(16, 4, mesh.shape["head"]), ("ctx_0", "ctx_1", "head"))
    placed = (
        P(CTX_HEAD, None),
        P(CTX_HEAD, None),
        P(CTX_HEAD, None),
        P(CTX_HEAD, None),
        P(CTX, "head", None),
        P(),
    )
    return jax.shard_map(
        body,
        mesh=torus,
        in_specs=placed,
        out_specs=(P(CTX, "head"), P(CTX, "head"), P(CTX, "head"), P(CTX, "head")),
        check_vma=False,
    )
```

profile of v0, /device:TPU:1, one launch (start us, length us, event | category | flops | bytes accessed | tf_op | source)
XLA Modules:
  0.0 881.9 jit_solution(4818153470860434396)
XLA Ops:
  11.0 19.3 %all-to-all-start.4 = ((s32[64,1,2]{2,1,0:T(1,128)}), s32[64,1,2]{2,1,0:T(1,128)S(1)}, u32[]{:S(2)}, u32[]{:S(2)}) async-start(s32[64,1,2]{2,1,0:T(1,128)} %bitcast.39), calls=%async_computation.4 | async-start | bytes 65536 | tf_op jit(solution)/shard_map/all_to_all | solution.py:129
  31.0 12.6 %all-to-all-done.4 = s32[64,1,2]{2,1,0:T(1,128)S(1)} async-done(((s32[64,1,2]{2,1,0:T(1,128)}), s32[64,1,2]{2,1,0:T(1,128)S(1)}, u32[]{:S(2)}, u32[]{:S(2)}) %all-to-all-start.4) | async-done | bytes 544 | tf_op jit(solution)/shard_map/all_to_all | solution.py:129
  43.7 6.4 all-to-all-start.3
  50.1 1.7 copy_bitcast_fusion.1
  51.8 4.8 all-to-all-done.3
  56.5 4.4 all-to-all-start.2
  60.9 1.7 copy_bitcast_fusion.2
  62.6 4.8 all-to-all-done.2
  67.4 4.4 all-to-all-start.1
  71.7 1.7 copy_bitcast_fusion.3
  73.8 4.5 all-to-all-done.1
  78.2 4.4 all-to-all-start
  82.7 2.8 gather_fusion
  85.5 3.6 all-to-all-done
  89.1 5.8 all-to-all-start.5
  103.8 1.3 broadcast_compare_fusion
  105.3 1.3 collective-permute-start.1
  106.6 4.0 collective-permute-start
  112.6 148.6 %all-reduce.18.cloned.1.call-done = (bf16[64,512]{1,0:T(8,128)(2,1)}, bf16[64,512]{1,0:T(8,128)(2,1)}) async-done(((bf16[64,512]{1,0:T(8,128)(2,1)}, bf16[64,512]{1,0:T(8,128)(2,1)}), (bf16[64,512]{1,0:T(8,128)(2,1)}, bf16[64,512]{1,0:T(8,128)(2,1)})) %all-reduce.18.cloned.1.call-update) | async-done | bytes 131088 | tf_op jit(solution)/shard_map/psum | solution.py:35
  261.1 1.5 stack.54
  262.6 1.5 stack.53
  266.0 70.3 %all-reduce.20.cloned.1.call-done = (bf16[1,64,4,1,128]{4,2,1,3,0:T(4,128)(2,1)}, bf16[1,64,4,1,128]{4,2,1,3,0:T(4,128)(2,1)}) async-done(((bf16[1,64,4,1,128]{4,2,1,3,0:T(4,128)(2,1)}, bf16[1,64,4,1,128]{4,2,1,3,0:T(4,128)(2,1)}), (bf16[1,64,4,1,128]{4,2,1,3,0:T(4,128)(2,1)}, bf16[1,64,4,1,128]{4,2,1,3,0:T(4,128)(2,1)})) %all-reduce.20.cloned.1.call-update) | async-done | bytes 131088 | tf_op jit(solution)/shard_map/psum | solution.py:35
  337.8 24.4 %pmax.14 = f32[1,128]{1,0:T(1,128)S(1)} all-reduce(f32[1,128]{1,0:T(1,128)S(1)} %bitcast.401), channel_id=1, replica_groups=mesh['ctx_0'=16,'ctx_1'=4,'head'=8] {'ctx_0'}, use_global_device_ids=true, to_apply=%region_5.6 | all-reduce | flops 128 | bytes 1024 | tf_op jit(solution)/shard_map/pmax | solution.py:41
  362.2 7.3 pmax.15
  370.7 21.2 %psum.90 = f32[1,128]{1,0:T(1,128)S(1)} all-reduce(f32[1,128]{1,0:T(1,128)S(1)} %bitcast.400), channel_id=1, replica_groups=mesh['ctx_0'=16,'ctx_1'=4,'head'=8] {'ctx_0'}, use_global_device_ids=true, to_apply=%region_10.11 | all-reduce | flops 128 | bytes 1024 | tf_op jit(solution)/shard_map/psum | solution.py:47
  391.9 6.7 psum.91
  398.6 102.9 %all-reduce.10.cloned.1.call-done = f32[1,128,128]{2,1,0:T(8,128)} async-done(((f32[1,128,128]{2,1,0:T(8,128)}), f32[1,128,128]{2,1,0:T(8,128)}) %all-reduce.10.cloned.1.call-update) | async-done | bytes 65552 | tf_op jit(solution)/shard_map/psum | solution.py:47
  501.6 63.9 %all-reduce.12.cloned.1.call-done = f32[1,128,128]{2,1,0:T(8,128)} async-done(((f32[1,128,128]{2,1,0:T(8,128)}), f32[1,128,128]{2,1,0:T(8,128)}) %all-reduce.12.cloned.1.call-update) | async-done | bytes 65552 | tf_op jit(solution)/shard_map/psum | solution.py:47
  565.5 1.0 multiply_reduce_fusion.1
  566.5 2.8 gather_fusion.1
  569.4 1.3 constant_dynamic-update-slice_fusion
  570.6 1.2 broadcast_dynamic-update-slice_fusion
  571.8 2.4 select_reduce_fusion
  574.1 1.2 bitcast_reduce_fusion
  575.3 1.1 convert_bitcast_fusion
  577.9 2.4 select_select_fusion
  580.6 1.7 multiply_convert_fusion
  583.9 2.5 broadcast_in_dim.195
  586.4 6.7 scatter_fusion
  593.1 15.0 %all-to-all-start.6 = ((bf16[64,2,64,256]{3,2,1,0:T(8,128)(2,1)}), bf16[64,2,64,256]{3,2,1,0:T(8,128)(2,1)}, u32[]{:S(2)}, u32[]{:S(2)}) async-start(bf16[64,2,64,256]{3,2,1,0:T(8,128)(2,1)} %bitcast.335), calls=%async_computation.6 | async-start | bytes 8388608 | tf_op jit(solution)/shard_map/all_to_all | solution.py:289
  612.4 1.3 collective-permute-start.2
  614.3 4.0 collective-permute-start.3
  621.2 154.1 %all-reduce.16.cloned.1.call-done = (f32[1,128,128]{2,1,0:T(8,128)}, f32[2,1,64,256]{3,2,1,0:T(8,128)}) async-done(((f32[1,128,128]{2,1,0:T(8,128)}, f32[2,1,64,256]{3,2,1,0:T(8,128)}), (f32[1,128,128]{2,1,0:T(8,128)}, f32[2,1,64,256]{3,2,1,0:T(8,128)})) %all-reduce.16.cloned.1.call-update) | async-done | bytes 196624 | tf_op jit(solution)/shard_map/psum | solution.py:47
  775.3 29.9 %psum.93 = bf16[1,2,64,128]{3,2,1,0:T(8,128)(2,1)S(1)} all-reduce(f32[1,2,64,128]{3,2,1,0:T(8,128)} %bitcast.398), channel_id=1, replica_groups=mesh['ctx_0'=16,'ctx_1'=4,'head'=8] {'ctx_1'}, use_global_device_ids=true, to_apply=%region_19.20 | all-reduce | flops 16384 | bytes 98304 | tf_op jit(solution)/shard_map/psum | solution.py:47
  805.2 3.8 fusion.18
  809.0 40.3 %all-reduce.14.cloned.1.call-done = f32[2,1,64,256]{3,2,1,0:T(8,128)} async-done(((f32[2,1,64,256]{3,2,1,0:T(8,128)}), f32[2,1,64,256]{3,2,1,0:T(8,128)}) %all-reduce.14.cloned.1.call-update) | async-done | bytes 131088 | tf_op jit(solution)/shard_map/psum | solution.py:47
  850.1 6.5 bitcast_convert_fusion
  856.8 17.0 %scatter_fusion.1 = f32[16,64,256]{2,1,0:T(8,128)S(1)} fusion(f32[16,64,256]{2,1,0:T(8,128)S(1)} %broadcast_in_dim.194, s32[128]{0:T(128)S(1)} %fusion.60, f32[128,64,256]{2,1,0:T(8,128)} %bitcast_convert_fusion), kind=kCustom, calls=%fused_computation.4 | custom fusion | flops 2097152 | bytes 25166336 | tf_op jit(solution)/shard_map/scatter-add | solution.py:299
  (144 shorter events, 27.2 us)
Async XLA Ops:
  7.2 23.1 %copy-start = (bf16[128,1024]{1,0:T(8,128)(2,1)S(1)}, bf16[128,1024]{1,0:T(8,128)(2,1)}, u32[]{:S(2)}) copy-start(bf16[128,1024]{1,0:T(8,128)(2,1)} %param.17) | copy-start | bytes 786436
  11.0 32.7 %all-to-all-start.4 = ((s32[64,1,2]{2,1,0:T(1,128)}), s32[64,1,2]{2,1,0:T(1,128)S(1)}, u32[]{:S(2)}, u32[]{:S(2)}) async-start(s32[64,1,2]{2,1,0:T(1,128)} %bitcast.39), calls=%async_computation.4 | async-start | bytes 65536 | tf_op jit(solution)/shard_map/all_to_all | solution.py:129
  43.7 12.9 %all-to-all-start.3 = ((bf16[128,8,128]{2,0,1:T(8,128)(2,1)}), bf16[128,8,128]{2,0,1:T(8,128)(2,1)S(1)}, u32[]{:S(2)}, u32[]{:S(2)}) async-start(bf16[128,8,128]{2,0,1:T(8,128)(2,1)} %copy_bitcast_fusion), calls=%async_computation.3 | async-start | bytes 524288 | tf_op jit(solution)/shard_map/all_to_all | solution.py:79
  56.5 10.9 %all-to-all-start.2 = ((bf16[128,8,128]{2,0,1:T(8,128)(2,1)}), bf16[128,8,128]{2,0,1:T(8,128)(2,1)S(1)}, u32[]{:S(2)}, u32[]{:S(2)}) async-start(bf16[128,8,128]{2,0,1:T(8,128)(2,1)} %copy_bitcast_fusion.1), calls=%async_computation.2 | async-start | bytes 524288 | tf_op jit(solution)/shard_map/all_to_all | solution.py:78
  67.4 10.9 %all-to-all-start.1 = ((bf16[128,8,128]{2,0,1:T(8,128)(2,1)}), bf16[128,8,128]{2,0,1:T(8,128)(2,1)S(1)}, u32[]{:S(2)}, u32[]{:S(2)}) async-start(bf16[128,8,128]{2,0,1:T(8,128)(2,1)} %copy_bitcast_fusion.2), calls=%async_computation.1 | async-start | bytes 524288 | tf_op jit(solution)/shard_map/all_to_all | solution.py:77
  78.2 10.9 %all-to-all-start = ((bf16[128,8,128]{2,0,1:T(8,128)(2,1)}), bf16[128,8,128]{2,0,1:T(8,128)(2,1)S(1)}, u32[]{:S(2)}, u32[]{:S(2)}) async-start(bf16[128,8,128]{2,0,1:T(8,128)(2,1)} %copy_bitcast_fusion.3), calls=%async_computation | async-start | bytes 524288 | tf_op jit(solution)/shard_map/all_to_all | solution.py:76
  89.1 5.9 copy-start.8
  89.1 11.7 %copy-start.7 = (s32[16,1,3]{0,1,2:T(1,128)S(1)}, s32[16,1,3]{0,1,2:T(1,128)}, u32[]{:S(2)}) copy-start(s32[16,1,3]{0,1,2:T(1,128)} %param.18) | copy-start | bytes 580
  89.1 477.4 %all-to-all-start.5 = ((bf16[64,2,64,256]{3,2,1,0:T(8,128)(2,1)}), bf16[64,2,64,256]{3,2,1,0:T(8,128)(2,1)}, u32[]{:S(2)}, u32[]{:S(2)}) async-start(bf16[64,2,64,256]{3,2,1,0:T(8,128)(2,1)} %bitcast.346), calls=%async_computation.5 | async-start | bytes 8388608 | tf_op jit(solution)/shard_map/all_to_all | solution.py:130
  94.9 166.2 %all-reduce.18.cloned.1.call-start = ((), (), s32[]{:S(2)}) async-start(), calls=%async_computation.11 | async-start | bytes 262144 | tf_op jit(solution)/shard_map/psum | solution.py:35
  105.3 6.2 collective-permute-start.1
  106.6 5.0 collective-permute-start
  111.4 224.8 %all-reduce.20.cloned.1.call-start = ((), (), s32[]{:S(2)}) async-start(), calls=%async_computation.12 | async-start | bytes 262144 | tf_op jit(solution)/shard_map/psum | solution.py:35
  264.1 237.4 %all-reduce.10.cloned.1.call-start = ((), (), s32[]{:S(2)}) async-start(), calls=%async_computation.7 | async-start | bytes 131072 | tf_op jit(solution)/shard_map/psum | solution.py:47
  370.4 195.1 %all-reduce.12.cloned.1.call-start = ((), (), s32[]{:S(2)}) async-start(), calls=%async_computation.8 | async-start | bytes 131072 | tf_op jit(solution)/shard_map/psum | solution.py:47
  575.3 2.6 copy-start.6
  576.4 6.4 copy-start.2
  582.3 1.4 copy-start.4
  593.1 257.0 %all-to-all-start.6 = ((bf16[64,2,64,256]{3,2,1,0:T(8,128)(2,1)}), bf16[64,2,64,256]{3,2,1,0:T(8,128)(2,1)}, u32[]{:S(2)}, u32[]{:S(2)}) async-start(bf16[64,2,64,256]{3,2,1,0:T(8,128)(2,1)} %bitcast.335), calls=%async_computation.6 | async-start | bytes 8388608 | tf_op jit(solution)/shard_map/all_to_all | solution.py:289
  608.1 167.2 %all-reduce.16.cloned.1.call-start = ((), (), s32[]{:S(2)}) async-start(), calls=%async_computation.10 | async-start | bytes 393216 | tf_op jit(solution)/shard_map/psum | solution.py:47
  609.9 1.6 copy-start.5
  609.9 2.2 copy-start.3
  612.4 8.7 collective-permute-start.2
  614.3 7.0 collective-permute-start.3
  621.1 228.1 %all-reduce.14.cloned.1.call-start = ((), (), s32[]{:S(2)}) async-start(), calls=%async_computation.9 | async-start | bytes 262144 | tf_op jit(solution)/shard_map/psum | solution.py:47
  856.8 18.3 %copy-start.1 = (bf16[128,1024]{1,0:T(8,128)(2,1)S(1)}, bf16[128,1024]{1,0:T(8,128)(2,1)}, u32[]{:S(2)}) copy-start(bf16[128,1024]{1,0:T(8,128)(2,1)} %param.17) | copy-start | bytes 786436
Sparse Core Ops, SparseCore 0:
  111.5 149.5 all-reduce.17
  264.2 71.9 all-reduce.19
  370.5 130.9 all-reduce.9
  503.7 61.7 all-reduce.11
  621.3 153.9 all-reduce.15
  777.5 71.7 all-reduce.13
where the time goes:
time: 885 us; the launch traced here: 882 us
  waiting for transfers between devices  610 us (69%)
  blocking collectives  89.5 us (10%)
  starting transfers between devices  70.3 us (8%)
  other arithmetic  37.8 us (4%)
  local copies, waits for them, and re-layouts  35.5 us (4%)
  between operations  21.4 us (2%)
  matrix products  17 us (2%)
    psum x4, waiting for transfers between devices, over_axes(): array = lax.psum(array, axis)  361 us
    psum x2, waiting for transfers between devices, spread(): array = lax.psum(array, axis)  219 us
    psum x3, blocking collectives, over_axes(): array = lax.psum(array, axis)  57.8 us
    pmax x2, blocking collectives, one_axis_at_a_time(): array = lax.pmax(array, axis)  31.7 us
    all_to_all x1, starting transfers between devices, body(): lax.all_to_all(requests, CTX, split_axis=0, concat_axis=0, tiled=True)  19.3 us
  transfers between devices with their start and end apart: 17, of which 12 were waited for; matrix products, arithmetic and copies ran while one was open for 4% of the time, Pallas kernels for 0%

commit v1 on v0

v1 whole, which is shorter than its diff:
```python
import functools

import jax
import jax.numpy as jnp
from jax import lax
from jax.experimental import pallas as pl
from jax.experimental.pallas import tpu as pltpu
from jax.sharding import Mesh
from jax.sharding import PartitionSpec as P

FEATURE_LENGTH = 128
SPAN_TOKENS = 64
RANDOM = 3
WORLDWIDE_COUNT = 2
Z_AXIS = "ctx_0"
Y_AXIS = "ctx_1"
CTX = (Z_AXIS, Y_AXIS)
CTX_HEAD = (Z_AXIS, Y_AXIS, "head")
NEG = -1e30
SCALE = FEATURE_LENGTH ** (-0.5)
UNROLL = 4
SLOTS = 1 + RANDOM
D = FEATURE_LENGTH
S = SPAN_TOKENS
G = WORLDWIDE_COUNT * SPAN_TOKENS
VMEM = pl.BlockSpec(memory_space=pltpu.VMEM)
SMEM = pl.BlockSpec(memory_space=pltpu.SMEM)
PARAMS = pltpu.CompilerParams(vmem_limit_bytes=56 * 2**20)


def dot_nt(a, b):
    return lax.dot_general(a, b, (((1,), (1,)), ((), ())), preferred_element_type=jnp.float32)


def dot_nn(a, b):
    return lax.dot_general(a, b, (((1,), (0,)), ((), ())), preferred_element_type=jnp.float32)


def dot_tn(a, b):
    return lax.dot_general(a, b, (((0,), (0,)), ((), ())), preferred_element_type=jnp.float32)


def list_masks(listed, block_total):
    inside = (listed >= 0) & (listed < block_total)
    kept = []
    for slot_pos in range(listed.shape[-1]):
        seen = jnp.zeros(listed.shape[:-1], dtype=jnp.bool_)
        for prior_pos in range(slot_pos):
            seen = seen | inside[..., prior_pos] & (listed[..., prior_pos] == listed[..., slot_pos])
        kept.append(inside[..., slot_pos] & jnp.logical_not(seen))
    return jnp.stack(kept, -1)


def exchange(array, axes):
    return lax.all_to_all(array, axes, split_axis=0, concat_axis=0, tiled=True)


def to_all(array, axes):
    count = lax.axis_size(axes)
    return exchange(jnp.broadcast_to(array[None], (count,) + array.shape), axes)


def by_head(first, second):
    rows = first.shape[0]
    heads = first.shape[1] // D
    both = jnp.concatenate([first.reshape(rows, heads, D), second.reshape(rows, heads, D)], 2)
    return exchange(both.transpose(1, 0, 2), "head").reshape(heads * rows, 2 * D)


def merge(parts):
    top = functools.reduce(jnp.maximum, [part[0] for part in parts])
    factors = [jnp.exp(part[0] - top) for part in parts]
    total = sum(part[1] * factor for part, factor in zip(parts, factors))
    slope = sum(part[2] * factor for part, factor in zip(parts, factors))
    return top, total, slope


def column_stats(scores, slopes):
    top = jnp.max(scores, axis=0, keepdims=True)
    weights = jnp.exp(scores - top)
    return (
        top,
        jnp.sum(weights, axis=0, keepdims=True),
        jnp.sum(weights * slopes, axis=0, keepdims=True),
    )


def own_scores(i, blocks, qd_ref, kv_ref, shared_ref, bias_ref):
    low = max(i - 1, 0) * S
    high = min(i + 2, blocks) * S
    q = qd_ref[i * S : (i + 1) * S, :D]
    dout = qd_ref[i * S : (i + 1) * S, D:]
    scores = dot_nt(kv_ref[low:high, :D], q) * SCALE
    slopes = dot_nt(kv_ref[low:high, D:], dout)
    global_scores = dot_nt(shared_ref[:, 2 * D : 3 * D], q) * SCALE
    global_scores = jnp.concatenate(
        [
            global_scores[g * S : (g + 1) * S] + bias_ref[i * WORLDWIDE_COUNT + g]
            for g in range(WORLDWIDE_COUNT)
        ],
        0,
    )
    global_slopes = dot_nt(shared_ref[:, 3 * D :], dout)
    return low, high, q, dout, scores, slopes, global_scores, global_slopes


def own_stats_kernel(bias_ref, qd_ref, kv_ref, shared_ref, own_ref, rows_ref):
    tokens = qd_ref.shape[0]
    blocks = tokens // S
    for i in range(blocks):
        _, _, _, _, scores, slopes, global_scores, global_slopes = own_scores(
            i, blocks, qd_ref, kv_ref, shared_ref, bias_ref
        )
        top, total, slope = merge(
            [column_stats(scores, slopes), column_stats(global_scores, global_slopes)]
        )
        own_ref[0, i : i + 1, :] = top
        own_ref[1, i : i + 1, :] = total
        own_ref[2, i : i + 1, :] = slope
    parts = []
    for low in range(0, tokens, G):
        scores = dot_nt(kv_ref[low : low + G, :D], shared_ref[:, :D]) * SCALE
        slopes = dot_nt(kv_ref[low : low + G, D:], shared_ref[:, D : 2 * D])
        parts.append(column_stats(scores, slopes))
    top, total, slope = merge(parts)
    rows_ref[0:1, :] = top
    rows_ref[1:2, :] = total
    rows_ref[2:3, :] = slope


def edge_stats_kernel(
    meta_ref, slot_ref, item_ref, cell_ref, qd_ref, kv_ref, own_ref, out_ref, top_ref, total_ref, slope_ref
):
    group = qd_ref.shape[0] // S
    blocks = own_ref.shape[1]
    top_ref[...] = jnp.full(top_ref.shape, NEG, jnp.float32)
    total_ref[...] = jnp.zeros(total_ref.shape, jnp.float32)
    slope_ref[...] = jnp.zeros(slope_ref.shape, jnp.float32)

    def step(t, carry):
        found = []
        for u in range(UNROLL):
            pos = t * UNROLL + u
            cell = pl.multiple_of(cell_ref[pos] * S, S)
            item = pl.multiple_of(item_ref[pos] * S, S)
            scores = dot_nt(kv_ref[pl.ds(cell, S), :D], qd_ref[pl.ds(item, S), :D]) * SCALE
            slopes = dot_nt(kv_ref[pl.ds(cell, S), D:], qd_ref[pl.ds(item, S), D:])
            found.append((slot_ref[pos], column_stats(scores, slopes)))
        for slot, (top, total, slope) in found:
            top_ref[pl.ds(slot, 1), :] = top
            total_ref[pl.ds(slot, 1), :] = total
            slope_ref[pl.ds(slot, 1), :] = slope
        return carry

    lax.fori_loop(0, meta_ref[0], step, 0)
    mine = pl.multiple_of(SLOTS * group + meta_ref[1] * blocks, 8)
    top_ref[pl.ds(mine, blocks), :] = own_ref[0]
    total_ref[pl.ds(mine, blocks), :] = own_ref[1]
    slope_ref[pl.ds(mine, blocks), :] = own_ref[2]
    top, total, slope = merge(
        [
            (
                top_ref[s * group : (s + 1) * group, :],
                total_ref[s * group : (s + 1) * group, :],
                slope_ref[s * group : (s + 1) * group, :],
            )
            for s in range(SLOTS + 1)
        ]
    )
    out_ref[0] = top
    out_ref[1] = total
    out_ref[2] = slope


def edge_grads_kernel(
    meta_ref, slot_ref, item_ref, cell_ref, qd_ref, kv_ref, parts_ref, table_ref, partial_ref, final_ref
):
    group = qd_ref.shape[0] // S
    lanes = parts_ref.shape[0]
    top, total, slope = merge(
        [(parts_ref[lane, 0], parts_ref[lane, 1], parts_ref[lane, 2]) for lane in range(lanes)]
    )
    inverse = 1.0 / total
    final_ref[0] = top
    final_ref[1] = inverse
    final_ref[2] = slope * inverse
    table_ref[...] = jnp.zeros(table_ref.shape, jnp.bfloat16)
    partial_ref[...] = jnp.zeros(partial_ref.shape, jnp.float32)

    def step(t, carry):
        found = []
        for u in range(UNROLL):
            pos = t * UNROLL + u
            live = slot_ref[pos] < SLOTS * group
            item_pos = item_ref[pos]
            cell = pl.multiple_of(cell_ref[pos] * S, S)
            item = pl.multiple_of(item_pos * S, S)
            key = kv_ref[pl.ds(cell, S), :D]
            value = kv_ref[pl.ds(cell, S), D:]
            q = qd_ref[pl.ds(item, S), :D]
            dout = qd_ref[pl.ds(item, S), D:]
            scores = dot_nt(key, q) * SCALE
            slopes = dot_nt(value, dout)
            prob = jnp.exp(scores - final_ref[0, pl.ds(item_pos, 1), :])
            prob = prob * final_ref[1, pl.ds(item_pos, 1), :]
            prob = jnp.where(live, prob, 0.0)
            dscore = prob * ((slopes - final_ref[2, pl.ds(item_pos, 1), :]) * SCALE)
            prob = prob.astype(jnp.bfloat16)
            dscore = dscore.astype(jnp.bfloat16)
            found.append(
                (
                    cell,
                    item,
                    dot_nn(dscore, q),
                    dot_nn(prob, dout),
                    dot_tn(prob, value),
                    dot_tn(dscore, key),
                )
            )
        for cell, item, dkey, dvalue, mixed, dq in found:
            at = pl.ds(cell, S)
            table_ref[at, :D] = (table_ref[at, :D].astype(jnp.float32) + dkey).astype(jnp.bfloat16)
            table_ref[at, D:] = (table_ref[at, D:].astype(jnp.float32) + dvalue).astype(jnp.bfloat16)
            at = pl.ds(item, S)
            partial_ref[at, :D] += mixed
            partial_ref[at, D:] += dq
        return carry

    lax.fori_loop(0, meta_ref[0], step, 0)


def own_grads_kernel(
    meta_ref, bias_ref, flag_ref, qd_ref, kv_ref, shared_ref, final_ref, rows_ref, pairs_ref, mixed_ref, shared_grad_ref
):
    tokens = qd_ref.shape[0]
    blocks = tokens // S
    first = meta_ref[1] * blocks
    rows = rows_ref[...]
    row_top = jnp.max(rows[:, 0:1, :], axis=0)
    factors = jnp.exp(rows[:, 0:1, :] - row_top[None])
    sums = jnp.sum(rows * factors, axis=0)
    row_inverse = 1.0 / sums[1:2]
    row_slope = sums[2:3] * row_inverse
    q = shared_ref[:, :D]
    dout = shared_ref[:, D : 2 * D]
    mixed = jnp.zeros((G, D), jnp.float32)
    dq = jnp.zeros((G, D), jnp.float32)
    for low in range(0, tokens, G):
        key = kv_ref[low : low + G, :D]
        value = kv_ref[low : low + G, D:]
        scores = dot_nt(key, q) * SCALE
        slopes = dot_nt(value, dout)
        prob = jnp.exp(scores - row_top) * row_inverse
        dscore = (prob * ((slopes - row_slope) * SCALE)).astype(jnp.bfloat16)
        prob = prob.astype(jnp.bfloat16)
        pairs_ref[low : low + G, :D] = dot_nn(dscore, q)
        pairs_ref[low : low + G, D:] = dot_nn(prob, dout)
        mixed = mixed + dot_tn(prob, value)
        dq = dq + dot_tn(dscore, key)
    shared_grad_ref[G:, :D] = mixed
    shared_grad_ref[G:, D:] = dq
    global_dkey = jnp.zeros((G, D), jnp.float32)
    global_dvalue = jnp.zeros((G, D), jnp.float32)
    for i in range(blocks):
        low, high, q, dout, scores, slopes, global_scores, global_slopes = own_scores(
            i, blocks, qd_ref, kv_ref, shared_ref, bias_ref
        )
        top = final_ref[0, pl.ds(first + i, 1), :]
        inverse = final_ref[1, pl.ds(first + i, 1), :] * flag_ref[i]
        slope = final_ref[2, pl.ds(first + i, 1), :]

        def both(scores, slopes):
            prob = jnp.exp(scores - top) * inverse
            dscore = (prob * ((slopes - slope) * SCALE)).astype(jnp.bfloat16)
            return prob.astype(jnp.bfloat16), dscore

        prob, dscore = both(scores, slopes)
        global_prob, global_dscore = both(global_scores, global_slopes)
        pairs_ref[low:high, :D] += dot_nn(dscore, q)
        pairs_ref[low:high, D:] += dot_nn(prob, dout)
        global_dkey = global_dkey + dot_nn(global_dscore, q)
        global_dvalue = global_dvalue + dot_nn(global_prob, dout)
        mixed_ref[i * S : (i + 1) * S, :D] = dot_tn(prob, kv_ref[low:high, D:]) + dot_tn(
            global_prob, shared_ref[:, 3 * D :]
        )
        mixed_ref[i * S : (i + 1) * S, D:] = dot_tn(dscore, kv_ref[low:high, :D]) + dot_tn(
            global_dscore, shared_ref[:, 2 * D : 3 * D]
        )
    shared_grad_ref[:G, :D] = global_dkey
    shared_grad_ref[:G, D:] = global_dvalue


def body(query, key_in, value_in, grad_out, random_blocks, universal_segment_indices):
    f32 = jnp.float32
    z_count = lax.axis_size(Z_AXIS)
    y_count = lax.axis_size(Y_AXIS)
    ctx_count = z_count * y_count
    z_place = lax.axis_index(Z_AXIS)
    y_place = lax.axis_index(Y_AXIS)
    ctx_place = z_place * y_count + y_place

    kv = by_head(key_in, value_in)
    query, grad_out, random_blocks, kv = lax.optimization_barrier(
        (query, grad_out, random_blocks, kv)
    )
    kv_all = lax.all_gather(kv, Z_AXIS, axis=0, tiled=True)
    qd = by_head(query, grad_out)
    tokens = qd.shape[0]
    block_count = tokens // S
    group = block_count * y_count
    block_total = ctx_count * block_count
    cells = z_count * block_count

    owners = universal_segment_indices // block_count
    starts = universal_segment_indices % block_count * S
    pieces = []
    for g in range(WORLDWIDE_COUNT):
        pieces.append(
            jnp.concatenate(
                [lax.dynamic_slice_in_dim(part, starts[g], S, 0) for part in (qd, kv)], 1
            )
        )
    chunk = G // ctx_count
    sent = jnp.concatenate(pieces, 0).reshape(ctx_count, chunk, 4 * D)
    arrived = exchange(sent, CTX)
    owner = owners[(ctx_place * chunk) // S]
    picked = lax.dynamic_slice_in_dim(arrived, owner, 1, 0)[0]
    shared = to_all(picked, CTX).reshape(G, 4 * D)

    qd_group = to_all(qd, Y_AXIS).reshape(group * S, 2 * D)
    random_group = to_all(random_blocks[:, 0, :], Y_AXIS).reshape(group, RANDOM)

    ids = z_place * group + jnp.arange(group, dtype=jnp.int32)
    local = jnp.arange(group, dtype=jnp.int32) % block_count
    globals_ = jnp.broadcast_to(universal_segment_indices[None], (group, WORLDWIDE_COUNT))
    listed = jnp.concatenate(
        [jnp.stack([ids - 1, ids, ids + 1], 1), random_group, globals_], 1
    )
    kept = list_masks(listed, block_total)
    is_global = jnp.any(ids[:, None] == universal_segment_indices[None], 1)
    border = jnp.where(local == 0, ids - 1, jnp.where(local == block_count - 1, ids + 1, -1))
    named = jnp.concatenate([border[:, None], random_group], 1)
    valid = jnp.concatenate(
        [((border >= 0) & (border < block_total))[:, None], kept[:, 3 : 3 + RANDOM]], 1
    )
    lane = named // block_count % y_count
    valid = valid & jnp.logical_not(is_global)[:, None] & (lane == y_place)
    cell = named // group * block_count + named % block_count
    valid = valid.T.reshape(-1)
    cell = cell.T.reshape(-1)
    entries = SLOTS * group
    order = jnp.arange(entries, dtype=jnp.int32)
    rank = jnp.cumsum(valid.astype(jnp.int32)) - 1
    edge_count = rank[-1] + 1
    hit = (rank[None, :] == order[:, None]) & valid[None, :]
    slot_list = jnp.sum(jnp.where(hit, order[None, :], 0), 1)
    cell_list = jnp.sum(jnp.where(hit, cell[None, :], 0), 1)
    slot_list = jnp.where(order < edge_count, slot_list, entries + group)
    item_list = jnp.where(order < edge_count, slot_list % group, 0)
    meta = jnp.stack([(edge_count + UNROLL - 1) // UNROLL, y_place]).astype(jnp.int32)
    lists = (meta, slot_list, item_list, cell_list)

    own_first = y_place * block_count
    own_kept = lax.dynamic_slice_in_dim(kept, own_first, block_count, 0)
    bias = jnp.where(own_kept[:, 3 + RANDOM :], 0.0, NEG).astype(f32).reshape(-1)
    own_ids = ctx_place * block_count + jnp.arange(block_count, dtype=jnp.int32)
    hits = own_ids[:, None] == universal_segment_indices[None]
    flags = jnp.where(jnp.any(hits, 1), 0.0, 1.0).astype(f32)

    own, rows = pl.pallas_call(
        own_stats_kernel,
        out_shape=(
            jax.ShapeDtypeStruct((3, block_count, S), f32),
            jax.ShapeDtypeStruct((3, G), f32),
        ),
        in_specs=[SMEM, VMEM, VMEM, VMEM],
        out_specs=(VMEM, VMEM),
        compiler_params=PARAMS,
        name="own_stats",
    )(bias, qd, kv, shared)
    rows_all = to_all(rows, CTX)

    stat_rows = (SLOTS + 1) * group + 8
    stats = pl.pallas_call(
        edge_stats_kernel,
        out_shape=jax.ShapeDtypeStruct((3, group, S), f32),
        in_specs=[SMEM] * 4 + [VMEM] * 3,
        out_specs=VMEM,
        scratch_shapes=[pltpu.VMEM((stat_rows, S), f32)] * 3,
        compiler_params=PARAMS,
        name="edge_stats",
    )(*lists, qd_group, kv_all, own)
    parts = to_all(stats, Y_AXIS)

    table, partial, final = pl.pallas_call(
        edge_grads_kernel,
        out_shape=(
            jax.ShapeDtypeStruct((cells * S, 2 * D), jnp.bfloat16),
            jax.ShapeDtypeStruct((group * S, 2 * D), f32),
            jax.ShapeDtypeStruct((3, group, S), f32),
        ),
        in_specs=[SMEM] * 4 + [VMEM] * 3,
        out_specs=(VMEM, VMEM, VMEM),
        compiler_params=PARAMS,
        name="edge_grads",
    )(*lists, qd_group, kv_all, parts)
    returned = lax.psum_scatter(table, Z_AXIS, scatter_dimension=0, tiled=True)

    pairs, mixed, shared_grads = pl.pallas_call(
        own_grads_kernel,
        out_shape=(
            jax.ShapeDtypeStruct((tokens, 2 * D), f32),
            jax.ShapeDtypeStruct((tokens, 2 * D), f32),
            jax.ShapeDtypeStruct((2 * G, 2 * D), f32),
        ),
        in_specs=[SMEM] * 3 + [VMEM] * 5,
        out_specs=(VMEM, VMEM, VMEM),
        compiler_params=PARAMS,
        name="own_grads",
    )(meta, bias, flags, qd, kv, shared, final, rows_all)

    spread = exchange(
        shared_grads.astype(jnp.bfloat16).reshape(ctx_count, 2 * G // ctx_count, 2 * D), CTX
    )
    summed = jnp.sum(spread.astype(f32), 0).astype(jnp.bfloat16)
    shared_sums = to_all(summed, CTX).reshape(2, WORLDWIDE_COUNT, 1, S, 2 * D).astype(f32)

    halves = exchange(
        partial.astype(jnp.bfloat16).reshape(y_count, tokens, 2 * D), Y_AXIS
    ).astype(f32)
    mixed = (jnp.sum(halves, 0) + mixed).reshape(block_count, S, 2 * D)
    pairs = (returned.astype(f32) + pairs).reshape(block_count, S, 2 * D)
    for g in range(WORLDWIDE_COUNT):
        mask = hits[:, g][:, None, None]
        mixed = jnp.where(mask, shared_sums[1, g], mixed)
        pairs = pairs + jnp.where(mask, shared_sums[0, g], 0.0)
    mixed = mixed.reshape(tokens, 2 * D).astype(jnp.bfloat16)
    pairs = pairs.reshape(tokens, 2 * D).astype(jnp.bfloat16)
    return mixed[:, :D], mixed[:, D:], pairs[:, :D], pairs[:, D:]


def solution(mesh):
    torus = Mesh(mesh.devices.reshape(16, 4, mesh.shape["head"]), ("ctx_0", "ctx_1", "head"))
    return on_torus(torus)


def on_torus(torus):
    placed = (
        P(CTX_HEAD, None),
        P(CTX_HEAD, None),
        P(CTX_HEAD, None),
        P(CTX_HEAD, None),
        P(CTX, "head", None),
        P(),
    )
    return jax.shard_map(
        body,
        mesh=torus,
        in_specs=placed,
        out_specs=(P(CTX, "head"), P(CTX, "head"), P(CTX, "head"), P(CTX, "head")),
        check_vma=False,
    )
```

time: 885 us -> 319 us (0.36)
  waiting for transfers between devices: 610 us -> 113 us
  Pallas kernels: 0 us -> 40.6 us
  blocking collectives: 89.5 us -> 52.8 us
  other arithmetic: 37.8 us -> 13.9 us
  starting transfers between devices: 70.3 us -> 51.3 us
  matrix products: 17 us -> 0 us
  local copies, waits for them, and re-layouts: 35.5 us -> 22.5 us
    psum x6 -> x0, waiting for transfers between devices: 580 us -> none  [the longest x4 361 us: over_axes(): array = lax.psum(array, axis)]
    all_to_all x7 -> x8, waiting for transfers between devices: 30.3 us -> 92.4 us  [exchange(): return lax.all_to_all(array, axes, split_axis=0, concat_axis=0, tiled=True)]
    psum x3 -> x0, blocking collectives: 57.8 us -> none  [over_axes(): array = lax.psum(array, axis)]
    all_to_all x0 -> x3, blocking collectives: none -> 52.8 us  [exchange(): return lax.all_to_all(array, axes, split_axis=0, concat_axis=0, tiled=True)]
    pallas_call x0 -> x4, Pallas kernels: none -> 40.6 us  [the longest x1 20.8 us: body(): pl.pallas_call(edge_grads_kernel, out_shape=(jax.ShapeDtypeStruct((cells...]
    pmax x2 -> x0, blocking collectives: 31.7 us -> none  [one_axis_at_a_time(): array = lax.pmax(array, axis)]
    scatter-add x4 -> x0, other arithmetic: 17.2 us -> none  [the longest x1 17 us: body(): table_grads = jnp.zeros((block_count * head_count, SPAN_TOKENS, 2 * FEATU...]
    dot_general x26 -> x0, matrix products: 17 us -> none  [the longest x1 3.77 us: body(): jnp.einsum('bhqsk,bhskd->bhqd', raw_affinity_derivative, collected_lookup...]
  transfers between devices with their start and end apart: 17 -> 10, of which waited for: 12 -> 10; matrix products, arithmetic and copies ran while one was open for 4% -> 8% of each run, Pallas kernels for 0% -> 4%
where the time goes in v1:
time: 319 us; the launch traced here: 317 us
  waiting for transfers between devices  113 us (35%)
  blocking collectives  52.8 us (17%)
  starting transfers between devices  51.3 us (16%)
  Pallas kernels  40.6 us (13%)
  between operations  22.9 us (7%)
  local copies, waits for them, and re-layouts  22.5 us (7%)
  other arithmetic  13.9 us (4%)
    all_to_all x8, waiting for transfers between devices, exchange(): return lax.all_to_all(array, axes, split_axis=0, concat_axis=0, tiled=True)  92.4 us
    all_to_all x3, blocking collectives, exchange(): return lax.all_to_all(array, axes, split_axis=0, concat_axis=0, tiled=True)  52.8 us
    all_to_all x8, starting transfers between devices, exchange(): return lax.all_to_all(array, axes, split_axis=0, concat_axis=0, tiled=True)  51.3 us
    pallas_call x1, Pallas kernels, body(): pl.pallas_call(edge_grads_kernel, out_shape=(jax.ShapeDtypeStruct((cells...  20.8 us
    all_gather x1, waiting for transfers between devices, body(): kv_all = lax.all_gather(kv, Z_AXIS, axis=0, tiled=True)  13.1 us
    pallas_call x1, Pallas kernels, body(): pl.pallas_call(own_grads_kernel, out_shape=(jax.ShapeDtypeStruct((tokens,...  8.84 us
    reduce_scatter x1, waiting for transfers between devices, body(): returned = lax.psum_scatter(table, Z_AXIS, scatter_dimension=0, tiled=True)  7.85 us
    pallas_call x1, Pallas kernels, body(): pl.pallas_call(edge_stats_kernel, out_shape=jax.ShapeDtypeStruct((3, grou...  7.54 us
  transfers between devices with their start and end apart: 10, of which 10 were waited for; matrix products, arithmetic and copies ran while one was open for 8% of the time, Pallas kernels for 4%

profile of v1, /device:TPU:1, one launch (start us, length us, event | category | flops | bytes accessed | tf_op | source)
XLA Modules:
  0.0 317.4 jit_solution(198017696978181513)
XLA Ops:
  7.2 1.0 copy-done
  8.2 1.1 copy_bitcast_fusion.2
  9.4 19.2 %all_to_all.55 = bf16[8,128,256]{2,1,0:T(8,128)(2,1)} all-to-all(bf16[8,128,256]{2,1,0:T(8,128)(2,1)S(1)} %maximum_bitcast_fusion), channel_id=1, replica_groups=mesh['ctx_0'=16,'ctx_1'=4,'head'=8] {'head'}, dimensions={0} | all-to-all | bytes 1048576 | tf_op jit(solution)/shard_map/all_to_all | solution.py:55
  28.8 0.9 maximum_bitcast_fusion.1
  29.6 4.4 %all-to-all-start.2 = ((bf16[8,128,256]{2,1,0:T(8,128)(2,1)}), bf16[8,128,256]{2,1,0:T(8,128)(2,1)S(1)}, u32[]{:S(2)}, u32[]{:S(2)}) async-start(bf16[8,128,256]{2,1,0:T(8,128)(2,1)} %maximum_bitcast_fusion.1), calls=%async_computation.2 | async-start | bytes 1048576 | tf_op jit(solution)/shard_map/all_to_all | solution.py:55
  40.5 0.8 constant_dynamic-slice_fusion.2
  41.3 2.1 all-to-all-done.2
  44.1 3.2 %all-to-all-start.1 = ((s32[4,16,3]{1,2,0:T(4,128)}), s32[4,16,3]{1,2,0:T(4,128)S(1)}, u32[]{:S(2)}, u32[]{:S(2)}) async-start(s32[4,16,3]{1,2,0:T(4,128)} %broadcast_in_dim.188), calls=%async_computation.1 | async-start | bytes 16384 | tf_op jit(solution)/shard_map/all_to_all | solution.py:55
  47.4 0.7 reshape.235
  48.1 3.5 %all-to-all-done.1 = s32[4,16,3]{1,2,0:T(4,128)S(1)} async-done(((s32[4,16,3]{1,2,0:T(4,128)}), s32[4,16,3]{1,2,0:T(4,128)S(1)}, u32[]{:S(2)}, u32[]{:S(2)}) %all-to-all-start.1) | async-done | bytes 800 | tf_op jit(solution)/shard_map/all_to_all | solution.py:55
  51.6 13.5 %all-to-all-start.3 = ((bf16[64,2,512]{2,1,0:T(2,128)(2,1)}), bf16[64,2,512]{2,1,0:T(2,128)(2,1)S(1)}, u32[]{:S(2)}, u32[]{:S(2)}) async-start(bf16[64,2,512]{2,1,0:T(2,128)(2,1)} %reshape.235), calls=%async_computation.3 | async-start | bytes 262144 | tf_op jit(solution)/shard_map/all_to_all | solution.py:55
  67.9 14.3 %all-to-all-done.3 = bf16[64,2,512]{2,1,0:T(2,128)(2,1)S(1)} async-done(((bf16[64,2,512]{2,1,0:T(2,128)(2,1)}), bf16[64,2,512]{2,1,0:T(2,128)(2,1)S(1)}, u32[]{:S(2)}, u32[]{:S(2)}) %all-to-all-start.3) | async-done | bytes 131104 | tf_op jit(solution)/shard_map/all_to_all | solution.py:55
  82.2 0.7 broadcast_in_dim.198
  83.0 5.1 %all-to-all-start.4 = ((bf16[64,2,512]{2,1,0:T(2,128)(2,1)}), bf16[64,2,512]{2,1,0:T(2,128)(2,1)S(1)}, u32[]{:S(2)}, u32[]{:S(2)}) async-start(bf16[64,2,512]{2,1,0:T(2,128)(2,1)} %broadcast_in_dim.198), calls=%async_computation.4 | async-start | bytes 262144 | tf_op jit(solution)/shard_map/all_to_all | solution.py:55
  88.8 15.9 %all-to-all-done.4 = bf16[64,2,512]{2,1,0:T(2,128)(2,1)S(1)} async-done(((bf16[64,2,512]{2,1,0:T(2,128)(2,1)}), bf16[64,2,512]{2,1,0:T(2,128)(2,1)S(1)}, u32[]{:S(2)}, u32[]{:S(2)}) %all-to-all-start.4) | async-done | bytes 131104 | tf_op jit(solution)/shard_map/all_to_all | solution.py:55
  104.7 1.5 broadcast_in_dim.204
  106.2 3.6 %all-to-all-start.5 = ((bf16[4,1024,256]{2,1,0:T(8,128)(2,1)}), bf16[4,1024,256]{2,1,0:T(8,128)(2,1)S(1)}, u32[]{:S(2)}, u32[]{:S(2)}) async-start(bf16[4,1024,256]{2,1,0:T(8,128)(2,1)} %broadcast_in_dim.204), calls=%async_computation.5 | async-start | bytes 4194304 | tf_op jit(solution)/shard_map/all_to_all | solution.py:55
  114.2 0.7 pad_add_fusion.1.meta_ref
  114.9 0.7 select_reduce_fusion
  116.1 0.7 reshape.236.shared_ref
  116.8 3.4 %own_stats.1 = (f32[3,16,64]{2,1,0:T(8,128)}, f32[3,128]{1,0:T(4,128)}) custom-call(f32[32]{0:T(128)} %reshape.231.bias_ref, bf16[1024,256]{1,0:T(8,128)(2,1)} %bitcast.88, bf16[1024,256]{1,0:T(8,128)(2,1)} %bitcast.92, bf16[128,512]{1,0:T(8,128)(2,1)} %reshape.236.shared_ref), custom_call_target="tpu_custom_call" | custom-call | tf_op jit(solution)/shard_map/own_stats/pallas_call | solution.py:370
  120.2 11.1 %all-to-all-done.5 = bf16[4,1024,256]{2,1,0:T(8,128)(2,1)S(1)} async-done(((bf16[4,1024,256]{2,1,0:T(8,128)(2,1)}), bf16[4,1024,256]{2,1,0:T(8,128)(2,1)S(1)}, u32[]{:S(2)}, u32[]{:S(2)}) %all-to-all-start.5) | async-done | bytes 2097184 | tf_op jit(solution)/shard_map/all_to_all | solution.py:55
  131.4 13.1 %all-gather.2.cloned.1.call-done.kv_ref = bf16[16384,256]{1,0:T(8,128)(2,1)} async-done(((bf16[1024,256]{1,0:T(8,128)(2,1)}), bf16[16384,256]{1,0:T(8,128)(2,1)}) %all-gather.2.cloned.1.call-update) | async-done | bytes 8388624 | tf_op jit(solution)/shard_map/all_gather | solution.py:306
  144.5 7.5 %edge_stats.1 = f32[3,64,64]{2,1,0:T(8,128)} custom-call(s32[2]{0:T(128)} %pad_add_fusion.1.meta_ref, s32[256]{0:T(256)} %get-tuple-element.55.slot_ref, s32[256]{0:T(256)} %get-tuple-element.54.item_ref, s32[256]{0:T(256)} %get-tuple-element.28.cell_ref, bf16[4096,256]{1,0:T(8,128)(2,1)} %bitcast.84, ...), custom_call_target="tpu_custom_call" | custom-call | tf_op jit(solution)/shard_map/edge_stats/pallas_call | solution.py:384
  152.0 0.9 broadcast_in_dim.205
  153.2 10.0 %all_to_all.56 = f32[4,1,12288]{2,1,0:T(1,128)S(1)} all-to-all(f32[4,1,12288]{2,1,0:T(1,128)S(1)} %reshape.243), channel_id=1, replica_groups=mesh['ctx_0'=16,'ctx_1'=4,'head'=8] {'ctx_1'}, dimensions={0} | all-to-all | bytes 393216 | tf_op jit(solution)/shard_map/all_to_all | solution.py:55
  163.7 1.2 reduce.3
  164.9 1.0 reshape.244.parts_ref
  165.9 20.8 %edge_grads.1 = (bf16[16384,256]{1,0:T(8,128)(2,1)}, f32[4096,256]{1,0:T(8,128)}, f32[3,64,64]{2,1,0:T(8,128)}) custom-call(s32[2]{0:T(128)} %pad_add_fusion.1.meta_ref, s32[256]{0:T(256)} %get-tuple-element.55.slot_ref, s32[256]{0:T(256)} %get-tuple-element.54.item_ref, s32[256]{0:T(256)} %get-tuple-element.28.cell_ref, bf16[4096,256]{1,0:T(8,128)(2,1)} %bitcast.85, ...), custom_call_target="tpu_custom_call" | custom-call | tf_op jit(solution)/shard_map/edge_grads/pallas_call | solution.py:395
  187.3 0.7 broadcast_in_dim.206
  188.0 12.9 %all-to-all-start.7 = ((f32[64,3,128]{2,1,0:T(4,128)}), f32[64,3,128]{2,1,0:T(4,128)S(1)}, u32[]{:S(2)}, u32[]{:S(2)}) async-start(f32[64,3,128]{2,1,0:T(4,128)} %broadcast_in_dim.206), calls=%async_computation.7 | async-start | bytes 262144 | tf_op jit(solution)/shard_map/all_to_all | solution.py:55
  201.5 14.3 %all-to-all-done.7.rows_ref = f32[64,3,128]{2,1,0:T(4,128)S(1)} async-done(((f32[64,3,128]{2,1,0:T(4,128)}), f32[64,3,128]{2,1,0:T(4,128)S(1)}, u32[]{:S(2)}, u32[]{:S(2)}) %all-to-all-start.7) | async-done | bytes 98336 | tf_op jit(solution)/shard_map/all_to_all | solution.py:55
  216.5 8.8 %own_grads.1 = (f32[1024,256]{1,0:T(8,128)}, f32[1024,256]{1,0:T(8,128)}, f32[256,256]{1,0:T(8,128)}) custom-call(s32[2]{0:T(128)} %pad_add_fusion.1.meta_ref, f32[32]{0:T(128)} %reshape.231.bias_ref, f32[16]{0:T(128)} %broadcast_select_fusion.flag_ref, bf16[1024,256]{1,0:T(8,128)(2,1)} %bitcast.89, bf16[1024,256]{1,0:T(8,128)(2,1)} %bitcast.93, ...), custom_call_target="tpu_custom_call" | custom-call | tf_op jit(solution)/shard_map/own_grads/pallas_call | solution.py:409
  225.3 1.0 convert_element_type.43
  226.3 23.6 %all_to_all.57 = bf16[64,4,256]{2,1,0:T(4,128)(2,1)S(1)} all-to-all(bf16[64,4,256]{2,1,0:T(4,128)(2,1)S(1)} %reshape.238), channel_id=1, replica_groups=mesh['ctx_0'=16,'ctx_1'=4,'head'=8] {'ctx_0','ctx_1'}, dimensions={0} | all-to-all | bytes 262144 | tf_op jit(solution)/shard_map/all_to_all | solution.py:55
  250.0 0.7 broadcast_in_dim.207
  250.7 4.9 %all-to-all-start.9 = ((bf16[64,4,256]{2,1,0:T(4,128)(2,1)}), bf16[64,4,256]{2,1,0:T(4,128)(2,1)S(1)}, u32[]{:S(2)}, u32[]{:S(2)}) async-start(bf16[64,4,256]{2,1,0:T(4,128)(2,1)} %broadcast_in_dim.207), calls=%async_computation.9 | async-start | bytes 262144 | tf_op jit(solution)/shard_map/all_to_all | solution.py:55
  255.6 3.8 %convert_element_type.46 = bf16[4096,256]{1,0:T(8,128)(2,1)} convert(f32[4096,256]{1,0:T(8,128)} %get-tuple-element.24) | non-fusion elementwise | flops 1048576 | bytes 6291456 | tf_op jit(solution)/shard_map/convert_element_type | solution.py:429
  259.4 13.2 %all-to-all-done.9 = bf16[64,4,256]{2,1,0:T(4,128)(2,1)S(1)} async-done(((bf16[64,4,256]{2,1,0:T(4,128)(2,1)}), bf16[64,4,256]{2,1,0:T(4,128)(2,1)S(1)}, u32[]{:S(2)}, u32[]{:S(2)}) %all-to-all-start.9) | async-done | bytes 131104 | tf_op jit(solution)/shard_map/all_to_all | solution.py:55
  272.6 3.6 %all-to-all-start.10 = ((bf16[4,1024,256]{2,1,0:T(8,128)(2,1)}), bf16[4,1024,256]{2,1,0:T(8,128)(2,1)S(1)}, u32[]{:S(2)}, u32[]{:S(2)}) async-start(bf16[4,1024,256]{2,1,0:T(8,128)(2,1)} %bitcast.25), calls=%async_computation.10 | async-start | bytes 4194304 | tf_op jit(solution)/shard_map/all_to_all | solution.py:55
  276.6 0.7 reshape.241
  277.3 1.5 slice_bitcast_fusion.3
  278.8 1.5 slice_bitcast_fusion.1
  280.3 17.9 %all-to-all-done.10 = bf16[4,1024,256]{2,1,0:T(8,128)(2,1)S(1)} async-done(((bf16[4,1024,256]{2,1,0:T(8,128)(2,1)}), bf16[4,1024,256]{2,1,0:T(8,128)(2,1)S(1)}, u32[]{:S(2)}, u32[]{:S(2)}) %all-to-all-start.10) | async-done | bytes 2097184 | tf_op jit(solution)/shard_map/all_to_all | solution.py:55
  299.3 0.8 fusion.23
  300.2 7.9 %reduce-scatter.2.cloned.1.call-done = bf16[1024,256]{1,0:T(8,128)(2,1)} async-done(((bf16[16384,256]{1,0:T(8,128)(2,1)}), bf16[1024,256]{1,0:T(8,128)(2,1)}) %reduce-scatter.2.cloned.1.call-update) | async-done | bytes 524304 | tf_op jit(solution)/shard_map/reduce_scatter | solution.py:407
  308.0 1.7 fusion.1
  309.8 0.8 fusion.22
  (90 shorter events, 11.4 us)
Async XLA Ops:
  7.2 1.0 copy-start
  7.2 21.5 %copy-start.7 = (bf16[128,1024]{1,0:T(8,128)(2,1)S(1)}, bf16[128,1024]{1,0:T(8,128)(2,1)}, u32[]{:S(2)}) copy-start(bf16[128,1024]{1,0:T(8,128)(2,1)} %param.6) | copy-start | bytes 786436
  7.2 21.5 %copy-start.6 = (bf16[128,1024]{1,0:T(8,128)(2,1)S(1)}, bf16[128,1024]{1,0:T(8,128)(2,1)}, u32[]{:S(2)}) copy-start(bf16[128,1024]{1,0:T(8,128)(2,1)} %param.9) | copy-start | bytes 786436
  7.2 137.3 %all-gather.2.cloned.1.call-start = ((), (), s32[]{:S(2)}) async-start(), calls=%async_computation.12 | async-start | bytes 8912896 | tf_op jit(solution)/shard_map/all_gather | solution.py:306
  28.6 5.5 %copy-start.12 = (s32[2]{0:T(128)S(1)}, s32[2]{0:T(128)}, u32[]{:S(2)}) copy-start(s32[2]{0:T(128)} %param.11) | copy-start | bytes 28
  28.6 11.9 %copy-start.14 = (s32[16,1,3]{0,1,2:T(1,128)S(1)}, s32[16,1,3]{0,1,2:T(1,128)}, u32[]{:S(2)}) copy-start(s32[16,1,3]{0,1,2:T(1,128)} %param.10) | copy-start | bytes 580
  29.6 13.8 %all-to-all-start.2 = ((bf16[8,128,256]{2,1,0:T(8,128)(2,1)}), bf16[8,128,256]{2,1,0:T(8,128)(2,1)S(1)}, u32[]{:S(2)}, u32[]{:S(2)}) async-start(bf16[8,128,256]{2,1,0:T(8,128)(2,1)} %maximum_bitcast_fusion.1), calls=%async_computation.2 | async-start | bytes 1048576 | tf_op jit(solution)/shard_map/all_to_all | solution.py:55
  43.5 62.7 %copy-start.2 = (bf16[8,128,256]{2,1,0:T(8,128)(2,1)}, bf16[8,128,256]{2,1,0:T(8,128)(2,1)S(1)}, u32[]{:S(2)}) copy-start(bf16[8,128,256]{2,1,0:T(8,128)(2,1)S(1)} %all-to-all-done.2) | copy-start | bytes 1572868
  44.1 7.5 %all-to-all-start.1 = ((s32[4,16,3]{1,2,0:T(4,128)}), s32[4,16,3]{1,2,0:T(4,128)S(1)}, u32[]{:S(2)}, u32[]{:S(2)}) async-start(s32[4,16,3]{1,2,0:T(4,128)} %broadcast_in_dim.188), calls=%async_computation.1 | async-start | bytes 16384 | tf_op jit(solution)/shard_map/all_to_all | solution.py:55
  51.6 30.7 %all-to-all-start.3 = ((bf16[64,2,512]{2,1,0:T(2,128)(2,1)}), bf16[64,2,512]{2,1,0:T(2,128)(2,1)S(1)}, u32[]{:S(2)}, u32[]{:S(2)}) async-start(bf16[64,2,512]{2,1,0:T(2,128)(2,1)} %reshape.235), calls=%async_computation.3 | async-start | bytes 262144 | tf_op jit(solution)/shard_map/all_to_all | solution.py:55
  83.0 21.8 %all-to-all-start.4 = ((bf16[64,2,512]{2,1,0:T(2,128)(2,1)}), bf16[64,2,512]{2,1,0:T(2,128)(2,1)S(1)}, u32[]{:S(2)}, u32[]{:S(2)}) async-start(bf16[64,2,512]{2,1,0:T(2,128)(2,1)} %broadcast_in_dim.198), calls=%async_computation.4 | async-start | bytes 262144 | tf_op jit(solution)/shard_map/all_to_all | solution.py:55
  106.2 25.2 %all-to-all-start.5 = ((bf16[4,1024,256]{2,1,0:T(8,128)(2,1)}), bf16[4,1024,256]{2,1,0:T(8,128)(2,1)S(1)}, u32[]{:S(2)}, u32[]{:S(2)}) async-start(bf16[4,1024,256]{2,1,0:T(8,128)(2,1)} %broadcast_in_dim.204), calls=%async_computation.5 | async-start | bytes 4194304 | tf_op jit(solution)/shard_map/all_to_all | solution.py:55
  109.8 198.2 %reduce-scatter.2.cloned.1.call-start = ((), (), s32[]{:S(2)}) async-start(), calls=%async_computation.13 | async-start | bytes 8912896 | tf_op jit(solution)/shard_map/reduce_scatter | solution.py:407
  131.4 13.1 %copy-start.1 = (bf16[4,1024,256]{2,1,0:T(8,128)(2,1)}, bf16[4,1024,256]{2,1,0:T(8,128)(2,1)S(1)}, u32[]{:S(2)}) copy-start(bf16[4,1024,256]{2,1,0:T(8,128)(2,1)S(1)} %all-to-all-done.5) | copy-start | bytes 6291460
  186.7 0.7 copy-start.13
  188.0 27.8 %all-to-all-start.7 = ((f32[64,3,128]{2,1,0:T(4,128)}), f32[64,3,128]{2,1,0:T(4,128)S(1)}, u32[]{:S(2)}, u32[]{:S(2)}) async-start(f32[64,3,128]{2,1,0:T(4,128)} %broadcast_in_dim.206), calls=%async_computation.7 | async-start | bytes 262144 | tf_op jit(solution)/shard_map/all_to_all | solution.py:55
  215.8 0.7 copy-start.5
  250.7 21.9 %all-to-all-start.9 = ((bf16[64,4,256]{2,1,0:T(4,128)(2,1)}), bf16[64,4,256]{2,1,0:T(4,128)(2,1)S(1)}, u32[]{:S(2)}, u32[]{:S(2)}) async-start(bf16[64,4,256]{2,1,0:T(4,128)(2,1)} %broadcast_in_dim.207), calls=%async_computation.9 | async-start | bytes 262144 | tf_op jit(solution)/shard_map/all_to_all | solution.py:55
  272.6 25.6 %all-to-all-start.10 = ((bf16[4,1024,256]{2,1,0:T(8,128)(2,1)}), bf16[4,1024,256]{2,1,0:T(8,128)(2,1)S(1)}, u32[]{:S(2)}, u32[]{:S(2)}) async-start(bf16[4,1024,256]{2,1,0:T(8,128)(2,1)} %bitcast.25), calls=%async_computation.10 | async-start | bytes 4194304 | tf_op jit(solution)/shard_map/all_to_all | solution.py:55
  276.2 22.3 %copy-start.4 = (f32[1024,256]{1,0:T(8,128)S(1)}, f32[1024,256]{1,0:T(8,128)}, u32[]{:S(2)}) copy-start(f32[1024,256]{1,0:T(8,128)} %get-tuple-element.25) | copy-start | bytes 3145732
  298.2 0.8 copy-start.10
  298.2 0.8 copy-start.11
  298.5 9.5 %copy-start.3 = (f32[1024,256]{1,0:T(8,128)S(1)}, f32[1024,256]{1,0:T(8,128)}, u32[]{:S(2)}) copy-start(f32[1024,256]{1,0:T(8,128)} %get-tuple-element.27) | copy-start | bytes 3145732
  298.5 9.5 %copy-start.8 = (f32[64,256]{1,0:T(8,128)S(1)}, f32[64,256]{1,0:T(8,128)}, u32[]{:S(2)}) copy-start(f32[64,256]{1,0:T(8,128)} %get-tuple-element.42) | copy-start | bytes 196612
  298.5 9.5 %copy-start.9 = (f32[64,256]{1,0:T(8,128)S(1)}, f32[64,256]{1,0:T(8,128)}, u32[]{:S(2)}) copy-start(f32[64,256]{1,0:T(8,128)} %get-tuple-element.43) | copy-start | bytes 196612
Sparse Core Ops, SparseCore 0:
  28.7 115.6 all-gather.1
  186.8 121.1 reduce-scatter.1

commit v2 on v1

--- a/solution.py
+++ b/solution.py
@@ -167,18 +167,30 @@
             for s in range(SLOTS + 1)
         ]
     )
-    out_ref[0] = top
-    out_ref[1] = total
-    out_ref[2] = slope
+    first = jnp.concatenate([top, total], 1)
+    second = jnp.concatenate([slope, slope], 1)
+    for lane in range(out_ref.shape[0]):
+        out_ref[lane, :group, :] = first
+        out_ref[lane, group:, :] = second
 
 
 def edge_grads_kernel(
-    meta_ref, slot_ref, item_ref, cell_ref, qd_ref, kv_ref, parts_ref, table_ref, partial_ref, final_ref
+    meta_ref, slot_ref, item_ref, cell_ref, qd_ref, kv_ref, parts_ref, table_ref, final_ref, mixed_ref, *rest
 ):
+    sent_refs = rest[:-1]
+    partial_ref = rest[-1]
     group = qd_ref.shape[0] // S
+    tokens = mixed_ref.shape[0]
     lanes = parts_ref.shape[0]
     top, total, slope = merge(
-        [(parts_ref[lane, 0], parts_ref[lane, 1], parts_ref[lane, 2]) for lane in range(lanes)]
+        [
+            (
+                parts_ref[lane, :group, :S],
+                parts_ref[lane, :group, S:],
+                parts_ref[lane, group:, :S],
+            )
+            for lane in range(lanes)
+        ]
     )
     inverse = 1.0 / total
     final_ref[0] = top
@@ -191,10 +203,11 @@
         found = []
         for u in range(UNROLL):
             pos = t * UNROLL + u
-            live = slot_ref[pos] < SLOTS * group
-            item_pos = item_ref[pos]
+            slot = slot_ref[pos]
+            live = slot < SLOTS * group
+            item_pos = lax.rem(slot, group)
             cell = pl.multiple_of(cell_ref[pos] * S, S)
-            item = pl.multiple_of(item_pos * S, S)
+            item = pl.multiple_of(item_ref[pos] * S, S)
             key = kv_ref[pl.ds(cell, S), :D]
             value = kv_ref[pl.ds(cell, S), D:]
             q = qd_ref[pl.ds(item, S), :D]
@@ -227,10 +240,25 @@
         return carry
 
     lax.fori_loop(0, meta_ref[0], step, 0)
+    mixed_ref[...] = partial_ref[:tokens, :]
+    for shift, sent_ref in enumerate(sent_refs):
+        low = (shift + 1) * tokens
+        sent_ref[...] = partial_ref[low : low + tokens, :].astype(jnp.bfloat16)
 
 
 def own_grads_kernel(
-    meta_ref, bias_ref, flag_ref, qd_ref, kv_ref, shared_ref, final_ref, rows_ref, pairs_ref, mixed_ref, shared_grad_ref
+    meta_ref,
+    bias_ref,
+    flag_ref,
+    qd_ref,
+    kv_ref,
+    shared_ref,
+    final_ref,
+    rows_ref,
+    edge_ref,
+    pairs_ref,
+    mixed_ref,
+    shared_grad_ref,
 ):
     tokens = qd_ref.shape[0]
     blocks = tokens // S
@@ -280,11 +308,16 @@
         pairs_ref[low:high, D:] += dot_nn(prob, dout)
         global_dkey = global_dkey + dot_nn(global_dscore, q)
         global_dvalue = global_dvalue + dot_nn(global_prob, dout)
-        mixed_ref[i * S : (i + 1) * S, :D] = dot_tn(prob, kv_ref[low:high, D:]) + dot_tn(
-            global_prob, shared_ref[:, 3 * D :]
-        )
-        mixed_ref[i * S : (i + 1) * S, D:] = dot_tn(dscore, kv_ref[low:high, :D]) + dot_tn(
-            global_dscore, shared_ref[:, 2 * D : 3 * D]
+        at = slice(i * S, (i + 1) * S)
+        mixed_ref[at, :D] = (
+            edge_ref[at, :D]
+            + dot_tn(prob, kv_ref[low:high, D:])
+            + dot_tn(global_prob, shared_ref[:, 3 * D :])
+        )
+        mixed_ref[at, D:] = (
+            edge_ref[at, D:]
+            + dot_tn(dscore, kv_ref[low:high, :D])
+            + dot_tn(global_dscore, shared_ref[:, 2 * D : 3 * D])
         )
     shared_grad_ref[:G, :D] = global_dkey
     shared_grad_ref[:G, D:] = global_dvalue
@@ -320,14 +353,19 @@
                 [lax.dynamic_slice_in_dim(part, starts[g], S, 0) for part in (qd, kv)], 1
             )
         )
-    chunk = G // ctx_count
-    sent = jnp.concatenate(pieces, 0).reshape(ctx_count, chunk, 4 * D)
-    arrived = exchange(sent, CTX)
-    owner = owners[(ctx_place * chunk) // S]
-    picked = lax.dynamic_slice_in_dim(arrived, owner, 1, 0)[0]
-    shared = to_all(picked, CTX).reshape(G, 4 * D)
-
-    qd_group = to_all(qd, Y_AXIS).reshape(group * S, 2 * D)
+    part = G // y_count
+    owner = owners[(y_place * part) // S]
+    sent = jnp.concatenate(pieces, 0).reshape(y_count, part, 4 * D)
+    picked = lax.dynamic_index_in_dim(exchange(sent, Y_AXIS), owner % y_count, 0, False)
+    sent = picked.reshape(z_count, part // z_count, 4 * D)
+    picked = lax.dynamic_index_in_dim(exchange(sent, Z_AXIS), owner // y_count, 0, False)
+    shared = to_all(picked, Z_AXIS).reshape(part, 4 * D)
+    shared = to_all(shared, Y_AXIS).reshape(G, 4 * D)
+
+    shifts = range(1, y_count)
+    forward = [[(i, (i + shift) % y_count) for i in range(y_count)] for shift in shifts]
+    backward = [[(i, (i - shift) % y_count) for i in range(y_count)] for shift in shifts]
+    qd_group = jnp.concatenate([qd] + [lax.ppermute(qd, Y_AXIS, pairs) for pairs in forward], 0)
     random_group = to_all(random_blocks[:, 0, :], Y_AXIS).reshape(group, RANDOM)
 
     ids = z_place * group + jnp.arange(group, dtype=jnp.int32)
@@ -356,7 +394,8 @@
     slot_list = jnp.sum(jnp.where(hit, order[None, :], 0), 1)
     cell_list = jnp.sum(jnp.where(hit, cell[None, :], 0), 1)
     slot_list = jnp.where(order < edge_count, slot_list, entries + group)
-    item_list = jnp.where(order < edge_count, slot_list % group, 0)
+    item_list = slot_list % group
+    item_list = (y_place - item_list // block_count) % y_count * block_count + item_list % block_count
     meta = jnp.stack([(edge_count + UNROLL - 1) // UNROLL, y_place]).astype(jnp.int32)
     lists = (meta, slot_list, item_list, cell_list)
 
@@ -378,33 +417,38 @@
         compiler_params=PARAMS,
         name="own_stats",
     )(bias, qd, kv, shared)
-    rows_all = to_all(rows, CTX)
+    rows_all = to_all(rows, Z_AXIS)
+    own, rows_all = lax.optimization_barrier((own, rows_all))
 
     stat_rows = (SLOTS + 1) * group + 8
     stats = pl.pallas_call(
         edge_stats_kernel,
-        out_shape=jax.ShapeDtypeStruct((3, group, S), f32),
+        out_shape=jax.ShapeDtypeStruct((y_count, 2 * group, 2 * S), f32),
         in_specs=[SMEM] * 4 + [VMEM] * 3,
         out_specs=VMEM,
         scratch_shapes=[pltpu.VMEM((stat_rows, S), f32)] * 3,
         compiler_params=PARAMS,
         name="edge_stats",
     )(*lists, qd_group, kv_all, own)
-    parts = to_all(stats, Y_AXIS)
-
-    table, partial, final = pl.pallas_call(
+    parts = exchange(stats, Y_AXIS)
+
+    table, final, edge_mixed, *halves = pl.pallas_call(
         edge_grads_kernel,
         out_shape=(
             jax.ShapeDtypeStruct((cells * S, 2 * D), jnp.bfloat16),
-            jax.ShapeDtypeStruct((group * S, 2 * D), f32),
             jax.ShapeDtypeStruct((3, group, S), f32),
-        ),
+            jax.ShapeDtypeStruct((tokens, 2 * D), f32),
+        )
+        + (jax.ShapeDtypeStruct((tokens, 2 * D), jnp.bfloat16),) * (y_count - 1),
         in_specs=[SMEM] * 4 + [VMEM] * 3,
-        out_specs=(VMEM, VMEM, VMEM),
+        out_specs=(VMEM,) * (y_count + 2),
+        scratch_shapes=[pltpu.VMEM((group * S, 2 * D), f32)],
         compiler_params=PARAMS,
         name="edge_grads",
     )(*lists, qd_group, kv_all, parts)
     returned = lax.psum_scatter(table, Z_AXIS, scatter_dimension=0, tiled=True)
+    halves = [lax.ppermute(half, Y_AXIS, pairs) for half, pairs in zip(halves, backward)]
+    rows_all = to_all(rows_all, Y_AXIS).reshape(ctx_count, 3, G)
 
     pairs, mixed, shared_grads = pl.pallas_call(
         own_grads_kernel,
@@ -413,22 +457,22 @@
             jax.ShapeDtypeStruct((tokens, 2 * D), f32),
             jax.ShapeDtypeStruct((2 * G, 2 * D), f32),
         ),
-        in_specs=[SMEM] * 3 + [VMEM] * 5,
+        in_specs=[SMEM] * 3 + [VMEM] * 6,
         out_specs=(VMEM, VMEM, VMEM),
         compiler_params=PARAMS,
         name="own_grads",
-    )(meta, bias, flags, qd, kv, shared, final, rows_all)
-
-    spread = exchange(
-        shared_grads.astype(jnp.bfloat16).reshape(ctx_count, 2 * G // ctx_count, 2 * D), CTX
-    )
-    summed = jnp.sum(spread.astype(f32), 0).astype(jnp.bfloat16)
-    shared_sums = to_all(summed, CTX).reshape(2, WORLDWIDE_COUNT, 1, S, 2 * D).astype(f32)
-
-    halves = exchange(
-        partial.astype(jnp.bfloat16).reshape(y_count, tokens, 2 * D), Y_AXIS
-    ).astype(f32)
-    mixed = (jnp.sum(halves, 0) + mixed).reshape(block_count, S, 2 * D)
+    )(meta, bias, flags, qd, kv, shared, final, rows_all, edge_mixed)
+
+    summed = shared_grads.astype(jnp.bfloat16)
+    for axis in (Y_AXIS, Z_AXIS):
+        count = lax.axis_size(axis)
+        summed = exchange(summed.reshape(count, -1, 2 * D), axis)
+        summed = jnp.sum(summed.astype(f32), 0).astype(jnp.bfloat16)
+    for axis in (Z_AXIS, Y_AXIS):
+        summed = to_all(summed, axis).reshape(-1, 2 * D)
+    shared_sums = summed.reshape(2, WORLDWIDE_COUNT, 1, S, 2 * D).astype(f32)
+
+    mixed = sum([half.astype(f32) for half in halves], mixed).reshape(block_count, S, 2 * D)
     pairs = (returned.astype(f32) + pairs).reshape(block_count, S, 2 * D)
     for g in range(WORLDWIDE_COUNT):
         mask = hits[:, g][:, None, None]

time: 319 us -> 307 us (0.962)
  waiting for transfers between devices: 113 us -> 89.3 us
  starting transfers between devices: 51.3 us -> 66.4 us
  local copies, waits for them, and re-layouts: 22.5 us -> 18.3 us
    all_to_all x8 -> x10, waiting for transfers between devices: 92.4 us -> 54.6 us  [exchange(): return lax.all_to_all(array, axes, split_axis=0, concat_axis=0, tiled=True)]
    reduce_scatter x1, waiting for transfers between devices: 7.85 us -> 34.7 us  [body(): returned = lax.psum_scatter(table, Z_AXIS, scatter_dimension=0, tiled=True)]
    ppermute x0 -> x6, starting transfers between devices: none -> 18.6 us  [the longest x3 10.7 us: body(): lax.ppermute(qd, Y_AXIS, pairs)]
    all_gather x1, waiting for transfers between devices: 13.1 us -> 0.01 us  [body(): kv_all = lax.all_gather(kv, Z_AXIS, axis=0, tiled=True)]
    convert_element_type x2, other arithmetic: 4.8 us -> 1.07 us  [the longest x1 1.05 us: body(): summed = shared_grads.astype(jnp.bfloat16)]
    all_to_all x8 -> x10, starting transfers between devices: 51.3 us -> 47.7 us  [exchange(): return lax.all_to_all(array, axes, split_axis=0, concat_axis=0, tiled=True)]
    concatenate x1 -> x2, other arithmetic: 0.01 us -> 3.26 us  [the longest x1 2.54 us: body(): jnp.concatenate([qd] + [lax.ppermute(qd, Y_AXIS, pairs) for pairs in forw...]
    all_to_all x3 -> x4, blocking collectives: 52.8 us -> 53.4 us  [exchange(): return lax.all_to_all(array, axes, split_axis=0, concat_axis=0, tiled=True)]
  transfers between devices with their start and end apart: 10 -> 18, of which waited for: 10 -> 10; matrix products, arithmetic and copies ran while one was open for 8% -> 9% of each run, Pallas kernels for 4% -> 4%
where the time goes in v2:
time: 307 us; the launch traced here: 304 us
  waiting for transfers between devices  89.3 us (29%)
  starting transfers between devices  66.4 us (22%)
  blocking collectives  53.4 us (17%)
  Pallas kernels  38.6 us (13%)
  between operations  23.6 us (8%)
  local copies, waits for them, and re-layouts  18.3 us (6%)
  other arithmetic  14.9 us (5%)
    all_to_all x10, waiting for transfers between devices, exchange(): return lax.all_to_all(array, axes, split_axis=0, concat_axis=0, tiled=True)  54.6 us
    all_to_all x4, blocking collectives, exchange(): return lax.all_to_all(array, axes, split_axis=0, concat_axis=0, tiled=True)  53.4 us
    all_to_all x10, starting transfers between devices, exchange(): return lax.all_to_all(array, axes, split_axis=0, concat_axis=0, tiled=True)  47.7 us
    reduce_scatter x1, waiting for transfers between devices, body(): returned = lax.psum_scatter(table, Z_AXIS, scatter_dimension=0, tiled=True)  34.7 us
    pallas_call x1, Pallas kernels, body(): pl.pallas_call(edge_grads_kernel, out_shape=(jax.ShapeDtypeStruct((cells...  18.6 us
    ppermute x3, starting transfers between devices, body(): lax.ppermute(qd, Y_AXIS, pairs)  10.7 us
    pallas_call x1, Pallas kernels, body(): pl.pallas_call(own_grads_kernel, out_shape=(jax.ShapeDtypeStruct((tokens,...  9.34 us
    ppermute x3, starting transfers between devices, body(): lax.ppermute(half, Y_AXIS, pairs)  7.92 us
  transfers between devices with their start and end apart: 18, of which 10 were waited for; matrix products, arithmetic and copies ran while one was open for 9% of the time, Pallas kernels for 4%

profile of v2, /device:TPU:1, one launch (start us, length us, event | category | flops | bytes accessed | tf_op | source)
XLA Modules:
  0.0 304.5 jit_solution(15249263258124520251)
XLA Ops:
  7.2 0.9 copy-done
  8.1 1.1 copy_bitcast_fusion.2
  9.3 19.2 %all_to_all.70 = bf16[8,128,256]{2,1,0:T(8,128)(2,1)} all-to-all(bf16[8,128,256]{2,1,0:T(8,128)(2,1)S(1)} %maximum_bitcast_fusion), channel_id=1, replica_groups=mesh['ctx_0'=16,'ctx_1'=4,'head'=8] {'head'}, dimensions={0} | all-to-all | bytes 1048576 | tf_op jit(solution)/shard_map/all_to_all | solution.py:55
  35.6 0.7 compare_reduce_fusion
  37.7 1.3 fusion.26
  41.6 3.3 %all-to-all-start.1 = ((s32[4,16,3]{1,2,0:T(4,128)}), s32[4,16,3]{1,2,0:T(4,128)S(1)}, u32[]{:S(2)}, u32[]{:S(2)}) async-start(s32[4,16,3]{1,2,0:T(4,128)} %broadcast_in_dim.197), calls=%async_computation.1 | async-start | bytes 16384 | tf_op jit(solution)/shard_map/all_to_all | solution.py:55
  44.9 1.0 copy_bitcast_fusion
  46.0 0.9 maximum_bitcast_fusion.1
  46.8 0.8 constant_dynamic-slice_fusion.3
  47.6 1.5 all-to-all-done.1
  49.1 5.5 %all-to-all-start.2 = ((bf16[8,128,256]{2,1,0:T(8,128)(2,1)}), bf16[8,128,256]{2,1,0:T(8,128)(2,1)S(1)}, u32[]{:S(2)}, u32[]{:S(2)}) async-start(bf16[8,128,256]{2,1,0:T(8,128)(2,1)} %maximum_bitcast_fusion.1), calls=%async_computation.2 | async-start | bytes 1048576 | tf_op jit(solution)/shard_map/all_to_all | solution.py:55
  59.1 4.9 %all-to-all-done.2 = bf16[8,128,256]{2,1,0:T(8,128)(2,1)S(1)} async-done(((bf16[8,128,256]{2,1,0:T(8,128)(2,1)}), bf16[8,128,256]{2,1,0:T(8,128)(2,1)S(1)}, u32[]{:S(2)}, u32[]{:S(2)}) %all-to-all-start.2) | async-done | bytes 524320 | tf_op jit(solution)/shard_map/all_to_all | solution.py:55
  64.7 3.3 %all-to-all-start.3 = ((bf16[4,32,512]{2,1,0:T(8,128)(2,1)}), bf16[4,32,512]{2,1,0:T(8,128)(2,1)S(1)}, u32[]{:S(2)}, u32[]{:S(2)}) async-start(bf16[4,32,512]{2,1,0:T(8,128)(2,1)} %bitcast.15), calls=%async_computation.3 | async-start | bytes 262144 | tf_op jit(solution)/shard_map/all_to_all | solution.py:55
  68.9 3.3 %collective-permute-start = (bf16[1024,256]{1,0:T(8,128)(2,1)S(1)}, bf16[1024,256]{1,0:T(8,128)(2,1)S(1)}, u32[]{:S(2)}, u32[]{:S(2)}) collective-permute-start(bf16[1024,256]{1,0:T(8,128)(2,1)S(1)} %bitcast.93), channel_id=1, source_target_pairs={{0,8},{8,16},{16,24},{24,0},{1,9},{9,17},{17,25},{25,1},{2,10},{10... | collective-permute-start | bytes 1572872 | tf_op jit(solution)/shard_map/ppermute | solution.py:368
  72.2 4.3 %collective-permute-start.1 = (bf16[1024,256]{1,0:T(8,128)(2,1)S(1)}, bf16[1024,256]{1,0:T(8,128)(2,1)S(1)}, u32[]{:S(2)}, u32[]{:S(2)}) collective-permute-start(bf16[1024,256]{1,0:T(8,128)(2,1)S(1)} %bitcast.94), channel_id=1, source_target_pairs={{0,16},{8,24},{16,0},{24,8},{1,17},{9,25},{17,1},{25,9},{2,18},{10... | collective-permute-start | bytes 1572872 | tf_op jit(solution)/shard_map/ppermute | solution.py:368
  76.5 3.1 %collective-permute-start.2 = (bf16[1024,256]{1,0:T(8,128)(2,1)S(1)}, bf16[1024,256]{1,0:T(8,128)(2,1)S(1)}, u32[]{:S(2)}, u32[]{:S(2)}) collective-permute-start(bf16[1024,256]{1,0:T(8,128)(2,1)S(1)} %bitcast.95), channel_id=1, source_target_pairs={{0,24},{8,0},{16,8},{24,16},{1,25},{9,1},{17,9},{25,17},{2,26},{10... | collective-permute-start | bytes 1572872 | tf_op jit(solution)/shard_map/ppermute | solution.py:368
  80.3 11.9 %all-to-all-start.4 = ((bf16[16,2,512]{2,1,0:T(2,128)(2,1)}), bf16[16,2,512]{2,1,0:T(2,128)(2,1)S(1)}, u32[]{:S(2)}, u32[]{:S(2)}) async-start(bf16[16,2,512]{2,1,0:T(2,128)(2,1)} %reshape.240), calls=%async_computation.4 | async-start | bytes 65536 | tf_op jit(solution)/shard_map/all_to_all | solution.py:55
  92.9 11.1 %all-to-all-done.4 = bf16[16,2,512]{2,1,0:T(2,128)(2,1)S(1)} async-done(((bf16[16,2,512]{2,1,0:T(2,128)(2,1)}), bf16[16,2,512]{2,1,0:T(2,128)(2,1)S(1)}, u32[]{:S(2)}, u32[]{:S(2)}) %all-to-all-start.4) | async-done | bytes 32800 | tf_op jit(solution)/shard_map/all_to_all | solution.py:55
  104.7 3.5 %all-to-all-start.5 = ((bf16[16,2,512]{2,1,0:T(2,128)(2,1)}), bf16[16,2,512]{2,1,0:T(2,128)(2,1)S(1)}, u32[]{:S(2)}, u32[]{:S(2)}) async-start(bf16[16,2,512]{2,1,0:T(2,128)(2,1)} %broadcast_in_dim.207), calls=%async_computation.5 | async-start | bytes 65536 | tf_op jit(solution)/shard_map/all_to_all | solution.py:55
  108.8 11.2 %all-to-all-done.5 = bf16[16,2,512]{2,1,0:T(2,128)(2,1)S(1)} async-done(((bf16[16,2,512]{2,1,0:T(2,128)(2,1)}), bf16[16,2,512]{2,1,0:T(2,128)(2,1)S(1)}, u32[]{:S(2)}, u32[]{:S(2)}) %all-to-all-start.5) | async-done | bytes 32800 | tf_op jit(solution)/shard_map/all_to_all | solution.py:55
  120.7 3.3 %all-to-all-start.6 = ((bf16[4,32,512]{2,1,0:T(8,128)(2,1)}), bf16[4,32,512]{2,1,0:T(8,128)(2,1)S(1)}, u32[]{:S(2)}, u32[]{:S(2)}) async-start(bf16[4,32,512]{2,1,0:T(8,128)(2,1)} %broadcast_in_dim.209), calls=%async_computation.6 | async-start | bytes 262144 | tf_op jit(solution)/shard_map/all_to_all | solution.py:55
  124.7 4.2 %all-to-all-done.6 = bf16[4,32,512]{2,1,0:T(8,128)(2,1)S(1)} async-done(((bf16[4,32,512]{2,1,0:T(8,128)(2,1)}), bf16[4,32,512]{2,1,0:T(8,128)(2,1)S(1)}, u32[]{:S(2)}, u32[]{:S(2)}) %all-to-all-start.6) | async-done | bytes 131104 | tf_op jit(solution)/shard_map/all_to_all | solution.py:55
  129.5 3.5 %own_stats.1 = (f32[3,16,64]{2,1,0:T(8,128)}, f32[3,128]{1,0:T(4,128)}) custom-call(f32[32]{0:T(128)} %reshape.235.bias_ref, bf16[1024,256]{1,0:T(8,128)(2,1)} %bitcast.96, bf16[1024,256]{1,0:T(8,128)(2,1)} %bitcast.90, bf16[128,512]{1,0:T(8,128)(2,1)} %bitcast.99), custom_call_target="tpu_custom_call" | custom-call | tf_op jit(solution)/shard_map/own_stats/pallas_call | solution.py:409
  133.0 1.3 broadcast_in_dim.215
  134.3 3.5 %all-to-all-start.7 = ((f32[16,3,128]{2,1,0:T(4,128)}), f32[16,3,128]{2,1,0:T(4,128)S(1)}, u32[]{:S(2)}, u32[]{:S(2)}) async-start(f32[16,3,128]{2,1,0:T(4,128)} %broadcast_in_dim.215), calls=%async_computation.7 | async-start | bytes 65536 | tf_op jit(solution)/shard_map/all_to_all | solution.py:55
  137.9 2.5 pad_maximum_fusion.qd_ref
  140.4 8.7 %all-to-all-done.7 = f32[16,3,128]{2,1,0:T(4,128)S(1)} async-done(((f32[16,3,128]{2,1,0:T(4,128)}), f32[16,3,128]{2,1,0:T(4,128)S(1)}, u32[]{:S(2)}, u32[]{:S(2)}) %all-to-all-start.7) | async-done | bytes 24608 | tf_op jit(solution)/shard_map/all_to_all | solution.py:55
  149.2 7.2 %edge_stats.1 = f32[4,128,128]{2,1,0:T(8,128)} custom-call(s32[2]{0:T(128)} %pad_add_fusion.1.meta_ref, s32[256]{0:T(256)} %get-tuple-element.43.slot_ref, s32[256]{0:T(256)} %get-tuple-element.42.item_ref, s32[256]{0:T(256)} %get-tuple-element.38.cell_ref, bf16[4096,256]{1,0:T(8,128)(2,1)} %pad_maximum_fusion.qd_ref, ...), custom_call_target="tpu_custom_call" | custom-call | tf_op jit(solution)/shard_map/edge_stats/pallas_call | solution.py:424
  156.4 9.6 %all_to_all.71.parts_ref = f32[4,128,128]{2,1,0:T(8,128)} all-to-all(f32[4,128,128]{2,1,0:T(8,128)} %edge_stats.1), channel_id=1, replica_groups=mesh['ctx_0'=16,'ctx_1'=4,'head'=8] {'ctx_1'}, dimensions={0} | all-to-all | bytes 524288 | tf_op jit(solution)/shard_map/all_to_all | solution.py:55
  166.0 18.6 %edge_grads.1 = (bf16[16384,256]{1,0:T(8,128)(2,1)}, f32[3,64,64]{2,1,0:T(8,128)}, f32[1024,256]{1,0:T(8,128)}, bf16[1024,256]{1,0:T(8,128)(2,1)}, bf16[1024,256]{1,0:T(8,128)(2,1)}, /*index=5*/bf16[1024,256]{1,0:T(8,128)(2,1)}) custom-call(s32[2]{0:T(128)} %pad_add_fusion.1.meta_ref, s32[256]{0:T(256)} %get-tuple-element.43.slot_ref, ...), custom_call_target="tpu_custom_call" | custom-call | tf_op jit(solution)/shard_map/edge_grads/pallas_call | solution.py:435
  185.4 6.5 %all-to-all-start.9 = ((f32[4,16,3,128]{3,1,2,0:T(8,128)}), f32[4,16,3,128]{3,1,2,0:T(8,128)S(1)}, u32[]{:S(2)}, u32[]{:S(2)}) async-start(f32[4,16,3,128]{3,1,2,0:T(8,128)} %broadcast_in_dim.216), calls=%async_computation.9 | async-start | bytes 196608 | tf_op jit(solution)/shard_map/all_to_all | solution.py:55
  192.5 4.1 %all-to-all-done.9 = f32[4,16,3,128]{3,1,2,0:T(8,128)S(1)} async-done(((f32[4,16,3,128]{3,1,2,0:T(8,128)}), f32[4,16,3,128]{3,1,2,0:T(8,128)S(1)}, u32[]{:S(2)}, u32[]{:S(2)}) %all-to-all-start.9) | async-done | bytes 98336 | tf_op jit(solution)/shard_map/all_to_all | solution.py:55
  197.3 9.3 %own_grads.1 = (f32[1024,256]{1,0:T(8,128)}, f32[1024,256]{1,0:T(8,128)}, f32[256,256]{1,0:T(8,128)}) custom-call(s32[2]{0:T(128)} %pad_add_fusion.1.meta_ref, f32[32]{0:T(128)} %reshape.235.bias_ref, f32[16]{0:T(128)} %broadcast_select_fusion.flag_ref, bf16[1024,256]{1,0:T(8,128)(2,1)} %bitcast.98, bf16[1024,256]{1,0:T(8,128)(2,1)} %bitcast.91, ...), custom_call_target="tpu_custom_call" | custom-call | tf_op jit(solution)/shard_map/own_grads/pallas_call | solution.py:453
  206.6 1.1 convert_element_type.48
  207.7 7.2 %all_to_all.72 = bf16[4,64,256]{2,1,0:T(8,128)(2,1)S(1)} all-to-all(bf16[4,64,256]{2,1,0:T(8,128)(2,1)S(1)} %bitcast.103), channel_id=1, replica_groups=mesh['ctx_0'=16,'ctx_1'=4,'head'=8] {'ctx_1'}, dimensions={0} | all-to-all | bytes 262144 | tf_op jit(solution)/shard_map/all_to_all | solution.py:55
  215.0 17.3 %all_to_all.73 = bf16[16,4,256]{2,1,0:T(4,128)(2,1)S(1)} all-to-all(bf16[16,4,256]{2,1,0:T(4,128)(2,1)S(1)} %reshape.244), channel_id=1, replica_groups=mesh['ctx_0'=16,'ctx_1'=4,'head'=8] {'ctx_0'}, dimensions={0} | all-to-all | bytes 65536 | tf_op jit(solution)/shard_map/all_to_all | solution.py:55
  232.9 3.5 %all-to-all-start.12 = ((bf16[16,4,256]{2,1,0:T(4,128)(2,1)}), bf16[16,4,256]{2,1,0:T(4,128)(2,1)S(1)}, u32[]{:S(2)}, u32[]{:S(2)}) async-start(bf16[16,4,256]{2,1,0:T(4,128)(2,1)} %broadcast_in_dim.217), calls=%async_computation.12 | async-start | bytes 65536 | tf_op jit(solution)/shard_map/all_to_all | solution.py:55
  236.4 2.8 collective-permute-start.3
  239.2 3.2 %collective-permute-start.4 = (bf16[1024,256]{1,0:T(8,128)(2,1)}, bf16[1024,256]{1,0:T(8,128)(2,1)S(1)}, u32[]{:S(2)}, u32[]{:S(2)}) collective-permute-start(bf16[1024,256]{1,0:T(8,128)(2,1)} %get-tuple-element.34), channel_id=1, source_target_pairs={{0,16},{8,24},{16,0},{24,8},{1,17},{9,25},{17,1},{25,9},{2,18},{10... | collective-permute-start | bytes 1572872 | tf_op jit(solution)/shard_map/ppermute | solution.py:450
  242.4 1.9 collective-permute-start.5
  244.4 4.0 %all-to-all-done.12 = bf16[16,4,256]{2,1,0:T(4,128)(2,1)S(1)} async-done(((bf16[16,4,256]{2,1,0:T(4,128)(2,1)}), bf16[16,4,256]{2,1,0:T(4,128)(2,1)S(1)}, u32[]{:S(2)}, u32[]{:S(2)}) %all-to-all-start.12) | async-done | bytes 32800 | tf_op jit(solution)/shard_map/all_to_all | solution.py:55
  249.0 3.3 %all-to-all-start.13 = ((bf16[4,64,256]{2,1,0:T(8,128)(2,1)}), bf16[4,64,256]{2,1,0:T(8,128)(2,1)S(1)}, u32[]{:S(2)}, u32[]{:S(2)}) async-start(bf16[4,64,256]{2,1,0:T(8,128)(2,1)} %broadcast_in_dim.219), calls=%async_computation.13 | async-start | bytes 262144 | tf_op jit(solution)/shard_map/all_to_all | solution.py:55
  252.7 4.8 %all-to-all-done.13 = bf16[4,64,256]{2,1,0:T(8,128)(2,1)S(1)} async-done(((bf16[4,64,256]{2,1,0:T(8,128)(2,1)}), bf16[4,64,256]{2,1,0:T(8,128)(2,1)S(1)}, u32[]{:S(2)}, u32[]{:S(2)}) %all-to-all-start.13) | async-done | bytes 131104 | tf_op jit(solution)/shard_map/all_to_all | solution.py:55
  257.6 1.9 fusion.4
  259.5 0.8 fusion.24
  260.3 34.7 %reduce-scatter.2.cloned.1.call-done = bf16[1024,256]{1,0:T(8,128)(2,1)} async-done(((bf16[16384,256]{1,0:T(8,128)(2,1)}), bf16[1024,256]{1,0:T(8,128)(2,1)}) %reduce-scatter.2.cloned.1.call-update) | async-done | bytes 524304 | tf_op jit(solution)/shard_map/reduce_scatter | solution.py:449
  295.0 1.8 fusion.1
  296.8 0.8 fusion.23
  (92 shorter events, 16.4 us)
Async XLA Ops:
  7.2 1.0 copy-start
  7.2 38.7 %copy-start.4 = (bf16[128,1024]{1,0:T(8,128)(2,1)S(1)}, bf16[128,1024]{1,0:T(8,128)(2,1)}, u32[]{:S(2)}) copy-start(bf16[128,1024]{1,0:T(8,128)(2,1)} %param.6) | copy-start | bytes 786436
  7.2 47.5 %copy-start.5 = (s32[2]{0:T(128)S(1)}, s32[2]{0:T(128)}, u32[]{:S(2)}) copy-start(s32[2]{0:T(128)} %param.11) | copy-start | bytes 28
  7.2 142.0 %all-gather.2.cloned.1.call-start = ((), (), s32[]{:S(2)}) async-start(), calls=%async_computation.15 | async-start | bytes 8912896 | tf_op jit(solution)/shard_map/all_gather | solution.py:339
  41.6 7.5 %all-to-all-start.1 = ((s32[4,16,3]{1,2,0:T(4,128)}), s32[4,16,3]{1,2,0:T(4,128)S(1)}, u32[]{:S(2)}, u32[]{:S(2)}) async-start(s32[4,16,3]{1,2,0:T(4,128)} %broadcast_in_dim.197), calls=%async_computation.1 | async-start | bytes 16384 | tf_op jit(solution)/shard_map/all_to_all | solution.py:55
  49.1 14.9 %all-to-all-start.2 = ((bf16[8,128,256]{2,1,0:T(8,128)(2,1)}), bf16[8,128,256]{2,1,0:T(8,128)(2,1)S(1)}, u32[]{:S(2)}, u32[]{:S(2)}) async-start(bf16[8,128,256]{2,1,0:T(8,128)(2,1)} %maximum_bitcast_fusion.1), calls=%async_computation.2 | async-start | bytes 1048576 | tf_op jit(solution)/shard_map/all_to_all | solution.py:55
  64.0 64.9 %copy-start.1 = (bf16[8,128,256]{2,1,0:T(8,128)(2,1)}, bf16[8,128,256]{2,1,0:T(8,128)(2,1)S(1)}, u32[]{:S(2)}) copy-start(bf16[8,128,256]{2,1,0:T(8,128)(2,1)S(1)} %all-to-all-done.2) | copy-start | bytes 1572868
  64.7 14.9 %all-to-all-start.3 = ((bf16[4,32,512]{2,1,0:T(8,128)(2,1)}), bf16[4,32,512]{2,1,0:T(8,128)(2,1)S(1)}, u32[]{:S(2)}, u32[]{:S(2)}) async-start(bf16[4,32,512]{2,1,0:T(8,128)(2,1)} %bitcast.15), calls=%async_computation.3 | async-start | bytes 262144 | tf_op jit(solution)/shard_map/all_to_all | solution.py:55
  68.9 69.0 %collective-permute-start = (bf16[1024,256]{1,0:T(8,128)(2,1)S(1)}, bf16[1024,256]{1,0:T(8,128)(2,1)S(1)}, u32[]{:S(2)}, u32[]{:S(2)}) collective-permute-start(bf16[1024,256]{1,0:T(8,128)(2,1)S(1)} %bitcast.93), channel_id=1, source_target_pairs={{0,8},{8,16},{16,24},{24,0},{1,9},{9,17},{17,25},{25,1},{2,10},{10... | collective-permute-start | bytes 1572872 | tf_op jit(solution)/shard_map/ppermute | solution.py:368
  72.2 65.7 %collective-permute-start.1 = (bf16[1024,256]{1,0:T(8,128)(2,1)S(1)}, bf16[1024,256]{1,0:T(8,128)(2,1)S(1)}, u32[]{:S(2)}, u32[]{:S(2)}) collective-permute-start(bf16[1024,256]{1,0:T(8,128)(2,1)S(1)} %bitcast.94), channel_id=1, source_target_pairs={{0,16},{8,24},{16,0},{24,8},{1,17},{9,25},{17,1},{25,9},{2,18},{10... | collective-permute-start | bytes 1572872 | tf_op jit(solution)/shard_map/ppermute | solution.py:368
  76.5 61.4 %collective-permute-start.2 = (bf16[1024,256]{1,0:T(8,128)(2,1)S(1)}, bf16[1024,256]{1,0:T(8,128)(2,1)S(1)}, u32[]{:S(2)}, u32[]{:S(2)}) collective-permute-start(bf16[1024,256]{1,0:T(8,128)(2,1)S(1)} %bitcast.95), channel_id=1, source_target_pairs={{0,24},{8,0},{16,8},{24,16},{1,25},{9,1},{17,9},{25,17},{2,26},{10... | collective-permute-start | bytes 1572872 | tf_op jit(solution)/shard_map/ppermute | solution.py:368
  80.3 23.8 %all-to-all-start.4 = ((bf16[16,2,512]{2,1,0:T(2,128)(2,1)}), bf16[16,2,512]{2,1,0:T(2,128)(2,1)S(1)}, u32[]{:S(2)}, u32[]{:S(2)}) async-start(bf16[16,2,512]{2,1,0:T(2,128)(2,1)} %reshape.240), calls=%async_computation.4 | async-start | bytes 65536 | tf_op jit(solution)/shard_map/all_to_all | solution.py:55
  104.7 15.3 %all-to-all-start.5 = ((bf16[16,2,512]{2,1,0:T(2,128)(2,1)}), bf16[16,2,512]{2,1,0:T(2,128)(2,1)S(1)}, u32[]{:S(2)}, u32[]{:S(2)}) async-start(bf16[16,2,512]{2,1,0:T(2,128)(2,1)} %broadcast_in_dim.207), calls=%async_computation.5 | async-start | bytes 65536 | tf_op jit(solution)/shard_map/all_to_all | solution.py:55
  120.7 8.2 %all-to-all-start.6 = ((bf16[4,32,512]{2,1,0:T(8,128)(2,1)}), bf16[4,32,512]{2,1,0:T(8,128)(2,1)S(1)}, u32[]{:S(2)}, u32[]{:S(2)}) async-start(bf16[4,32,512]{2,1,0:T(8,128)(2,1)} %broadcast_in_dim.209), calls=%async_computation.6 | async-start | bytes 262144 | tf_op jit(solution)/shard_map/all_to_all | solution.py:55
  128.9 0.7 copy-start.2
  134.3 14.9 %all-to-all-start.7 = ((f32[16,3,128]{2,1,0:T(4,128)}), f32[16,3,128]{2,1,0:T(4,128)S(1)}, u32[]{:S(2)}, u32[]{:S(2)}) async-start(f32[16,3,128]{2,1,0:T(4,128)} %broadcast_in_dim.215), calls=%async_computation.7 | async-start | bytes 65536 | tf_op jit(solution)/shard_map/all_to_all | solution.py:55
  137.8 157.2 %reduce-scatter.2.cloned.1.call-start = ((), (), s32[]{:S(2)}) async-start(), calls=%async_computation.16 | async-start | bytes 8912896 | tf_op jit(solution)/shard_map/reduce_scatter | solution.py:449
  184.6 57.8 %copy-start.6 = (bf16[1024,256]{1,0:T(8,128)(2,1)S(1)}, bf16[1024,256]{1,0:T(8,128)(2,1)}, u32[]{:S(2)}) copy-start(bf16[1024,256]{1,0:T(8,128)(2,1)} %get-tuple-element.35) | copy-start | bytes 1572868
  185.4 11.2 %all-to-all-start.9 = ((f32[4,16,3,128]{3,1,2,0:T(8,128)}), f32[4,16,3,128]{3,1,2,0:T(8,128)S(1)}, u32[]{:S(2)}, u32[]{:S(2)}) async-start(f32[4,16,3,128]{3,1,2,0:T(8,128)} %broadcast_in_dim.216), calls=%async_computation.9 | async-start | bytes 196608 | tf_op jit(solution)/shard_map/all_to_all | solution.py:55
  206.6 88.4 %copy-start.3 = (f32[1024,256]{1,0:T(8,128)S(1)}, f32[1024,256]{1,0:T(8,128)}, u32[]{:S(2)}) copy-start(f32[1024,256]{1,0:T(8,128)} %get-tuple-element.37) | copy-start | bytes 3145732
  232.9 15.4 %all-to-all-start.12 = ((bf16[16,4,256]{2,1,0:T(4,128)(2,1)}), bf16[16,4,256]{2,1,0:T(4,128)(2,1)S(1)}, u32[]{:S(2)}, u32[]{:S(2)}) async-start(bf16[16,4,256]{2,1,0:T(4,128)(2,1)} %broadcast_in_dim.217), calls=%async_computation.12 | async-start | bytes 65536 | tf_op jit(solution)/shard_map/all_to_all | solution.py:55
  236.4 21.2 %collective-permute-start.3 = (bf16[1024,256]{1,0:T(8,128)(2,1)}, bf16[1024,256]{1,0:T(8,128)(2,1)S(1)}, u32[]{:S(2)}, u32[]{:S(2)}) collective-permute-start(bf16[1024,256]{1,0:T(8,128)(2,1)} %get-tuple-element.33), channel_id=1, source_target_pairs={{0,24},{8,0},{16,8},{24,16},{1,25},{9,1},{17,9},{25,17},{2,26},{10... | collective-permute-start | bytes 1572872 | tf_op jit(solution)/shard_map/ppermute | solution.py:450
  239.2 18.4 %collective-permute-start.4 = (bf16[1024,256]{1,0:T(8,128)(2,1)}, bf16[1024,256]{1,0:T(8,128)(2,1)S(1)}, u32[]{:S(2)}, u32[]{:S(2)}) collective-permute-start(bf16[1024,256]{1,0:T(8,128)(2,1)} %get-tuple-element.34), channel_id=1, source_target_pairs={{0,16},{8,24},{16,0},{24,8},{1,17},{9,25},{17,1},{25,9},{2,18},{10... | collective-permute-start | bytes 1572872 | tf_op jit(solution)/shard_map/ppermute | solution.py:450
  242.4 15.2 %collective-permute-start.5 = (bf16[1024,256]{1,0:T(8,128)(2,1)S(1)}, bf16[1024,256]{1,0:T(8,128)(2,1)S(1)}, u32[]{:S(2)}, u32[]{:S(2)}) collective-permute-start(bf16[1024,256]{1,0:T(8,128)(2,1)S(1)} %copy-done.6), channel_id=1, source_target_pairs={{0,8},{8,16},{16,24},{24,0},{1,9},{9,17},{17,25},{25,1},{2,10},{10... | collective-permute-start | bytes 1572872 | tf_op jit(solution)/shard_map/ppermute | solution.py:450
  249.0 8.5 %all-to-all-start.13 = ((bf16[4,64,256]{2,1,0:T(8,128)(2,1)}), bf16[4,64,256]{2,1,0:T(8,128)(2,1)S(1)}, u32[]{:S(2)}, u32[]{:S(2)}) async-start(bf16[4,64,256]{2,1,0:T(8,128)(2,1)} %broadcast_in_dim.219), calls=%async_computation.13 | async-start | bytes 262144 | tf_op jit(solution)/shard_map/all_to_all | solution.py:55
Sparse Core Ops, SparseCore 0:
  28.7 107.2 all-gather.1
  184.7 110.2 reduce-scatter.1

commit v3 on v2

--- a/solution.py
+++ b/solution.py
@@ -19,12 +19,15 @@
 NEG = -1e30
 SCALE = FEATURE_LENGTH ** (-0.5)
 UNROLL = 4
+DEPTH = 8
+STAGES = 16
 SLOTS = 1 + RANDOM
 D = FEATURE_LENGTH
 S = SPAN_TOKENS
 G = WORLDWIDE_COUNT * SPAN_TOKENS
 VMEM = pl.BlockSpec(memory_space=pltpu.VMEM)
 SMEM = pl.BlockSpec(memory_space=pltpu.SMEM)
+ANY = pl.BlockSpec(memory_space=pl.ANY)
 PARAMS = pltpu.CompilerParams(vmem_limit_bytes=56 * 2**20)
 
 
@@ -128,41 +131,110 @@
     rows_ref[2:3, :] = slope
 
 
+def cell_fetcher(meta_ref, cell_ref, kv_ref, fetch_ref, fetch_sems):
+    def copies(t):
+        found = []
+        for u in range(UNROLL):
+            buffer = lax.rem(t, DEPTH) * UNROLL + u
+            cell = pl.multiple_of(cell_ref[t * UNROLL + u] * S, S)
+            found.append(
+                pltpu.make_async_copy(
+                    kv_ref.at[pl.ds(cell, S), :], fetch_ref.at[buffer], fetch_sems.at[buffer]
+                )
+            )
+        return found
+
+    def start(t):
+        @pl.when(t < meta_ref[0])
+        def _():
+            for copy in copies(t):
+                copy.start()
+
+    def wait(t):
+        for copy in copies(t):
+            copy.wait()
+
+    return start, wait
+
+
+def diagonal(qd):
+    zeros = jnp.zeros((S, D), jnp.bfloat16)
+    return jnp.concatenate(
+        [jnp.concatenate([qd[:, :D], zeros], 1), jnp.concatenate([zeros, qd[:, D:]], 1)], 0
+    )
+
+
+def lane_scale():
+    return jnp.where(lax.broadcasted_iota(jnp.int32, (1, 2 * S), 1) < S, SCALE, 1.0)
+
+
 def edge_stats_kernel(
-    meta_ref, slot_ref, item_ref, cell_ref, qd_ref, kv_ref, own_ref, out_ref, top_ref, total_ref, slope_ref
+    meta_ref,
+    slot_ref,
+    item_ref,
+    cell_ref,
+    qd_ref,
+    kv_ref,
+    own_ref,
+    out_ref,
+    table_ref,
+    top_ref,
+    total_ref,
+    slope_ref,
+    zero_ref,
+    fetch_ref,
+    fetch_sems,
+    zero_sems,
 ):
     group = qd_ref.shape[0] // S
     blocks = own_ref.shape[1]
+    start, wait = cell_fetcher(meta_ref, cell_ref, kv_ref, fetch_ref, fetch_sems)
+    for t in range(DEPTH):
+        start(t)
+    rows = zero_ref.shape[0]
+    zero_ref[...] = jnp.zeros(zero_ref.shape, jnp.bfloat16)
+    clears = [
+        pltpu.make_async_copy(zero_ref, table_ref.at[pl.ds(i * rows, rows), :], zero_sems.at[i])
+        for i in range(table_ref.shape[0] // rows)
+    ]
+    for clear in clears:
+        clear.start()
     top_ref[...] = jnp.full(top_ref.shape, NEG, jnp.float32)
     total_ref[...] = jnp.zeros(total_ref.shape, jnp.float32)
     slope_ref[...] = jnp.zeros(slope_ref.shape, jnp.float32)
+    factor = lane_scale()
 
     def step(t, carry):
+        wait(t)
         found = []
         for u in range(UNROLL):
             pos = t * UNROLL + u
-            cell = pl.multiple_of(cell_ref[pos] * S, S)
             item = pl.multiple_of(item_ref[pos] * S, S)
-            scores = dot_nt(kv_ref[pl.ds(cell, S), :D], qd_ref[pl.ds(item, S), :D]) * SCALE
-            slopes = dot_nt(kv_ref[pl.ds(cell, S), D:], qd_ref[pl.ds(item, S), D:])
-            found.append((slot_ref[pos], column_stats(scores, slopes)))
-        for slot, (top, total, slope) in found:
+            pairs = fetch_ref[lax.rem(t, DEPTH) * UNROLL + u]
+            both = dot_nt(pairs, diagonal(qd_ref[pl.ds(item, S), :])) * factor
+            top = jnp.max(both, axis=0, keepdims=True)
+            weights = jnp.exp(both - top)
+            total = jnp.sum(weights, axis=0, keepdims=True)
+            slope = jnp.sum(weights * pltpu.roll(both, S, 1), axis=0, keepdims=True)
+            found.append((slot_ref[pos], top, total, slope))
+        for slot, top, total, slope in found:
             top_ref[pl.ds(slot, 1), :] = top
             total_ref[pl.ds(slot, 1), :] = total
             slope_ref[pl.ds(slot, 1), :] = slope
+        start(t + DEPTH)
         return carry
 
     lax.fori_loop(0, meta_ref[0], step, 0)
     mine = pl.multiple_of(SLOTS * group + meta_ref[1] * blocks, 8)
-    top_ref[pl.ds(mine, blocks), :] = own_ref[0]
-    total_ref[pl.ds(mine, blocks), :] = own_ref[1]
-    slope_ref[pl.ds(mine, blocks), :] = own_ref[2]
+    top_ref[pl.ds(mine, blocks), :S] = own_ref[0]
+    total_ref[pl.ds(mine, blocks), :S] = own_ref[1]
+    slope_ref[pl.ds(mine, blocks), :S] = own_ref[2]
     top, total, slope = merge(
         [
             (
-                top_ref[s * group : (s + 1) * group, :],
-                total_ref[s * group : (s + 1) * group, :],
-                slope_ref[s * group : (s + 1) * group, :],
+                top_ref[s * group : (s + 1) * group, :S],
+                total_ref[s * group : (s + 1) * group, :S],
+                slope_ref[s * group : (s + 1) * group, :S],
             )
             for s in range(SLOTS + 1)
         ]
@@ -172,22 +244,40 @@
     for lane in range(out_ref.shape[0]):
         out_ref[lane, :group, :] = first
         out_ref[lane, group:, :] = second
+    for clear in clears:
+        clear.wait()
 
 
 def edge_grads_kernel(
-    meta_ref, slot_ref, item_ref, cell_ref, qd_ref, kv_ref, parts_ref, table_ref, final_ref, mixed_ref, *rest
+    meta_ref,
+    slot_ref,
+    item_ref,
+    cell_ref,
+    order_ref,
+    last_ref,
+    qd_ref,
+    kv_ref,
+    parts_ref,
+    cleared_ref,
+    table_ref,
+    final_ref,
+    mixed_ref,
+    *rest,
 ):
-    sent_refs = rest[:-1]
-    partial_ref = rest[-1]
+    sent_refs = rest[:-6]
+    partial_ref, sum_ref, stage_ref, fetch_ref, fetch_sems, stage_sems = rest[-6:]
     group = qd_ref.shape[0] // S
     tokens = mixed_ref.shape[0]
     lanes = parts_ref.shape[0]
+    start, wait = cell_fetcher(meta_ref, cell_ref, kv_ref, fetch_ref, fetch_sems)
+    for t in range(DEPTH):
+        start(t)
     top, total, slope = merge(
         [
             (
-                parts_ref[lane, :group, :S],
-                parts_ref[lane, :group, S:],
-                parts_ref[lane, group:, :S],
+                parts_ref[lane, :group, :],
+                pltpu.roll(parts_ref[lane, :group, :], S, 1),
+                parts_ref[lane, group:, :],
             )
             for lane in range(lanes)
         ]
@@ -196,47 +286,53 @@
     final_ref[0] = top
     final_ref[1] = inverse
     final_ref[2] = slope * inverse
-    table_ref[...] = jnp.zeros(table_ref.shape, jnp.bfloat16)
     partial_ref[...] = jnp.zeros(partial_ref.shape, jnp.float32)
+    sum_ref[...] = jnp.zeros(sum_ref.shape, jnp.float32)
+    factor = lane_scale()
+    low_half = lax.broadcasted_iota(jnp.int32, (S, 2 * S), 1) < S
+
+    def stage_copy(stage, cell):
+        at = pl.ds(pl.multiple_of(cell * S, S), S)
+        return pltpu.make_async_copy(stage_ref.at[stage], table_ref.at[at, :], stage_sems.at[stage])
 
     def step(t, carry):
+        wait(t)
         found = []
         for u in range(UNROLL):
             pos = t * UNROLL + u
             slot = slot_ref[pos]
             live = slot < SLOTS * group
-            item_pos = lax.rem(slot, group)
-            cell = pl.multiple_of(cell_ref[pos] * S, S)
+            row = pl.ds(lax.rem(slot, group), 1)
             item = pl.multiple_of(item_ref[pos] * S, S)
-            key = kv_ref[pl.ds(cell, S), :D]
-            value = kv_ref[pl.ds(cell, S), D:]
-            q = qd_ref[pl.ds(item, S), :D]
-            dout = qd_ref[pl.ds(item, S), D:]
-            scores = dot_nt(key, q) * SCALE
-            slopes = dot_nt(value, dout)
-            prob = jnp.exp(scores - final_ref[0, pl.ds(item_pos, 1), :])
-            prob = prob * final_ref[1, pl.ds(item_pos, 1), :]
-            prob = jnp.where(live, prob, 0.0)
-            dscore = prob * ((slopes - final_ref[2, pl.ds(item_pos, 1), :]) * SCALE)
-            prob = prob.astype(jnp.bfloat16)
-            dscore = dscore.astype(jnp.bfloat16)
-            found.append(
-                (
-                    cell,
-                    item,
-                    dot_nn(dscore, q),
-                    dot_nn(prob, dout),
-                    dot_tn(prob, value),
-                    dot_tn(dscore, key),
-                )
-            )
-        for cell, item, dkey, dvalue, mixed, dq in found:
-            at = pl.ds(cell, S)
-            table_ref[at, :D] = (table_ref[at, :D].astype(jnp.float32) + dkey).astype(jnp.bfloat16)
-            table_ref[at, D:] = (table_ref[at, D:].astype(jnp.float32) + dvalue).astype(jnp.bfloat16)
+            pairs = fetch_ref[lax.rem(t, DEPTH) * UNROLL + u]
+            corner = diagonal(qd_ref[pl.ds(item, S), :])
+            both = dot_nt(pairs, corner) * factor
+            prob = jnp.exp(both - final_ref[0, row, :]) * final_ref[1, row, :]
+            dscore = prob * ((pltpu.roll(both, S, 1) - final_ref[2, row, :]) * SCALE)
+            packed = jnp.where(low_half, dscore, pltpu.roll(prob, S, 1))
+            packed = jnp.where(live, packed, 0.0).astype(jnp.bfloat16)
+            found.append((pos, item, dot_nn(packed, corner), dot_tn(packed, pairs)))
+        running = sum_ref[...]
+        for pos, item, grads, crossed in found:
+            fresh = order_ref[pos] != order_ref[jnp.maximum(pos - 1, 0)]
+            running = grads + jnp.where(fresh, 0.0, running)
+
+            @pl.when(last_ref[pos] > 0)
+            def _():
+                stage = lax.rem(order_ref[pos], STAGES)
+
+                @pl.when(order_ref[pos] >= STAGES)
+                def _():
+                    stage_copy(stage, cell_ref[pos]).wait()
+
+                stage_ref[stage] = running.astype(jnp.bfloat16)
+                stage_copy(stage, cell_ref[pos]).start()
+
             at = pl.ds(item, S)
-            partial_ref[at, :D] += mixed
-            partial_ref[at, D:] += dq
+            partial_ref[at, :D] += crossed[S:, D:]
+            partial_ref[at, D:] += crossed[:S, :D]
+        sum_ref[...] = running
+        start(t + DEPTH)
         return carry
 
     lax.fori_loop(0, meta_ref[0], step, 0)
@@ -244,6 +340,11 @@
     for shift, sent_ref in enumerate(sent_refs):
         low = (shift + 1) * tokens
         sent_ref[...] = partial_ref[low : low + tokens, :].astype(jnp.bfloat16)
+    for stage in range(STAGES):
+
+        @pl.when(stage < meta_ref[2])
+        def _():
+            stage_copy(stage, 0).wait()
 
 
 def own_grads_kernel(
@@ -293,9 +394,9 @@
         low, high, q, dout, scores, slopes, global_scores, global_slopes = own_scores(
             i, blocks, qd_ref, kv_ref, shared_ref, bias_ref
         )
-        top = final_ref[0, pl.ds(first + i, 1), :]
-        inverse = final_ref[1, pl.ds(first + i, 1), :] * flag_ref[i]
-        slope = final_ref[2, pl.ds(first + i, 1), :]
+        top = final_ref[0, pl.ds(first + i, 1), :S]
+        inverse = final_ref[1, pl.ds(first + i, 1), :S] * flag_ref[i]
+        slope = final_ref[2, pl.ds(first + i, 1), :S]
 
         def both(scores, slopes):
             prob = jnp.exp(scores - top) * inverse
@@ -338,6 +439,9 @@
     )
     kv_all = lax.all_gather(kv, Z_AXIS, axis=0, tiled=True)
     qd = by_head(query, grad_out)
+    random_blocks, universal_segment_indices, qd = lax.optimization_barrier(
+        (random_blocks, universal_segment_indices, qd)
+    )
     tokens = qd.shape[0]
     block_count = tokens // S
     group = block_count * y_count
@@ -388,15 +492,23 @@
     cell = cell.T.reshape(-1)
     entries = SLOTS * group
     order = jnp.arange(entries, dtype=jnp.int32)
-    rank = jnp.cumsum(valid.astype(jnp.int32)) - 1
-    edge_count = rank[-1] + 1
+    label = cell * entries + order
+    rank = jnp.sum((valid[None, :] & (label[None, :] < label[:, None])).astype(jnp.int32), 1)
+    edge_count = jnp.sum(valid.astype(jnp.int32))
     hit = (rank[None, :] == order[:, None]) & valid[None, :]
     slot_list = jnp.sum(jnp.where(hit, order[None, :], 0), 1)
     cell_list = jnp.sum(jnp.where(hit, cell[None, :], 0), 1)
-    slot_list = jnp.where(order < edge_count, slot_list, entries + group)
+    real = order < edge_count
+    fresh = real & ((order == 0) | (cell_list != jnp.roll(cell_list, 1)))
+    last_list = real & ((order == edge_count - 1) | (cell_list != jnp.roll(cell_list, -1)))
+    order_list = jnp.sum((fresh[None, :] & (order[None, :] <= order[:, None])).astype(jnp.int32), 1) - 1
+    slot_list = jnp.where(real, slot_list, entries + group)
     item_list = slot_list % group
     item_list = (y_place - item_list // block_count) % y_count * block_count + item_list % block_count
-    meta = jnp.stack([(edge_count + UNROLL - 1) // UNROLL, y_place]).astype(jnp.int32)
+    last_list = last_list.astype(jnp.int32)
+    meta = jnp.stack(
+        [(edge_count + UNROLL - 1) // UNROLL, y_place, jnp.sum(fresh.astype(jnp.int32))]
+    ).astype(jnp.int32)
     lists = (meta, slot_list, item_list, cell_list)
 
     own_first = y_place * block_count
@@ -417,16 +529,24 @@
         compiler_params=PARAMS,
         name="own_stats",
     )(bias, qd, kv, shared)
-    rows_all = to_all(rows, Z_AXIS)
-    own, rows_all = lax.optimization_barrier((own, rows_all))
 
     stat_rows = (SLOTS + 1) * group + 8
-    stats = pl.pallas_call(
+    fetch_scratch = [
+        pltpu.VMEM((DEPTH * UNROLL, S, 2 * D), jnp.bfloat16),
+        pltpu.SemaphoreType.DMA((DEPTH * UNROLL,)),
+    ]
+    stats, cleared = pl.pallas_call(
         edge_stats_kernel,
-        out_shape=jax.ShapeDtypeStruct((y_count, 2 * group, 2 * S), f32),
-        in_specs=[SMEM] * 4 + [VMEM] * 3,
-        out_specs=VMEM,
-        scratch_shapes=[pltpu.VMEM((stat_rows, S), f32)] * 3,
+        out_shape=(
+            jax.ShapeDtypeStruct((y_count, 2 * group, 2 * S), f32),
+            jax.ShapeDtypeStruct((cells * S, 2 * D), jnp.bfloat16),
+        ),
+        in_specs=[SMEM] * 4 + [VMEM, ANY, VMEM],
+        out_specs=(VMEM, ANY),
+        scratch_shapes=[pltpu.VMEM((stat_rows, 2 * S), f32)] * 3
+        + [pltpu.VMEM((tokens, 2 * D), jnp.bfloat16)]
+        + fetch_scratch
+        + [pltpu.SemaphoreType.DMA((z_count,))],
         compiler_params=PARAMS,
         name="edge_stats",
     )(*lists, qd_group, kv_all, own)
@@ -436,19 +556,26 @@
         edge_grads_kernel,
         out_shape=(
             jax.ShapeDtypeStruct((cells * S, 2 * D), jnp.bfloat16),
-            jax.ShapeDtypeStruct((3, group, S), f32),
+            jax.ShapeDtypeStruct((3, group, 2 * S), f32),
             jax.ShapeDtypeStruct((tokens, 2 * D), f32),
         )
         + (jax.ShapeDtypeStruct((tokens, 2 * D), jnp.bfloat16),) * (y_count - 1),
-        in_specs=[SMEM] * 4 + [VMEM] * 3,
-        out_specs=(VMEM,) * (y_count + 2),
-        scratch_shapes=[pltpu.VMEM((group * S, 2 * D), f32)],
+        in_specs=[SMEM] * 6 + [VMEM, ANY, VMEM, ANY],
+        out_specs=(ANY,) + (VMEM,) * (y_count + 1),
+        scratch_shapes=[
+            pltpu.VMEM((group * S, 2 * D), f32),
+            pltpu.VMEM((S, 2 * D), f32),
+            pltpu.VMEM((STAGES, S, 2 * D), jnp.bfloat16),
+        ]
+        + fetch_scratch
+        + [pltpu.SemaphoreType.DMA((STAGES,))],
+        input_output_aliases={9: 0},
         compiler_params=PARAMS,
         name="edge_grads",
-    )(*lists, qd_group, kv_all, parts)
+    )(*lists, order_list, last_list, qd_group, kv_all, parts, cleared)
     returned = lax.psum_scatter(table, Z_AXIS, scatter_dimension=0, tiled=True)
     halves = [lax.ppermute(half, Y_AXIS, pairs) for half, pairs in zip(halves, backward)]
-    rows_all = to_all(rows_all, Y_AXIS).reshape(ctx_count, 3, G)
+    rows_all = to_all(to_all(rows, Z_AXIS), Y_AXIS).reshape(ctx_count, 3, G)
 
     pairs, mixed, shared_grads = pl.pallas_call(
         own_grads_kernel,

time: 307 us -> 315 us (1.026)
  blocking collectives: 53.4 us -> 40.9 us
  other arithmetic: 14.9 us -> 23 us
  local copies, waits for them, and re-layouts: 18.3 us -> 25.5 us
  Pallas kernels: 38.6 us -> 42.4 us
    reduce_scatter x1, waiting for transfers between devices: 34.7 us -> 19.1 us  [body(): returned = lax.psum_scatter(table, Z_AXIS, scatter_dimension=0, tiled=True)]
    all_to_all x10 -> x11, waiting for transfers between devices: 54.6 us -> 70 us  [exchange(): return lax.all_to_all(array, axes, split_axis=0, concat_axis=0, tiled=True)]
    all_to_all x4 -> x3, blocking collectives: 53.4 us -> 40.9 us  [exchange(): return lax.all_to_all(array, axes, split_axis=0, concat_axis=0, tiled=True)]
    unnamed x15 -> x40, local copies, waits for them, and re-layouts: 2.24 us -> 7.3 us
    reduce_sum x1 -> x5, other arithmetic: 0.73 us -> 5.37 us  [the longest x1 1.89 us: body(): jnp.sum(fresh.astype(jnp.int32))]
    all_to_all x10 -> x11, starting transfers between devices: 47.7 us -> 52.3 us  [exchange(): return lax.all_to_all(array, axes, split_axis=0, concat_axis=0, tiled=True)]
    pallas_call x1, Pallas kernels: 18.6 us -> 21.8 us  [body(): pl.pallas_call(edge_grads_kernel, out_shape=(jax.ShapeDtypeStruct((cells...]
  transfers between devices with their start and end apart: 18 -> 19, of which waited for: 10 -> 11; matrix products, arithmetic and copies ran while one was open for 9% -> 13% of each run, Pallas kernels for 4% -> 4%
where the time goes in v3:
time: 315 us; the launch traced here: 313 us
  waiting for transfers between devices  89.2 us (28%)
  starting transfers between devices  68.9 us (22%)
  Pallas kernels  42.4 us (13%)
  blocking collectives  40.9 us (13%)
  local copies, waits for them, and re-layouts  25.5 us (8%)
  between operations  23.2 us (7%)
  other arithmetic  23 us (7%)
    all_to_all x11, waiting for transfers between devices, exchange(): return lax.all_to_all(array, axes, split_axis=0, concat_axis=0, tiled=True)  70 us
    all_to_all x11, starting transfers between devices, exchange(): return lax.all_to_all(array, axes, split_axis=0, concat_axis=0, tiled=True)  52.3 us
    all_to_all x3, blocking collectives, exchange(): return lax.all_to_all(array, axes, split_axis=0, concat_axis=0, tiled=True)  40.9 us
    pallas_call x1, Pallas kernels, body(): pl.pallas_call(edge_grads_kernel, out_shape=(jax.ShapeDtypeStruct((cells...  21.8 us
    reduce_scatter x1, waiting for transfers between devices, body(): returned = lax.psum_scatter(table, Z_AXIS, scatter_dimension=0, tiled=True)  19.1 us
    pallas_call x1, Pallas kernels, body(): pl.pallas_call(own_grads_kernel, out_shape=(jax.ShapeDtypeStruct((tokens,...  9.35 us
    ppermute x3, starting transfers between devices, body(): lax.ppermute(qd, Y_AXIS, pairs)  8.42 us
    ppermute x3, starting transfers between devices, body(): lax.ppermute(half, Y_AXIS, pairs)  8.18 us
  transfers between devices with their start and end apart: 19, of which 11 were waited for; matrix products, arithmetic and copies ran while one was open for 13% of the time, Pallas kernels for 4%

profile of v3, /device:TPU:1, one launch (start us, length us, event | category | flops | bytes accessed | tf_op | source)
XLA Modules:
  0.0 313.0 jit_solution(17159857091772859378)
XLA Ops:
  9.4 19.2 %all_to_all.70 = bf16[8,128,256]{2,1,0:T(8,128)(2,1)} all-to-all(bf16[8,128,256]{2,1,0:T(8,128)(2,1)S(1)} %maximum_bitcast_fusion), channel_id=1, replica_groups=mesh['ctx_0'=16,'ctx_1'=4,'head'=8] {'head'}, dimensions={0} | all-to-all | bytes 1048576 | tf_op jit(solution)/shard_map/all_to_all | solution.py:58
  29.6 4.4 %all-to-all-start.1 = ((bf16[8,128,256]{2,1,0:T(8,128)(2,1)}), bf16[8,128,256]{2,1,0:T(8,128)(2,1)S(1)}, u32[]{:S(2)}, u32[]{:S(2)}) async-start(bf16[8,128,256]{2,1,0:T(8,128)(2,1)} %maximum_bitcast_fusion.1), calls=%async_computation.1 | async-start | bytes 1048576 | tf_op jit(solution)/shard_map/all_to_all | solution.py:58
  35.7 7.7 %all-to-all-done.1 = bf16[8,128,256]{2,1,0:T(8,128)(2,1)S(1)} async-done(((bf16[8,128,256]{2,1,0:T(8,128)(2,1)}), bf16[8,128,256]{2,1,0:T(8,128)(2,1)S(1)}, u32[]{:S(2)}, u32[]{:S(2)}) %all-to-all-start.1) | async-done | bytes 524320 | tf_op jit(solution)/shard_map/all_to_all | solution.py:58
  49.9 1.9 collective-permute-start
  51.9 1.9 collective-permute-start.1
  53.8 4.6 %collective-permute-start.2 = (bf16[1024,256]{1,0:T(8,128)(2,1)S(1)}, bf16[1024,256]{1,0:T(8,128)(2,1)S(1)}, u32[]{:S(2)}, u32[]{:S(2)}) collective-permute-start(bf16[1024,256]{1,0:T(8,128)(2,1)S(1)} %bitcast.91), channel_id=1, source_target_pairs={{0,24},{8,0},{16,8},{24,16},{1,25},{9,1},{17,9},{25,17},{2,26},{10... | collective-permute-start | bytes 1572872 | tf_op jit(solution)/shard_map/ppermute | solution.py:472
  59.0 3.6 %all-to-all-start.2 = ((s32[4,16,3]{1,2,0:T(4,128)}), s32[4,16,3]{1,2,0:T(4,128)S(1)}, u32[]{:S(2)}, u32[]{:S(2)}) async-start(s32[4,16,3]{1,2,0:T(4,128)} %broadcast_in_dim.202), calls=%async_computation.2 | async-start | bytes 16384 | tf_op jit(solution)/shard_map/all_to_all | solution.py:58
  67.9 11.8 %all-to-all-done.2 = s32[4,16,3]{1,2,0:T(4,128)S(1)} async-done(((s32[4,16,3]{1,2,0:T(4,128)}), s32[4,16,3]{1,2,0:T(4,128)S(1)}, u32[]{:S(2)}, u32[]{:S(2)}) %all-to-all-start.2) | async-done | bytes 800 | tf_op jit(solution)/shard_map/all_to_all | solution.py:58
  79.7 4.8 %all-to-all-start.3 = ((bf16[4,32,512]{2,1,0:T(8,128)(2,1)}), bf16[4,32,512]{2,1,0:T(8,128)(2,1)S(1)}, u32[]{:S(2)}, u32[]{:S(2)}) async-start(bf16[4,32,512]{2,1,0:T(8,128)(2,1)} %bitcast.15), calls=%async_computation.3 | async-start | bytes 262144 | tf_op jit(solution)/shard_map/all_to_all | solution.py:58
  86.0 1.1 not_and_fusion.1
  87.1 1.2 not_and_fusion
  88.9 1.8 convert_reduce_fusion.2
  90.7 1.2 and.315
  95.1 1.1 fusion.17
  97.4 1.4 reshape.256
  98.8 10.8 %all-to-all-start.4 = ((bf16[16,2,512]{2,1,0:T(2,128)(2,1)}), bf16[16,2,512]{2,1,0:T(2,128)(2,1)S(1)}, u32[]{:S(2)}, u32[]{:S(2)}) async-start(bf16[16,2,512]{2,1,0:T(2,128)(2,1)} %reshape.256), calls=%async_computation.4 | async-start | bytes 65536 | tf_op jit(solution)/shard_map/all_to_all | solution.py:58
  109.6 1.9 convert_reduce_fusion.3
  113.4 8.0 %all-to-all-done.4 = bf16[16,2,512]{2,1,0:T(2,128)(2,1)S(1)} async-done(((bf16[16,2,512]{2,1,0:T(2,128)(2,1)}), bf16[16,2,512]{2,1,0:T(2,128)(2,1)S(1)}, u32[]{:S(2)}, u32[]{:S(2)}) %all-to-all-start.4) | async-done | bytes 32800 | tf_op jit(solution)/shard_map/all_to_all | solution.py:58
  122.1 3.5 %all-to-all-start.5 = ((bf16[16,2,512]{2,1,0:T(2,128)(2,1)}), bf16[16,2,512]{2,1,0:T(2,128)(2,1)S(1)}, u32[]{:S(2)}, u32[]{:S(2)}) async-start(bf16[16,2,512]{2,1,0:T(2,128)(2,1)} %broadcast_in_dim.214), calls=%async_computation.5 | async-start | bytes 65536 | tf_op jit(solution)/shard_map/all_to_all | solution.py:58
  126.2 11.1 %all-to-all-done.5 = bf16[16,2,512]{2,1,0:T(2,128)(2,1)S(1)} async-done(((bf16[16,2,512]{2,1,0:T(2,128)(2,1)}), bf16[16,2,512]{2,1,0:T(2,128)(2,1)S(1)}, u32[]{:S(2)}, u32[]{:S(2)}) %all-to-all-start.5) | async-done | bytes 32800 | tf_op jit(solution)/shard_map/all_to_all | solution.py:58
  137.9 4.3 %all-to-all-start.6 = ((bf16[4,32,512]{2,1,0:T(8,128)(2,1)}), bf16[4,32,512]{2,1,0:T(8,128)(2,1)S(1)}, u32[]{:S(2)}, u32[]{:S(2)}) async-start(bf16[4,32,512]{2,1,0:T(8,128)(2,1)} %broadcast_in_dim.216), calls=%async_computation.6 | async-start | bytes 262144 | tf_op jit(solution)/shard_map/all_to_all | solution.py:58
  142.3 1.2 pad_add_fusion.1.meta_ref
  143.5 3.6 %all-to-all-done.6 = bf16[4,32,512]{2,1,0:T(8,128)(2,1)S(1)} async-done(((bf16[4,32,512]{2,1,0:T(8,128)(2,1)}), bf16[4,32,512]{2,1,0:T(8,128)(2,1)S(1)}, u32[]{:S(2)}, u32[]{:S(2)}) %all-to-all-start.6) | async-done | bytes 131104 | tf_op jit(solution)/shard_map/all_to_all | solution.py:58
  147.7 3.5 %own_stats.1 = (f32[3,16,64]{2,1,0:T(8,128)}, f32[3,128]{1,0:T(4,128)}) custom-call(f32[32]{0:T(128)} %reshape.254.bias_ref, bf16[1024,256]{1,0:T(8,128)(2,1)} %bitcast.94, bf16[1024,256]{1,0:T(8,128)(2,1)} %bitcast.87, bf16[128,512]{1,0:T(8,128)(2,1)} %bitcast.96), custom_call_target="tpu_custom_call" | custom-call | tf_op jit(solution)/shard_map/own_stats/pallas_call | solution.py:521
  152.3 1.1 constant_dynamic-update-slice_fusion.1
  153.5 1.3 copy-done.1
  154.8 7.7 %edge_stats.1 = (f32[4,128,128]{2,1,0:T(8,128)}, bf16[16384,256]{1,0:T(8,128)(2,1)}) custom-call(s32[3]{0:T(128)} %pad_add_fusion.1.meta_ref, s32[256]{0:T(256)} %get-tuple-element.49.slot_ref, s32[256]{0:T(256)} %get-tuple-element.48.item_ref, s32[256]{0:T(256)} %copy-done.10, bf16[4096,256]{1,0:T(8,128)(2,1)} %copy-done.1, ...), custom_call_target="tpu_custom_call" | custom-call | tf_op jit(solution)/shard_map/edge_stats/pallas_call | solution.py:538
  162.5 4.7 %all-to-all-start.7 = ((f32[4,128,128]{2,1,0:T(8,128)}), f32[4,128,128]{2,1,0:T(8,128)S(1)}, u32[]{:S(2)}, u32[]{:S(2)}) async-start(f32[4,128,128]{2,1,0:T(8,128)} %get-tuple-element.32), calls=%async_computation.7 | async-start | bytes 524288 | tf_op jit(solution)/shard_map/all_to_all | solution.py:58
  167.2 1.8 and_convert_fusion.last_ref
  169.0 3.7 %all-to-all-done.7.parts_ref = f32[4,128,128]{2,1,0:T(8,128)S(1)} async-done(((f32[4,128,128]{2,1,0:T(8,128)}), f32[4,128,128]{2,1,0:T(8,128)S(1)}, u32[]{:S(2)}, u32[]{:S(2)}) %all-to-all-start.7) | async-done | bytes 262176 | tf_op jit(solution)/shard_map/all_to_all | solution.py:58
  173.4 21.8 %edge_grads.1 = (bf16[16384,256]{1,0:T(8,128)(2,1)}, f32[3,64,128]{2,1,0:T(8,128)}, f32[1024,256]{1,0:T(8,128)}, bf16[1024,256]{1,0:T(8,128)(2,1)}, bf16[1024,25...) custom-call(s32[3]{0:T(128)} %pad_add_fusion.1.meta_ref, ...), custom_call_target="tpu_custom_call", output_to_operand_aliasing={{0}: (9, {})} | custom-call | tf_op jit(solution)/shard_map/edge_grads/pallas_call | solution.py:555
  196.6 4.9 %all-to-all-start.8 = ((f32[16,3,128]{2,1,0:T(4,128)}), f32[16,3,128]{2,1,0:T(4,128)S(1)}, u32[]{:S(2)}, u32[]{:S(2)}) async-start(f32[16,3,128]{2,1,0:T(4,128)} %broadcast_in_dim.220), calls=%async_computation.8 | async-start | bytes 65536 | tf_op jit(solution)/shard_map/all_to_all | solution.py:58
  201.6 11.4 %all-to-all-done.8 = f32[16,3,128]{2,1,0:T(4,128)S(1)} async-done(((f32[16,3,128]{2,1,0:T(4,128)}), f32[16,3,128]{2,1,0:T(4,128)S(1)}, u32[]{:S(2)}, u32[]{:S(2)}) %all-to-all-start.8) | async-done | bytes 24608 | tf_op jit(solution)/shard_map/all_to_all | solution.py:58
  213.6 4.5 %all-to-all-start.9 = ((f32[4,16,3,128]{3,1,2,0:T(8,128)}), f32[4,16,3,128]{3,1,2,0:T(8,128)S(1)}, u32[]{:S(2)}, u32[]{:S(2)}) async-start(f32[4,16,3,128]{3,1,2,0:T(8,128)} %broadcast_in_dim.221), calls=%async_computation.9 | async-start | bytes 196608 | tf_op jit(solution)/shard_map/all_to_all | solution.py:58
  218.7 4.1 %all-to-all-done.9 = f32[4,16,3,128]{3,1,2,0:T(8,128)S(1)} async-done(((f32[4,16,3,128]{3,1,2,0:T(8,128)}), f32[4,16,3,128]{3,1,2,0:T(8,128)S(1)}, u32[]{:S(2)}, u32[]{:S(2)}) %all-to-all-start.9) | async-done | bytes 98336 | tf_op jit(solution)/shard_map/all_to_all | solution.py:58
  223.4 9.3 %own_grads.1 = (f32[1024,256]{1,0:T(8,128)}, f32[1024,256]{1,0:T(8,128)}, f32[256,256]{1,0:T(8,128)}) custom-call(s32[3]{0:T(128)} %pad_add_fusion.1.meta_ref, f32[32]{0:T(128)} %reshape.254.bias_ref, f32[16]{0:T(128)} %broadcast_select_fusion.flag_ref, bf16[1024,256]{1,0:T(8,128)(2,1)} %bitcast.95, bf16[1024,256]{1,0:T(8,128)(2,1)} %bitcast.88, ...), custom_call_target="tpu_custom_call" | custom-call | tf_op jit(solution)/shard_map/own_grads/pallas_call | solution.py:580
  233.9 7.2 %all_to_all.71 = bf16[4,64,256]{2,1,0:T(8,128)(2,1)S(1)} all-to-all(bf16[4,64,256]{2,1,0:T(8,128)(2,1)S(1)} %bitcast.100), channel_id=1, replica_groups=mesh['ctx_0'=16,'ctx_1'=4,'head'=8] {'ctx_1'}, dimensions={0} | all-to-all | bytes 262144 | tf_op jit(solution)/shard_map/all_to_all | solution.py:58
  241.1 14.4 %all_to_all.72 = bf16[16,4,256]{2,1,0:T(4,128)(2,1)S(1)} all-to-all(bf16[16,4,256]{2,1,0:T(4,128)(2,1)S(1)} %reshape.260), channel_id=1, replica_groups=mesh['ctx_0'=16,'ctx_1'=4,'head'=8] {'ctx_0'}, dimensions={0} | all-to-all | bytes 65536 | tf_op jit(solution)/shard_map/all_to_all | solution.py:58
  256.2 3.5 %all-to-all-start.12 = ((bf16[16,4,256]{2,1,0:T(4,128)(2,1)}), bf16[16,4,256]{2,1,0:T(4,128)(2,1)S(1)}, u32[]{:S(2)}, u32[]{:S(2)}) async-start(bf16[16,4,256]{2,1,0:T(4,128)(2,1)} %broadcast_in_dim.222), calls=%async_computation.12 | async-start | bytes 65536 | tf_op jit(solution)/shard_map/all_to_all | solution.py:58
  259.7 2.8 collective-permute-start.3
  262.5 3.4 %collective-permute-start.4 = (bf16[1024,256]{1,0:T(8,128)(2,1)}, bf16[1024,256]{1,0:T(8,128)(2,1)S(1)}, u32[]{:S(2)}, u32[]{:S(2)}) collective-permute-start(bf16[1024,256]{1,0:T(8,128)(2,1)} %get-tuple-element.40), channel_id=1, source_target_pairs={{0,16},{8,24},{16,0},{24,8},{1,17},{9,25},{17,1},{25,9},{2,18},{10... | collective-permute-start | bytes 1572872 | tf_op jit(solution)/shard_map/ppermute | solution.py:577
  266.0 1.9 collective-permute-start.5
  267.9 3.6 %all-to-all-done.12 = bf16[16,4,256]{2,1,0:T(4,128)(2,1)S(1)} async-done(((bf16[16,4,256]{2,1,0:T(4,128)(2,1)}), bf16[16,4,256]{2,1,0:T(4,128)(2,1)S(1)}, u32[]{:S(2)}, u32[]{:S(2)}) %all-to-all-start.12) | async-done | bytes 32800 | tf_op jit(solution)/shard_map/all_to_all | solution.py:58
  272.2 3.3 %all-to-all-start.13 = ((bf16[4,64,256]{2,1,0:T(8,128)(2,1)}), bf16[4,64,256]{2,1,0:T(8,128)(2,1)S(1)}, u32[]{:S(2)}, u32[]{:S(2)}) async-start(bf16[4,64,256]{2,1,0:T(8,128)(2,1)} %broadcast_in_dim.224), calls=%async_computation.13 | async-start | bytes 262144 | tf_op jit(solution)/shard_map/all_to_all | solution.py:58
  275.9 4.9 %all-to-all-done.13 = bf16[4,64,256]{2,1,0:T(8,128)(2,1)S(1)} async-done(((bf16[4,64,256]{2,1,0:T(8,128)(2,1)}), bf16[4,64,256]{2,1,0:T(8,128)(2,1)S(1)}, u32[]{:S(2)}, u32[]{:S(2)}) %all-to-all-start.13) | async-done | bytes 131104 | tf_op jit(solution)/shard_map/all_to_all | solution.py:58
  281.8 1.9 fusion.4
  284.5 19.1 %reduce-scatter.2.cloned.1.call-done = bf16[1024,256]{1,0:T(8,128)(2,1)} async-done(((bf16[16384,256]{1,0:T(8,128)(2,1)}), bf16[1024,256]{1,0:T(8,128)(2,1)}) %reduce-scatter.2.cloned.1.call-update) | async-done | bytes 524304 | tf_op jit(solution)/shard_map/reduce_scatter | solution.py:576
  303.6 1.7 fusion.1
  (119 shorter events, 29.8 us)
Async XLA Ops:
  7.2 1.0 copy-start
  7.2 21.5 %copy-start.9 = (bf16[128,1024]{1,0:T(8,128)(2,1)S(1)}, bf16[128,1024]{1,0:T(8,128)(2,1)}, u32[]{:S(2)}) copy-start(bf16[128,1024]{1,0:T(8,128)(2,1)} %param.6) | copy-start | bytes 786436
  7.2 21.4 %copy-start.8 = (bf16[128,1024]{1,0:T(8,128)(2,1)S(1)}, bf16[128,1024]{1,0:T(8,128)(2,1)}, u32[]{:S(2)}) copy-start(bf16[128,1024]{1,0:T(8,128)(2,1)} %param.9) | copy-start | bytes 786436
  7.2 146.3 %all-gather.2.cloned.1.call-start = ((), (), s32[]{:S(2)}) async-start(), calls=%async_computation.15 | async-start | bytes 8912896 | tf_op jit(solution)/shard_map/all_gather | solution.py:440
  28.6 14.9 %copy-start.13 = (s32[2]{0:T(128)S(1)}, s32[2]{0:T(128)}, u32[]{:S(2)}) copy-start(s32[2]{0:T(128)} %param.11) | copy-start | bytes 28
  28.6 29.8 %copy-start.17 = (s32[16,1,3]{0,1,2:T(1,128)S(1)}, s32[16,1,3]{0,1,2:T(1,128)}, u32[]{:S(2)}) copy-start(s32[16,1,3]{0,1,2:T(1,128)} %param.10) | copy-start | bytes 580
  29.6 13.8 %all-to-all-start.1 = ((bf16[8,128,256]{2,1,0:T(8,128)(2,1)}), bf16[8,128,256]{2,1,0:T(8,128)(2,1)S(1)}, u32[]{:S(2)}, u32[]{:S(2)}) async-start(bf16[8,128,256]{2,1,0:T(8,128)(2,1)} %maximum_bitcast_fusion.1), calls=%async_computation.1 | async-start | bytes 1048576 | tf_op jit(solution)/shard_map/all_to_all | solution.py:58
  43.5 103.6 %copy-start.2 = (bf16[8,128,256]{2,1,0:T(8,128)(2,1)}, bf16[8,128,256]{2,1,0:T(8,128)(2,1)S(1)}, u32[]{:S(2)}) copy-start(bf16[8,128,256]{2,1,0:T(8,128)(2,1)S(1)} %all-to-all-done.1) | copy-start | bytes 1572868
  49.9 101.3 %collective-permute-start = (bf16[1024,256]{1,0:T(8,128)(2,1)S(1)}, bf16[1024,256]{1,0:T(8,128)(2,1)}, u32[]{:S(2)}, u32[]{:S(2)}) collective-permute-start(bf16[1024,256]{1,0:T(8,128)(2,1)S(1)} %bitcast.89), channel_id=1, source_target_pairs={{0,8},{8,16},{16,24},{24,0},{1,9},{9,17},{17,25},{25,1},{2,10},{10... | collective-permute-start | bytes 1572872 | tf_op jit(solution)/shard_map/ppermute | solution.py:472
  51.9 100.4 %collective-permute-start.1 = (bf16[1024,256]{1,0:T(8,128)(2,1)S(1)}, bf16[1024,256]{1,0:T(8,128)(2,1)}, u32[]{:S(2)}, u32[]{:S(2)}) collective-permute-start(bf16[1024,256]{1,0:T(8,128)(2,1)S(1)} %bitcast.90), channel_id=1, source_target_pairs={{0,16},{8,24},{16,0},{24,8},{1,17},{9,25},{17,1},{25,9},{2,18},{10... | collective-permute-start | bytes 1572872 | tf_op jit(solution)/shard_map/ppermute | solution.py:472
  53.8 99.6 %collective-permute-start.2 = (bf16[1024,256]{1,0:T(8,128)(2,1)S(1)}, bf16[1024,256]{1,0:T(8,128)(2,1)S(1)}, u32[]{:S(2)}, u32[]{:S(2)}) collective-permute-start(bf16[1024,256]{1,0:T(8,128)(2,1)S(1)} %bitcast.91), channel_id=1, source_target_pairs={{0,24},{8,0},{16,8},{24,16},{1,25},{9,1},{17,9},{25,17},{2,26},{10... | collective-permute-start | bytes 1572872 | tf_op jit(solution)/shard_map/ppermute | solution.py:472
  59.0 20.7 %all-to-all-start.2 = ((s32[4,16,3]{1,2,0:T(4,128)}), s32[4,16,3]{1,2,0:T(4,128)S(1)}, u32[]{:S(2)}, u32[]{:S(2)}) async-start(s32[4,16,3]{1,2,0:T(4,128)} %broadcast_in_dim.202), calls=%async_computation.2 | async-start | bytes 16384 | tf_op jit(solution)/shard_map/all_to_all | solution.py:58
  79.7 17.1 %all-to-all-start.3 = ((bf16[4,32,512]{2,1,0:T(8,128)(2,1)}), bf16[4,32,512]{2,1,0:T(8,128)(2,1)S(1)}, u32[]{:S(2)}, u32[]{:S(2)}) async-start(bf16[4,32,512]{2,1,0:T(8,128)(2,1)} %bitcast.15), calls=%async_computation.3 | async-start | bytes 262144 | tf_op jit(solution)/shard_map/all_to_all | solution.py:58
  88.3 2.4 copy-start.15
  88.9 3.0 copy-start.12
  95.0 58.5 %copy-start.10 = (s32[256]{0:T(256)}, s32[256]{0:T(256)S(1)}, u32[]{:S(2)}) copy-start(s32[256]{0:T(256)S(1)} %get-tuple-element.45.cell_ref) | copy-start | bytes 3076
  98.8 22.6 %all-to-all-start.4 = ((bf16[16,2,512]{2,1,0:T(2,128)(2,1)}), bf16[16,2,512]{2,1,0:T(2,128)(2,1)S(1)}, u32[]{:S(2)}, u32[]{:S(2)}) async-start(bf16[16,2,512]{2,1,0:T(2,128)(2,1)} %reshape.256), calls=%async_computation.4 | async-start | bytes 65536 | tf_op jit(solution)/shard_map/all_to_all | solution.py:58
  122.1 15.2 %all-to-all-start.5 = ((bf16[16,2,512]{2,1,0:T(2,128)(2,1)}), bf16[16,2,512]{2,1,0:T(2,128)(2,1)S(1)}, u32[]{:S(2)}, u32[]{:S(2)}) async-start(bf16[16,2,512]{2,1,0:T(2,128)(2,1)} %broadcast_in_dim.214), calls=%async_computation.5 | async-start | bytes 65536 | tf_op jit(solution)/shard_map/all_to_all | solution.py:58
  137.9 9.1 %all-to-all-start.6 = ((bf16[4,32,512]{2,1,0:T(8,128)(2,1)}), bf16[4,32,512]{2,1,0:T(8,128)(2,1)S(1)}, u32[]{:S(2)}, u32[]{:S(2)}) async-start(bf16[4,32,512]{2,1,0:T(8,128)(2,1)} %broadcast_in_dim.216), calls=%async_computation.6 | async-start | bytes 262144 | tf_op jit(solution)/shard_map/all_to_all | solution.py:58
  147.1 0.7 copy-start.3
  153.4 1.3 copy-start.1
  154.8 12.4 %copy-start.11 = (s32[256]{0:T(256)S(1)}, s32[256]{0:T(256)}, u32[]{:S(2)}) copy-start(s32[256]{0:T(256)} %copy-done.10) | copy-start | bytes 3076
  162.5 10.2 %all-to-all-start.7 = ((f32[4,128,128]{2,1,0:T(8,128)}), f32[4,128,128]{2,1,0:T(8,128)S(1)}, u32[]{:S(2)}, u32[]{:S(2)}) async-start(f32[4,128,128]{2,1,0:T(8,128)} %get-tuple-element.32), calls=%async_computation.7 | async-start | bytes 524288 | tf_op jit(solution)/shard_map/all_to_all | solution.py:58
  167.2 136.4 %reduce-scatter.2.cloned.1.call-start = ((), (), s32[]{:S(2)}) async-start(), calls=%async_computation.16 | async-start | bytes 8912896 | tf_op jit(solution)/shard_map/reduce_scatter | solution.py:576
  172.7 0.7 copy-start.4
  195.3 0.7 copy-start.16
  195.3 6.2 %copy-start.14 = (s32[2]{0:T(128)S(1)}, s32[2]{0:T(128)}, u32[]{:S(2)}) copy-start(s32[2]{0:T(128)} %param.11) | copy-start | bytes 28
  196.6 16.4 %all-to-all-start.8 = ((f32[16,3,128]{2,1,0:T(4,128)}), f32[16,3,128]{2,1,0:T(4,128)S(1)}, u32[]{:S(2)}, u32[]{:S(2)}) async-start(f32[16,3,128]{2,1,0:T(4,128)} %broadcast_in_dim.220), calls=%async_computation.8 | async-start | bytes 65536 | tf_op jit(solution)/shard_map/all_to_all | solution.py:58
  213.6 9.1 %all-to-all-start.9 = ((f32[4,16,3,128]{3,1,2,0:T(8,128)}), f32[4,16,3,128]{3,1,2,0:T(8,128)S(1)}, u32[]{:S(2)}, u32[]{:S(2)}) async-start(f32[4,16,3,128]{3,1,2,0:T(8,128)} %broadcast_in_dim.221), calls=%async_computation.9 | async-start | bytes 196608 | tf_op jit(solution)/shard_map/all_to_all | solution.py:58
  232.8 49.0 %copy-start.6 = (f32[1024,256]{1,0:T(8,128)S(1)}, f32[1024,256]{1,0:T(8,128)}, u32[]{:S(2)}) copy-start(f32[1024,256]{1,0:T(8,128)} %get-tuple-element.38) | copy-start | bytes 3145732
  256.2 15.3 %all-to-all-start.12 = ((bf16[16,4,256]{2,1,0:T(4,128)(2,1)}), bf16[16,4,256]{2,1,0:T(4,128)(2,1)S(1)}, u32[]{:S(2)}, u32[]{:S(2)}) async-start(bf16[16,4,256]{2,1,0:T(4,128)(2,1)} %broadcast_in_dim.222), calls=%async_computation.12 | async-start | bytes 65536 | tf_op jit(solution)/shard_map/all_to_all | solution.py:58
  259.7 21.2 %collective-permute-start.3 = (bf16[1024,256]{1,0:T(8,128)(2,1)}, bf16[1024,256]{1,0:T(8,128)(2,1)S(1)}, u32[]{:S(2)}, u32[]{:S(2)}) collective-permute-start(bf16[1024,256]{1,0:T(8,128)(2,1)} %get-tuple-element.39), channel_id=1, source_target_pairs={{0,24},{8,0},{16,8},{24,16},{1,25},{9,1},{17,9},{25,17},{2,26},{10... | collective-permute-start | bytes 1572872 | tf_op jit(solution)/shard_map/ppermute | solution.py:577
  262.5 18.4 %collective-permute-start.4 = (bf16[1024,256]{1,0:T(8,128)(2,1)}, bf16[1024,256]{1,0:T(8,128)(2,1)S(1)}, u32[]{:S(2)}, u32[]{:S(2)}) collective-permute-start(bf16[1024,256]{1,0:T(8,128)(2,1)} %get-tuple-element.40), channel_id=1, source_target_pairs={{0,16},{8,24},{16,0},{24,8},{1,17},{9,25},{17,1},{25,9},{2,18},{10... | collective-permute-start | bytes 1572872 | tf_op jit(solution)/shard_map/ppermute | solution.py:577
  266.0 14.9 %collective-permute-start.5 = (bf16[1024,256]{1,0:T(8,128)(2,1)}, bf16[1024,256]{1,0:T(8,128)(2,1)S(1)}, u32[]{:S(2)}, u32[]{:S(2)}) collective-permute-start(bf16[1024,256]{1,0:T(8,128)(2,1)} %get-tuple-element.41), channel_id=1, source_target_pairs={{0,8},{8,16},{16,24},{24,0},{1,9},{9,17},{17,25},{25,1},{2,10},{10... | collective-permute-start | bytes 1572872 | tf_op jit(solution)/shard_map/ppermute | solution.py:577
  272.2 8.6 %all-to-all-start.13 = ((bf16[4,64,256]{2,1,0:T(8,128)(2,1)}), bf16[4,64,256]{2,1,0:T(8,128)(2,1)S(1)}, u32[]{:S(2)}, u32[]{:S(2)}) async-start(bf16[4,64,256]{2,1,0:T(8,128)(2,1)} %broadcast_in_dim.224), calls=%async_computation.13 | async-start | bytes 262144 | tf_op jit(solution)/shard_map/all_to_all | solution.py:58
  280.9 0.8 copy-start.7
  281.8 21.8 %copy-start.5 = (f32[1024,256]{1,0:T(8,128)S(1)}, f32[1024,256]{1,0:T(8,128)}, u32[]{:S(2)}) copy-start(f32[1024,256]{1,0:T(8,128)} %get-tuple-element.43) | copy-start | bytes 3145732
Sparse Core Ops, SparseCore 0:
  28.7 106.7 all-gather.1
  195.4 108.1 reduce-scatter.1

commit v4 on v3

--- a/solution.py
+++ b/solution.py
@@ -18,9 +18,10 @@
 CTX_HEAD = (Z_AXIS, Y_AXIS, "head")
 NEG = -1e30
 SCALE = FEATURE_LENGTH ** (-0.5)
-UNROLL = 4
-DEPTH = 8
-STAGES = 16
+UNROLL = 8
+DEPTH = 4
+STAGES = 32
+CODE = 32
 SLOTS = 1 + RANDOM
 D = FEATURE_LENGTH
 S = SPAN_TOKENS
@@ -105,6 +106,33 @@
     )
     global_slopes = dot_nt(shared_ref[:, 3 * D :], dout)
     return low, high, q, dout, scores, slopes, global_scores, global_slopes
+
+
+def pick_kernel(index_ref, qd_ref, kv_ref, code_ref, out_ref, rows_ref, sems):
+    blocks = qd_ref.shape[0] // S
+    lanes = out_ref.shape[0]
+    part = S // lanes
+    copies = []
+    for g in range(WORLDWIDE_COUNT):
+        first = pl.multiple_of(lax.rem(index_ref[g], blocks) * S, S)
+        for pos, ref in enumerate((qd_ref, kv_ref)):
+            copies.append(
+                pltpu.make_async_copy(
+                    ref.at[pl.ds(first, S), :],
+                    rows_ref.at[pl.ds(g * S, S), pl.ds(pos * 2 * D, 2 * D)],
+                    sems.at[2 * g + pos],
+                )
+            )
+    for copy in copies:
+        copy.start()
+    for lane in range(lanes):
+        out_ref[lane, WORLDWIDE_COUNT * part :, :] = code_ref[...]
+    for copy in copies:
+        copy.wait()
+    for lane in range(lanes):
+        for g in range(WORLDWIDE_COUNT):
+            low = g * S + lane * part
+            out_ref[lane, g * part : (g + 1) * part, :] = rows_ref[low : low + part, :]
 
 
 def own_stats_kernel(bias_ref, qd_ref, kv_ref, shared_ref, own_ref, rows_ref):
@@ -254,7 +282,7 @@
     item_ref,
     cell_ref,
     order_ref,
-    last_ref,
+    mark_ref,
     qd_ref,
     kv_ref,
     parts_ref,
@@ -297,6 +325,13 @@
 
     def step(t, carry):
         wait(t)
+        for u in range(UNROLL):
+            pos = t * UNROLL + u
+
+            @pl.when(mark_ref[pos] >= 2)
+            def _():
+                stage_copy(lax.rem(order_ref[pos], STAGES), cell_ref[pos]).wait()
+
         found = []
         for u in range(UNROLL):
             pos = t * UNROLL + u
@@ -316,22 +351,18 @@
         for pos, item, grads, crossed in found:
             fresh = order_ref[pos] != order_ref[jnp.maximum(pos - 1, 0)]
             running = grads + jnp.where(fresh, 0.0, running)
-
-            @pl.when(last_ref[pos] > 0)
-            def _():
-                stage = lax.rem(order_ref[pos], STAGES)
-
-                @pl.when(order_ref[pos] >= STAGES)
-                def _():
-                    stage_copy(stage, cell_ref[pos]).wait()
-
-                stage_ref[stage] = running.astype(jnp.bfloat16)
-                stage_copy(stage, cell_ref[pos]).start()
-
+            stage_ref[lax.rem(order_ref[pos], STAGES)] = running.astype(jnp.bfloat16)
             at = pl.ds(item, S)
             partial_ref[at, :D] += crossed[S:, D:]
             partial_ref[at, D:] += crossed[:S, :D]
         sum_ref[...] = running
+        for u in range(UNROLL):
+            pos = t * UNROLL + u
+
+            @pl.when(lax.rem(mark_ref[pos], 2) > 0)
+            def _():
+                stage_copy(lax.rem(order_ref[pos], STAGES), cell_ref[pos]).start()
+
         start(t + DEPTH)
         return carry
 
@@ -439,38 +470,53 @@
     )
     kv_all = lax.all_gather(kv, Z_AXIS, axis=0, tiled=True)
     qd = by_head(query, grad_out)
-    random_blocks, universal_segment_indices, qd = lax.optimization_barrier(
-        (random_blocks, universal_segment_indices, qd)
-    )
     tokens = qd.shape[0]
     block_count = tokens // S
     group = block_count * y_count
     block_total = ctx_count * block_count
     cells = z_count * block_count
 
+    part = S // y_count
+    codes = random_blocks.reshape(1, -1)
+    codes = jnp.concatenate([codes // CODE, codes % CODE], 1).astype(jnp.bfloat16)
+    codes = jnp.pad(codes, ((0, 15), (0, 4 * D - codes.shape[1])))
+    sent = pl.pallas_call(
+        pick_kernel,
+        out_shape=jax.ShapeDtypeStruct((y_count, WORLDWIDE_COUNT * part + 16, 4 * D), jnp.bfloat16),
+        in_specs=[SMEM, ANY, ANY, VMEM],
+        out_specs=VMEM,
+        scratch_shapes=[
+            pltpu.VMEM((G, 4 * D), jnp.bfloat16),
+            pltpu.SemaphoreType.DMA((2 * WORLDWIDE_COUNT,)),
+        ],
+        compiler_params=PARAMS,
+        name="pick",
+    )(universal_segment_indices, qd, kv, codes)
     owners = universal_segment_indices // block_count
-    starts = universal_segment_indices % block_count * S
-    pieces = []
-    for g in range(WORLDWIDE_COUNT):
-        pieces.append(
-            jnp.concatenate(
-                [lax.dynamic_slice_in_dim(part, starts[g], S, 0) for part in (qd, kv)], 1
-            )
-        )
-    part = G // y_count
-    owner = owners[(y_place * part) // S]
-    sent = jnp.concatenate(pieces, 0).reshape(y_count, part, 4 * D)
-    picked = lax.dynamic_index_in_dim(exchange(sent, Y_AXIS), owner % y_count, 0, False)
-    sent = picked.reshape(z_count, part // z_count, 4 * D)
-    picked = lax.dynamic_index_in_dim(exchange(sent, Z_AXIS), owner // y_count, 0, False)
-    shared = to_all(picked, Z_AXIS).reshape(part, 4 * D)
-    shared = to_all(shared, Y_AXIS).reshape(G, 4 * D)
+
+    def chosen(arrived, place):
+        count = arrived.shape[0]
+        mask = jnp.arange(count, dtype=jnp.int32)[:, None] == place[None]
+        return jnp.sum(jnp.where(mask[:, :, None, None], arrived, 0), 0)
+
+    arrived = exchange(sent, Y_AXIS)
+    codes = arrived[:, WORLDWIDE_COUNT * part, : 2 * block_count * RANDOM]
+    codes = codes.astype(jnp.int32).reshape(y_count, 2, block_count * RANDOM)
+    random_group = (codes[:, 0] * CODE + codes[:, 1]).reshape(group, RANDOM)
+    arrived = arrived[:, : WORLDWIDE_COUNT * part].reshape(y_count, WORLDWIDE_COUNT, part, 4 * D)
+    qd_sent, arrived = lax.optimization_barrier((qd, arrived))
+    picked = chosen(arrived, owners % y_count)
+    sent = picked.reshape(WORLDWIDE_COUNT, z_count, -1, 4 * D).transpose(1, 0, 2, 3)
+    picked = chosen(exchange(sent, Z_AXIS), owners // y_count)
+    shared = to_all(picked, Z_AXIS).transpose(1, 0, 2, 3).reshape(WORLDWIDE_COUNT, part, 4 * D)
+    shared = to_all(shared, Y_AXIS).transpose(1, 0, 2, 3).reshape(G, 4 * D)
 
     shifts = range(1, y_count)
     forward = [[(i, (i + shift) % y_count) for i in range(y_count)] for shift in shifts]
     backward = [[(i, (i - shift) % y_count) for i in range(y_count)] for shift in shifts]
-    qd_group = jnp.concatenate([qd] + [lax.ppermute(qd, Y_AXIS, pairs) for pairs in forward], 0)
-    random_group = to_all(random_blocks[:, 0, :], Y_AXIS).reshape(group, RANDOM)
+    qd_group = jnp.concatenate(
+        [qd] + [lax.ppermute(qd_sent, Y_AXIS, pairs) for pairs in forward], 0
+    )
 
     ids = z_place * group + jnp.arange(group, dtype=jnp.int32)
     local = jnp.arange(group, dtype=jnp.int32) % block_count
@@ -505,7 +551,7 @@
     slot_list = jnp.where(real, slot_list, entries + group)
     item_list = slot_list % group
     item_list = (y_place - item_list // block_count) % y_count * block_count + item_list % block_count
-    last_list = last_list.astype(jnp.int32)
+    mark_list = last_list.astype(jnp.int32) + 2 * (fresh & (order_list >= STAGES))
     meta = jnp.stack(
         [(edge_count + UNROLL - 1) // UNROLL, y_place, jnp.sum(fresh.astype(jnp.int32))]
     ).astype(jnp.int32)
@@ -572,7 +618,7 @@
         input_output_aliases={9: 0},
         compiler_params=PARAMS,
         name="edge_grads",
-    )(*lists, order_list, last_list, qd_group, kv_all, parts, cleared)
+    )(*lists, order_list, mark_list, qd_group, kv_all, parts, cleared)
     returned = lax.psum_scatter(table, Z_AXIS, scatter_dimension=0, tiled=True)
     halves = [lax.ppermute(half, Y_AXIS, pairs) for half, pairs in zip(halves, backward)]
     rows_all = to_all(to_all(rows, Z_AXIS), Y_AXIS).reshape(ctx_count, 3, G)

time: 315 us -> 289 us (0.917)
  local copies, waits for them, and re-layouts: 25.5 us -> 16.6 us
  Pallas kernels: 42.4 us -> 35.6 us
  between operations: 23.2 us -> 17.2 us
  waiting for transfers between devices: 89.2 us -> 85.3 us
    reduce_scatter x1, waiting for transfers between devices: 19.1 us -> 6.88 us  [body(): returned = lax.psum_scatter(table, Z_AXIS, scatter_dimension=0, tiled=True)]
    all_gather x1, waiting for transfers between devices: 0.02 us -> 12.1 us  [body(): kv_all = lax.all_gather(kv, Z_AXIS, axis=0, tiled=True)]
    pallas_call x1, Pallas kernels: 21.8 us -> 13.7 us  [body(): pl.pallas_call(edge_grads_kernel, out_shape=(jax.ShapeDtypeStruct((cells...]
    unnamed x40 -> x22, local copies, waits for them, and re-layouts: 7.3 us -> 3.08 us
    all_to_all x11 -> x10, waiting for transfers between devices: 70 us -> 66.3 us  [exchange(): return lax.all_to_all(array, axes, split_axis=0, concat_axis=0, tiled=True)]
    all_to_all x11 -> x10, starting transfers between devices: 52.3 us -> 53.7 us  [exchange(): return lax.all_to_all(array, axes, split_axis=0, concat_axis=0, tiled=True)]
  transfers between devices with their start and end apart: 19 -> 18, of which waited for: 11 -> 12; matrix products, arithmetic and copies ran while one was open for 13% -> 10% of each run, Pallas kernels for 4% -> 5%
where the time goes in v4:
time: 289 us; the launch traced here: 286 us
  waiting for transfers between devices  85.3 us (30%)
  starting transfers between devices  70.5 us (24%)
  blocking collectives  41 us (14%)
  Pallas kernels  35.6 us (12%)
  other arithmetic  20.2 us (7%)
  between operations  17.2 us (6%)
  local copies, waits for them, and re-layouts  16.6 us (6%)
    all_to_all x10, waiting for transfers between devices, exchange(): return lax.all_to_all(array, axes, split_axis=0, concat_axis=0, tiled=True)  66.3 us
    all_to_all x10, starting transfers between devices, exchange(): return lax.all_to_all(array, axes, split_axis=0, concat_axis=0, tiled=True)  53.7 us
    all_to_all x3, blocking collectives, exchange(): return lax.all_to_all(array, axes, split_axis=0, concat_axis=0, tiled=True)  41 us
    pallas_call x1, Pallas kernels, body(): pl.pallas_call(edge_grads_kernel, out_shape=(jax.ShapeDtypeStruct((cells...  13.7 us
    all_gather x1, waiting for transfers between devices, body(): kv_all = lax.all_gather(kv, Z_AXIS, axis=0, tiled=True)  12.1 us
    pallas_call x1, Pallas kernels, body(): pl.pallas_call(own_grads_kernel, out_shape=(jax.ShapeDtypeStruct((tokens,...  9.38 us
    ppermute x3, starting transfers between devices, body(): lax.ppermute(qd_sent, Y_AXIS, pairs)  8.76 us
    ppermute x3, starting transfers between devices, body(): lax.ppermute(half, Y_AXIS, pairs)  8.07 us
  transfers between devices with their start and end apart: 18, of which 12 were waited for; matrix products, arithmetic and copies ran while one was open for 10% of the time, Pallas kernels for 5%

profile of v4, /device:TPU:1, one launch (start us, length us, event | category | flops | bytes accessed | tf_op | source)
XLA Modules:
  0.0 286.5 jit_solution(2577360251878487776)
XLA Ops:
  7.3 1.0 copy-done
  8.2 1.1 copy_bitcast_fusion.2
  9.4 19.2 %all_to_all.65 = bf16[8,128,256]{2,1,0:T(8,128)(2,1)} all-to-all(bf16[8,128,256]{2,1,0:T(8,128)(2,1)S(1)} %maximum_bitcast_fusion), channel_id=1, replica_groups=mesh['ctx_0'=16,'ctx_1'=4,'head'=8] {'head'}, dimensions={0} | all-to-all | bytes 1048576 | tf_op jit(solution)/shard_map/all_to_all | solution.py:59
  28.7 1.3 fusion.40
  30.7 1.0 copy_bitcast_fusion
  32.7 4.4 %all-to-all-start.1 = ((bf16[8,128,256]{2,1,0:T(8,128)(2,1)}), bf16[8,128,256]{2,1,0:T(8,128)(2,1)S(1)}, u32[]{:S(2)}, u32[]{:S(2)}) async-start(bf16[8,128,256]{2,1,0:T(8,128)(2,1)} %maximum_bitcast_fusion.1), calls=%async_computation.1 | async-start | bytes 1048576 | tf_op jit(solution)/shard_map/all_to_all | solution.py:59
  38.1 8.4 %all-to-all-done.1 = bf16[8,128,256]{2,1,0:T(8,128)(2,1)S(1)} async-done(((bf16[8,128,256]{2,1,0:T(8,128)(2,1)}), bf16[8,128,256]{2,1,0:T(8,128)(2,1)S(1)}, u32[]{:S(2)}, u32[]{:S(2)}) %all-to-all-start.1) | async-done | bytes 524320 | tf_op jit(solution)/shard_map/all_to_all | solution.py:59
  47.3 2.3 pick.1
  49.6 3.4 %all-to-all-start.2 = ((bf16[4,48,512]{2,1,0:T(8,128)(2,1)}), bf16[4,48,512]{2,1,0:T(8,128)(2,1)S(1)}, u32[]{:S(2)}, u32[]{:S(2)}) async-start(bf16[4,48,512]{2,1,0:T(8,128)(2,1)} %pick.1), calls=%async_computation.2 | async-start | bytes 393216 | tf_op jit(solution)/shard_map/all_to_all | solution.py:59
  54.3 3.9 %all-to-all-done.2 = bf16[4,48,512]{2,1,0:T(8,128)(2,1)S(1)} async-done(((bf16[4,48,512]{2,1,0:T(8,128)(2,1)}), bf16[4,48,512]{2,1,0:T(8,128)(2,1)S(1)}, u32[]{:S(2)}, u32[]{:S(2)}) %all-to-all-start.2) | async-done | bytes 196640 | tf_op jit(solution)/shard_map/all_to_all | solution.py:59
  58.2 2.5 collective-permute-start
  60.7 3.3 %collective-permute-start.1 = (bf16[1024,256]{1,0:T(8,128)(2,1)}, bf16[1024,256]{1,0:T(8,128)(2,1)S(1)}, u32[]{:S(2)}, u32[]{:S(2)}) collective-permute-start(bf16[1024,256]{1,0:T(8,128)(2,1)} %bitcast.98), channel_id=1, source_target_pairs={{0,16},{8,24},{16,0},{24,8},{1,17},{9,25},{17,1},{25,9},{2,18},{10... | collective-permute-start | bytes 1572872 | tf_op jit(solution)/shard_map/ppermute | solution.py:518
  64.1 2.9 %collective-permute-start.2 = (bf16[1024,256]{1,0:T(8,128)(2,1)}, bf16[1024,256]{1,0:T(8,128)(2,1)S(1)}, u32[]{:S(2)}, u32[]{:S(2)}) collective-permute-start(bf16[1024,256]{1,0:T(8,128)(2,1)} %bitcast.99), channel_id=1, source_target_pairs={{0,24},{8,0},{16,8},{24,16},{1,25},{9,1},{17,9},{25,17},{2,26},{10... | collective-permute-start | bytes 1572872 | tf_op jit(solution)/shard_map/ppermute | solution.py:518
  68.0 11.5 %all-to-all-start.3 = ((bf16[16,2,1,512]{3,1,2,0:T(2,128)(2,1)}), bf16[16,2,1,512]{3,1,2,0:T(2,128)(2,1)S(1)}, u32[]{:S(2)}, u32[]{:S(2)}) async-start(bf16[16,2,1,512]{3,1,2,0:T(2,128)(2,1)} %copy.178), calls=%async_computation.3 | async-start | bytes 65536 | tf_op jit(solution)/shard_map/all_to_all | solution.py:59
  82.4 1.2 fusion.25
  84.3 7.3 %all-to-all-done.3 = bf16[16,2,1,512]{3,1,2,0:T(2,128)(2,1)S(1)} async-done(((bf16[16,2,1,512]{3,1,2,0:T(2,128)(2,1)}), bf16[16,2,1,512]{3,1,2,0:T(2,128)(2,1)S(1)}, u32[]{:S(2)}, u32[]{:S(2)}) %all-to-all-start.3) | async-done | bytes 32800 | tf_op jit(solution)/shard_map/all_to_all | solution.py:59
  92.3 4.2 %all-to-all-start.4 = ((bf16[16,2,1,512]{3,1,2,0:T(2,128)(2,1)}), bf16[16,2,1,512]{3,1,2,0:T(2,128)(2,1)S(1)}, u32[]{:S(2)}, u32[]{:S(2)}) async-start(bf16[16,2,1,512]{3,1,2,0:T(2,128)(2,1)} %broadcast_in_dim.236), calls=%async_computation.4 | async-start | bytes 65536 | tf_op jit(solution)/shard_map/all_to_all | solution.py:59
  96.5 2.0 convert_reduce_fusion.3
  100.7 7.8 %all-to-all-done.4 = bf16[16,2,1,512]{3,1,2,0:T(2,128)(2,1)S(1)} async-done(((bf16[16,2,1,512]{3,1,2,0:T(2,128)(2,1)}), bf16[16,2,1,512]{3,1,2,0:T(2,128)(2,1)S(1)}, u32[]{:S(2)}, u32[]{:S(2)}) %all-to-all-start.4) | async-done | bytes 32800 | tf_op jit(solution)/shard_map/all_to_all | solution.py:59
  109.1 3.3 %all-to-all-start.5 = ((bf16[4,2,16,512]{3,2,1,0:T(8,128)(2,1)}), bf16[4,2,16,512]{3,2,1,0:T(8,128)(2,1)S(1)}, u32[]{:S(2)}, u32[]{:S(2)}) async-start(bf16[4,2,16,512]{3,2,1,0:T(8,128)(2,1)} %broadcast_in_dim.238), calls=%async_computation.5 | async-start | bytes 262144 | tf_op jit(solution)/shard_map/all_to_all | solution.py:59
  112.5 1.3 pad_add_fusion.1.meta_ref
  113.7 3.6 %all-to-all-done.5 = bf16[4,2,16,512]{3,2,1,0:T(8,128)(2,1)S(1)} async-done(((bf16[4,2,16,512]{3,2,1,0:T(8,128)(2,1)}), bf16[4,2,16,512]{3,2,1,0:T(8,128)(2,1)S(1)}, u32[]{:S(2)}, u32[]{:S(2)}) %all-to-all-start.5) | async-done | bytes 131104 | tf_op jit(solution)/shard_map/all_to_all | solution.py:59
  118.0 3.4 %own_stats.1 = (f32[3,16,64]{2,1,0:T(8,128)}, f32[3,128]{1,0:T(4,128)}) custom-call(f32[32]{0:T(128)} %reshape.387.bias_ref, bf16[1024,256]{1,0:T(8,128)(2,1)} %bitcast.100, bf16[1024,256]{1,0:T(8,128)(2,1)} %bitcast.94, bf16[128,512]{1,0:T(8,128)(2,1)} %bitcast.103), custom_call_target="tpu_custom_call" | custom-call | tf_op jit(solution)/shard_map/own_stats/pallas_call | solution.py:567
  121.5 2.5 pad_maximum_fusion.qd_ref
  124.0 12.1 %all-gather.2.cloned.1.call-done.kv_ref = bf16[16384,256]{1,0:T(8,128)(2,1)} async-done(((bf16[1024,256]{1,0:T(8,128)(2,1)}), bf16[16384,256]{1,0:T(8,128)(2,1)}) %all-gather.2.cloned.1.call-update) | async-done | bytes 8388624 | tf_op jit(solution)/shard_map/all_gather | solution.py:471
  136.1 6.8 %edge_stats.1 = (f32[4,128,128]{2,1,0:T(8,128)}, bf16[16384,256]{1,0:T(8,128)(2,1)}) custom-call(s32[3]{0:T(128)} %pad_add_fusion.1.meta_ref, s32[256]{0:T(256)} %get-tuple-element.49.slot_ref, s32[256]{0:T(256)} %get-tuple-element.48.item_ref, s32[256]{0:T(256)} %copy-done.5, bf16[4096,256]{1,0:T(8,128)(2,1)} %pad_maximum_fusion.qd_ref, ...), custom_call_target="tpu_custom_call" | custom-call | tf_op jit(solution)/shard_map/edge_stats/pallas_call | solution.py:584
  142.9 5.4 %all-to-all-start.6 = ((f32[4,128,128]{2,1,0:T(8,128)}), f32[4,128,128]{2,1,0:T(8,128)S(1)}, u32[]{:S(2)}, u32[]{:S(2)}) async-start(f32[4,128,128]{2,1,0:T(8,128)} %get-tuple-element.30), calls=%async_computation.6 | async-start | bytes 524288 | tf_op jit(solution)/shard_map/all_to_all | solution.py:59
  148.3 2.6 fusion.26
  150.9 3.0 %all-to-all-done.6.parts_ref = f32[4,128,128]{2,1,0:T(8,128)S(1)} async-done(((f32[4,128,128]{2,1,0:T(8,128)}), f32[4,128,128]{2,1,0:T(8,128)S(1)}, u32[]{:S(2)}, u32[]{:S(2)}) %all-to-all-start.6) | async-done | bytes 262176 | tf_op jit(solution)/shard_map/all_to_all | solution.py:59
  154.5 13.7 %edge_grads.1 = (bf16[16384,256]{1,0:T(8,128)(2,1)}, f32[3,64,128]{2,1,0:T(8,128)}, f32[1024,256]{1,0:T(8,128)}, bf16[1024,256]{1,0:T(8,128)(2,1)}, bf16[1024,25...) custom-call(s32[3]{0:T(128)} %pad_add_fusion.1.meta_ref, ...), custom_call_target="tpu_custom_call", output_to_operand_aliasing={{0}: (9, {})} | custom-call | tf_op jit(solution)/shard_map/edge_grads/pallas_call | solution.py:601
  169.5 11.2 %all-to-all-start.7 = ((f32[16,3,128]{2,1,0:T(4,128)}), f32[16,3,128]{2,1,0:T(4,128)S(1)}, u32[]{:S(2)}, u32[]{:S(2)}) async-start(f32[16,3,128]{2,1,0:T(4,128)} %broadcast_in_dim.242), calls=%async_computation.7 | async-start | bytes 65536 | tf_op jit(solution)/shard_map/all_to_all | solution.py:59
  180.9 11.5 %all-to-all-done.7 = f32[16,3,128]{2,1,0:T(4,128)S(1)} async-done(((f32[16,3,128]{2,1,0:T(4,128)}), f32[16,3,128]{2,1,0:T(4,128)S(1)}, u32[]{:S(2)}, u32[]{:S(2)}) %all-to-all-start.7) | async-done | bytes 24608 | tf_op jit(solution)/shard_map/all_to_all | solution.py:59
  193.0 3.3 %all-to-all-start.8 = ((f32[4,16,3,128]{3,1,2,0:T(8,128)}), f32[4,16,3,128]{3,1,2,0:T(8,128)S(1)}, u32[]{:S(2)}, u32[]{:S(2)}) async-start(f32[4,16,3,128]{3,1,2,0:T(8,128)} %broadcast_in_dim.243), calls=%async_computation.8 | async-start | bytes 196608 | tf_op jit(solution)/shard_map/all_to_all | solution.py:59
  196.9 4.1 %all-to-all-done.8 = f32[4,16,3,128]{3,1,2,0:T(8,128)S(1)} async-done(((f32[4,16,3,128]{3,1,2,0:T(8,128)}), f32[4,16,3,128]{3,1,2,0:T(8,128)S(1)}, u32[]{:S(2)}, u32[]{:S(2)}) %all-to-all-start.8) | async-done | bytes 98336 | tf_op jit(solution)/shard_map/all_to_all | solution.py:59
  201.7 9.4 %own_grads.1 = (f32[1024,256]{1,0:T(8,128)}, f32[1024,256]{1,0:T(8,128)}, f32[256,256]{1,0:T(8,128)}) custom-call(s32[3]{0:T(128)} %pad_add_fusion.1.meta_ref, f32[32]{0:T(128)} %reshape.387.bias_ref, f32[16]{0:T(128)} %broadcast_select_fusion.1.flag_ref, bf16[1024,256]{1,0:T(8,128)(2,1)} %bitcast.102, bf16[1024,256]{1,0:T(8,128)(2,1)} %bitcast.95, ...), custom_call_target="tpu_custom_call" | custom-call | tf_op jit(solution)/shard_map/own_grads/pallas_call | solution.py:626
  211.0 1.1 convert_element_type.89
  212.1 7.2 %all_to_all.66 = bf16[4,64,256]{2,1,0:T(8,128)(2,1)S(1)} all-to-all(bf16[4,64,256]{2,1,0:T(8,128)(2,1)S(1)} %bitcast.107), channel_id=1, replica_groups=mesh['ctx_0'=16,'ctx_1'=4,'head'=8] {'ctx_1'}, dimensions={0} | all-to-all | bytes 262144 | tf_op jit(solution)/shard_map/all_to_all | solution.py:59
  219.4 14.6 %all_to_all.67 = bf16[16,4,256]{2,1,0:T(4,128)(2,1)S(1)} all-to-all(bf16[16,4,256]{2,1,0:T(4,128)(2,1)S(1)} %reshape.393), channel_id=1, replica_groups=mesh['ctx_0'=16,'ctx_1'=4,'head'=8] {'ctx_0'}, dimensions={0} | all-to-all | bytes 65536 | tf_op jit(solution)/shard_map/all_to_all | solution.py:59
  234.6 3.5 %all-to-all-start.11 = ((bf16[16,4,256]{2,1,0:T(4,128)(2,1)}), bf16[16,4,256]{2,1,0:T(4,128)(2,1)S(1)}, u32[]{:S(2)}, u32[]{:S(2)}) async-start(bf16[16,4,256]{2,1,0:T(4,128)(2,1)} %broadcast_in_dim.244), calls=%async_computation.11 | async-start | bytes 65536 | tf_op jit(solution)/shard_map/all_to_all | solution.py:59
  238.1 2.6 collective-permute-start.3
  240.7 3.6 %collective-permute-start.4 = (bf16[1024,256]{1,0:T(8,128)(2,1)}, bf16[1024,256]{1,0:T(8,128)(2,1)S(1)}, u32[]{:S(2)}, u32[]{:S(2)}) collective-permute-start(bf16[1024,256]{1,0:T(8,128)(2,1)} %get-tuple-element.38), channel_id=1, source_target_pairs={{0,16},{8,24},{16,0},{24,8},{1,17},{9,25},{17,1},{25,9},{2,18},{10... | collective-permute-start | bytes 1572872 | tf_op jit(solution)/shard_map/ppermute | solution.py:623
  244.3 1.9 collective-permute-start.5
  246.2 3.9 %all-to-all-done.11 = bf16[16,4,256]{2,1,0:T(4,128)(2,1)S(1)} async-done(((bf16[16,4,256]{2,1,0:T(4,128)(2,1)}), bf16[16,4,256]{2,1,0:T(4,128)(2,1)S(1)}, u32[]{:S(2)}, u32[]{:S(2)}) %all-to-all-start.11) | async-done | bytes 32800 | tf_op jit(solution)/shard_map/all_to_all | solution.py:59
  250.8 3.3 %all-to-all-start.12 = ((bf16[4,64,256]{2,1,0:T(8,128)(2,1)}), bf16[4,64,256]{2,1,0:T(8,128)(2,1)S(1)}, u32[]{:S(2)}, u32[]{:S(2)}) async-start(bf16[4,64,256]{2,1,0:T(8,128)(2,1)} %broadcast_in_dim.246), calls=%async_computation.12 | async-start | bytes 262144 | tf_op jit(solution)/shard_map/all_to_all | solution.py:59
  254.5 12.9 %all-to-all-done.12 = bf16[4,64,256]{2,1,0:T(8,128)(2,1)S(1)} async-done(((bf16[4,64,256]{2,1,0:T(8,128)(2,1)}), bf16[4,64,256]{2,1,0:T(8,128)(2,1)S(1)}, u32[]{:S(2)}, u32[]{:S(2)}) %all-to-all-start.12) | async-done | bytes 131104 | tf_op jit(solution)/shard_map/all_to_all | solution.py:59
  267.5 1.9 fusion.4
  270.2 6.9 %reduce-scatter.2.cloned.1.call-done = bf16[1024,256]{1,0:T(8,128)(2,1)} async-done(((bf16[16384,256]{1,0:T(8,128)(2,1)}), bf16[1024,256]{1,0:T(8,128)(2,1)}) %reduce-scatter.2.cloned.1.call-update) | async-done | bytes 524304 | tf_op jit(solution)/shard_map/reduce_scatter | solution.py:622
  277.0 1.7 fusion.1
  (106 shorter events, 18.4 us)
Async XLA Ops:
  7.2 1.1 copy-start
  7.2 30.1 %copy-start.9 = (s32[16,1,3]{0,1,2:T(1,128)S(1)}, s32[16,1,3]{0,1,2:T(1,128)}, u32[]{:S(2)}) copy-start(s32[16,1,3]{0,1,2:T(1,128)} %param.10) | copy-start | bytes 580
  7.2 24.5 %copy-start.4 = (bf16[128,1024]{1,0:T(8,128)(2,1)S(1)}, bf16[128,1024]{1,0:T(8,128)(2,1)}, u32[]{:S(2)}) copy-start(bf16[128,1024]{1,0:T(8,128)(2,1)} %param.6) | copy-start | bytes 786436
  7.2 29.9 %copy-start.6 = (s32[2]{0:T(128)S(1)}, s32[2]{0:T(128)}, u32[]{:S(2)}) copy-start(s32[2]{0:T(128)} %index_ref.1) | copy-start | bytes 28
  7.2 128.9 %all-gather.2.cloned.1.call-start = ((), (), s32[]{:S(2)}) async-start(), calls=%async_computation.14 | async-start | bytes 8912896 | tf_op jit(solution)/shard_map/all_gather | solution.py:471
  9.3 70.2 %copy-start.7 = (s32[2]{0:T(128)S(1)}, s32[2]{0:T(128)}, u32[]{:S(2)}) copy-start(s32[2]{0:T(128)} %index_ref.1) | copy-start | bytes 28
  32.7 13.8 %all-to-all-start.1 = ((bf16[8,128,256]{2,1,0:T(8,128)(2,1)}), bf16[8,128,256]{2,1,0:T(8,128)(2,1)S(1)}, u32[]{:S(2)}, u32[]{:S(2)}) async-start(bf16[8,128,256]{2,1,0:T(8,128)(2,1)} %maximum_bitcast_fusion.1), calls=%async_computation.1 | async-start | bytes 1048576 | tf_op jit(solution)/shard_map/all_to_all | solution.py:59
  46.5 0.8 copy-start.1
  49.6 8.6 %all-to-all-start.2 = ((bf16[4,48,512]{2,1,0:T(8,128)(2,1)}), bf16[4,48,512]{2,1,0:T(8,128)(2,1)S(1)}, u32[]{:S(2)}, u32[]{:S(2)}) async-start(bf16[4,48,512]{2,1,0:T(8,128)(2,1)} %pick.1), calls=%async_computation.2 | async-start | bytes 393216 | tf_op jit(solution)/shard_map/all_to_all | solution.py:59
  58.2 63.3 %collective-permute-start = (bf16[1024,256]{1,0:T(8,128)(2,1)}, bf16[1024,256]{1,0:T(8,128)(2,1)S(1)}, u32[]{:S(2)}, u32[]{:S(2)}) collective-permute-start(bf16[1024,256]{1,0:T(8,128)(2,1)} %bitcast.97), channel_id=1, source_target_pairs={{0,8},{8,16},{16,24},{24,0},{1,9},{9,17},{17,25},{25,1},{2,10},{10... | collective-permute-start | bytes 1572872 | tf_op jit(solution)/shard_map/ppermute | solution.py:518
  60.7 60.7 %collective-permute-start.1 = (bf16[1024,256]{1,0:T(8,128)(2,1)}, bf16[1024,256]{1,0:T(8,128)(2,1)S(1)}, u32[]{:S(2)}, u32[]{:S(2)}) collective-permute-start(bf16[1024,256]{1,0:T(8,128)(2,1)} %bitcast.98), channel_id=1, source_target_pairs={{0,16},{8,24},{16,0},{24,8},{1,17},{9,25},{17,1},{25,9},{2,18},{10... | collective-permute-start | bytes 1572872 | tf_op jit(solution)/shard_map/ppermute | solution.py:518
  64.1 57.4 %collective-permute-start.2 = (bf16[1024,256]{1,0:T(8,128)(2,1)}, bf16[1024,256]{1,0:T(8,128)(2,1)S(1)}, u32[]{:S(2)}, u32[]{:S(2)}) collective-permute-start(bf16[1024,256]{1,0:T(8,128)(2,1)} %bitcast.99), channel_id=1, source_target_pairs={{0,24},{8,0},{16,8},{24,16},{1,25},{9,1},{17,9},{25,17},{2,26},{10... | collective-permute-start | bytes 1572872 | tf_op jit(solution)/shard_map/ppermute | solution.py:518
  68.0 23.5 %all-to-all-start.3 = ((bf16[16,2,1,512]{3,1,2,0:T(2,128)(2,1)}), bf16[16,2,1,512]{3,1,2,0:T(2,128)(2,1)S(1)}, u32[]{:S(2)}, u32[]{:S(2)}) async-start(bf16[16,2,1,512]{3,1,2,0:T(2,128)(2,1)} %copy.178), calls=%async_computation.3 | async-start | bytes 65536 | tf_op jit(solution)/shard_map/all_to_all | solution.py:59
  82.3 53.7 %copy-start.5 = (s32[256]{0:T(256)}, s32[256]{0:T(256)S(1)}, u32[]{:S(2)}) copy-start(s32[256]{0:T(256)S(1)} %get-tuple-element.43.cell_ref) | copy-start | bytes 3076
  92.3 16.2 %all-to-all-start.4 = ((bf16[16,2,1,512]{3,1,2,0:T(2,128)(2,1)}), bf16[16,2,1,512]{3,1,2,0:T(2,128)(2,1)S(1)}, u32[]{:S(2)}, u32[]{:S(2)}) async-start(bf16[16,2,1,512]{3,1,2,0:T(2,128)(2,1)} %broadcast_in_dim.236), calls=%async_computation.4 | async-start | bytes 65536 | tf_op jit(solution)/shard_map/all_to_all | solution.py:59
  109.1 8.2 %all-to-all-start.5 = ((bf16[4,2,16,512]{3,2,1,0:T(8,128)(2,1)}), bf16[4,2,16,512]{3,2,1,0:T(8,128)(2,1)S(1)}, u32[]{:S(2)}, u32[]{:S(2)}) async-start(bf16[4,2,16,512]{3,2,1,0:T(8,128)(2,1)} %broadcast_in_dim.238), calls=%async_computation.5 | async-start | bytes 262144 | tf_op jit(solution)/shard_map/all_to_all | solution.py:59
  142.9 11.0 %all-to-all-start.6 = ((f32[4,128,128]{2,1,0:T(8,128)}), f32[4,128,128]{2,1,0:T(8,128)S(1)}, u32[]{:S(2)}, u32[]{:S(2)}) async-start(f32[4,128,128]{2,1,0:T(8,128)} %get-tuple-element.30), calls=%async_computation.6 | async-start | bytes 524288 | tf_op jit(solution)/shard_map/all_to_all | solution.py:59
  148.3 128.7 %reduce-scatter.2.cloned.1.call-start = ((), (), s32[]{:S(2)}) async-start(), calls=%async_computation.15 | async-start | bytes 8912896 | tf_op jit(solution)/shard_map/reduce_scatter | solution.py:622
  153.8 0.7 copy-start.2
  168.3 0.7 copy-start.8
  168.3 76.0 %copy-start.10 = (bf16[1024,256]{1,0:T(8,128)(2,1)S(1)}, bf16[1024,256]{1,0:T(8,128)(2,1)}, u32[]{:S(2)}) copy-start(bf16[1024,256]{1,0:T(8,128)(2,1)} %get-tuple-element.39) | copy-start | bytes 1572868
  169.5 22.8 %all-to-all-start.7 = ((f32[16,3,128]{2,1,0:T(4,128)}), f32[16,3,128]{2,1,0:T(4,128)S(1)}, u32[]{:S(2)}, u32[]{:S(2)}) async-start(f32[16,3,128]{2,1,0:T(4,128)} %broadcast_in_dim.242), calls=%async_computation.7 | async-start | bytes 65536 | tf_op jit(solution)/shard_map/all_to_all | solution.py:59
  193.0 7.9 %all-to-all-start.8 = ((f32[4,16,3,128]{3,1,2,0:T(8,128)}), f32[4,16,3,128]{3,1,2,0:T(8,128)S(1)}, u32[]{:S(2)}, u32[]{:S(2)}) async-start(f32[4,16,3,128]{3,1,2,0:T(8,128)} %broadcast_in_dim.243), calls=%async_computation.8 | async-start | bytes 196608 | tf_op jit(solution)/shard_map/all_to_all | solution.py:59
  211.0 66.0 %copy-start.3 = (f32[1024,256]{1,0:T(8,128)S(1)}, f32[1024,256]{1,0:T(8,128)}, u32[]{:S(2)}) copy-start(f32[1024,256]{1,0:T(8,128)} %get-tuple-element.41) | copy-start | bytes 3145732
  234.6 15.6 %all-to-all-start.11 = ((bf16[16,4,256]{2,1,0:T(4,128)(2,1)}), bf16[16,4,256]{2,1,0:T(4,128)(2,1)S(1)}, u32[]{:S(2)}, u32[]{:S(2)}) async-start(bf16[16,4,256]{2,1,0:T(4,128)(2,1)} %broadcast_in_dim.244), calls=%async_computation.11 | async-start | bytes 65536 | tf_op jit(solution)/shard_map/all_to_all | solution.py:59
  238.1 29.3 %collective-permute-start.3 = (bf16[1024,256]{1,0:T(8,128)(2,1)}, bf16[1024,256]{1,0:T(8,128)(2,1)S(1)}, u32[]{:S(2)}, u32[]{:S(2)}) collective-permute-start(bf16[1024,256]{1,0:T(8,128)(2,1)} %get-tuple-element.37), channel_id=1, source_target_pairs={{0,24},{8,0},{16,8},{24,16},{1,25},{9,1},{17,9},{25,17},{2,26},{10... | collective-permute-start | bytes 1572872 | tf_op jit(solution)/shard_map/ppermute | solution.py:623
  240.7 26.8 %collective-permute-start.4 = (bf16[1024,256]{1,0:T(8,128)(2,1)}, bf16[1024,256]{1,0:T(8,128)(2,1)S(1)}, u32[]{:S(2)}, u32[]{:S(2)}) collective-permute-start(bf16[1024,256]{1,0:T(8,128)(2,1)} %get-tuple-element.38), channel_id=1, source_target_pairs={{0,16},{8,24},{16,0},{24,8},{1,17},{9,25},{17,1},{25,9},{2,18},{10... | collective-permute-start | bytes 1572872 | tf_op jit(solution)/shard_map/ppermute | solution.py:623
  244.3 23.2 %collective-permute-start.5 = (bf16[1024,256]{1,0:T(8,128)(2,1)S(1)}, bf16[1024,256]{1,0:T(8,128)(2,1)S(1)}, u32[]{:S(2)}, u32[]{:S(2)}) collective-permute-start(bf16[1024,256]{1,0:T(8,128)(2,1)S(1)} %copy-done.10), channel_id=1, source_target_pairs={{0,8},{8,16},{16,24},{24,0},{1,9},{9,17},{17,25},{25,1},{2,10},{10... | collective-permute-start | bytes 1572872 | tf_op jit(solution)/shard_map/ppermute | solution.py:623
  250.8 16.5 %all-to-all-start.12 = ((bf16[4,64,256]{2,1,0:T(8,128)(2,1)}), bf16[4,64,256]{2,1,0:T(8,128)(2,1)S(1)}, u32[]{:S(2)}, u32[]{:S(2)}) async-start(bf16[4,64,256]{2,1,0:T(8,128)(2,1)} %broadcast_in_dim.246), calls=%async_computation.12 | async-start | bytes 262144 | tf_op jit(solution)/shard_map/all_to_all | solution.py:59
Sparse Core Ops, SparseCore 0:
  28.8 107.2 all-gather.1
  168.4 108.5 reduce-scatter.1

commit v5 on v4

--- a/solution.py
+++ b/solution.py
@@ -22,6 +22,7 @@
 DEPTH = 4
 STAGES = 32
 CODE = 32
+LOG2E = 1.4426950408889634
 SLOTS = 1 + RANDOM
 D = FEATURE_LENGTH
 S = SPAN_TOKENS
@@ -160,27 +161,23 @@
 
 
 def cell_fetcher(meta_ref, cell_ref, kv_ref, fetch_ref, fetch_sems):
-    def copies(t):
-        found = []
-        for u in range(UNROLL):
-            buffer = lax.rem(t, DEPTH) * UNROLL + u
-            cell = pl.multiple_of(cell_ref[t * UNROLL + u] * S, S)
-            found.append(
-                pltpu.make_async_copy(
-                    kv_ref.at[pl.ds(cell, S), :], fetch_ref.at[buffer], fetch_sems.at[buffer]
-                )
-            )
-        return found
-
     def start(t):
         @pl.when(t < meta_ref[0])
         def _():
-            for copy in copies(t):
-                copy.start()
+            bank = t & (DEPTH - 1)
+            for u in range(UNROLL):
+                cell = pl.multiple_of(cell_ref[t * UNROLL + u] * S, S)
+                pltpu.make_async_copy(
+                    kv_ref.at[pl.ds(cell, S), :],
+                    fetch_ref.at[bank, pl.ds(u * S, S), :],
+                    fetch_sems.at[bank],
+                ).start()
 
     def wait(t):
-        for copy in copies(t):
-            copy.wait()
+        bank = t & (DEPTH - 1)
+        pltpu.make_async_copy(
+            kv_ref.at[pl.ds(0, UNROLL * S), :], fetch_ref.at[bank], fetch_sems.at[bank]
+        ).wait()
 
     return start, wait
 
@@ -192,8 +189,8 @@
     )
 
 
-def lane_scale():
-    return jnp.where(lax.broadcasted_iota(jnp.int32, (1, 2 * S), 1) < S, SCALE, 1.0)
+def lane_scale(low, high):
+    return jnp.where(lax.broadcasted_iota(jnp.int32, (1, 2 * S), 1) < S, low, high)
 
 
 def edge_stats_kernel(
@@ -230,7 +227,7 @@
     top_ref[...] = jnp.full(top_ref.shape, NEG, jnp.float32)
     total_ref[...] = jnp.zeros(total_ref.shape, jnp.float32)
     slope_ref[...] = jnp.zeros(slope_ref.shape, jnp.float32)
-    factor = lane_scale()
+    factor = lane_scale(SCALE, 1.0)
 
     def step(t, carry):
         wait(t)
@@ -238,7 +235,7 @@
         for u in range(UNROLL):
             pos = t * UNROLL + u
             item = pl.multiple_of(item_ref[pos] * S, S)
-            pairs = fetch_ref[lax.rem(t, DEPTH) * UNROLL + u]
+            pairs = fetch_ref[t & (DEPTH - 1), u * S : (u + 1) * S, :]
             both = dot_nt(pairs, diagonal(qd_ref[pl.ds(item, S), :])) * factor
             top = jnp.max(both, axis=0, keepdims=True)
             weights = jnp.exp(both - top)
@@ -278,11 +275,13 @@
 
 def edge_grads_kernel(
     meta_ref,
-    slot_ref,
+    row_ref,
     item_ref,
     cell_ref,
-    order_ref,
-    mark_ref,
+    stage_pos_ref,
+    fresh_ref,
+    last_ref,
+    reuse_ref,
     qd_ref,
     kv_ref,
     parts_ref,
@@ -311,12 +310,14 @@
         ]
     )
     inverse = 1.0 / total
-    final_ref[0] = top
-    final_ref[1] = inverse
-    final_ref[2] = slope * inverse
+    final_ref[0, :group, :] = top * LOG2E
+    final_ref[1, :group, :] = inverse
+    final_ref[2, :group, :] = slope * inverse * SCALE
+    final_ref[0, group:, :] = jnp.full((8, 2 * S), -NEG, jnp.float32)
+    final_ref[1:, group:, :] = jnp.zeros((2, 8, 2 * S), jnp.float32)
     partial_ref[...] = jnp.zeros(partial_ref.shape, jnp.float32)
     sum_ref[...] = jnp.zeros(sum_ref.shape, jnp.float32)
-    factor = lane_scale()
+    factor = lane_scale(SCALE * LOG2E, SCALE)
     low_half = lax.broadcasted_iota(jnp.int32, (S, 2 * S), 1) < S
 
     def stage_copy(stage, cell):
@@ -328,40 +329,36 @@
         for u in range(UNROLL):
             pos = t * UNROLL + u
 
-            @pl.when(mark_ref[pos] >= 2)
+            @pl.when(reuse_ref[pos] > 0)
             def _():
-                stage_copy(lax.rem(order_ref[pos], STAGES), cell_ref[pos]).wait()
+                stage_copy(stage_pos_ref[pos], 0).wait()
 
         found = []
         for u in range(UNROLL):
             pos = t * UNROLL + u
-            slot = slot_ref[pos]
-            live = slot < SLOTS * group
-            row = pl.ds(lax.rem(slot, group), 1)
+            row = pl.ds(row_ref[pos], 1)
             item = pl.multiple_of(item_ref[pos] * S, S)
-            pairs = fetch_ref[lax.rem(t, DEPTH) * UNROLL + u]
+            pairs = fetch_ref[t & (DEPTH - 1), u * S : (u + 1) * S, :]
             corner = diagonal(qd_ref[pl.ds(item, S), :])
             both = dot_nt(pairs, corner) * factor
-            prob = jnp.exp(both - final_ref[0, row, :]) * final_ref[1, row, :]
-            dscore = prob * ((pltpu.roll(both, S, 1) - final_ref[2, row, :]) * SCALE)
-            packed = jnp.where(low_half, dscore, pltpu.roll(prob, S, 1))
-            packed = jnp.where(live, packed, 0.0).astype(jnp.bfloat16)
-            found.append((pos, item, dot_nn(packed, corner), dot_tn(packed, pairs)))
+            prob = jnp.exp2(both - final_ref[0, row, :]) * final_ref[1, row, :]
+            dscore = prob * (pltpu.roll(both, S, 1) - final_ref[2, row, :])
+            packed = jnp.where(low_half, dscore, pltpu.roll(prob, S, 1)).astype(jnp.bfloat16)
+            found.append((pos, item, jnp.concatenate([dot_nn(packed[:, :S], corner[:S, :D]), dot_nn(packed[:, S:], corner[S:, D:])], 1), dot_tn(packed[:, S:], pairs[:, D:]), dot_tn(packed[:, :S], pairs[:, :D])))
         running = sum_ref[...]
-        for pos, item, grads, crossed in found:
-            fresh = order_ref[pos] != order_ref[jnp.maximum(pos - 1, 0)]
-            running = grads + jnp.where(fresh, 0.0, running)
-            stage_ref[lax.rem(order_ref[pos], STAGES)] = running.astype(jnp.bfloat16)
+        for pos, item, grads, mixed, dq in found:
+            running = grads + jnp.where(fresh_ref[pos] > 0, 0.0, running)
+            stage_ref[stage_pos_ref[pos]] = running.astype(jnp.bfloat16)
             at = pl.ds(item, S)
-            partial_ref[at, :D] += crossed[S:, D:]
-            partial_ref[at, D:] += crossed[:S, :D]
+            partial_ref[at, :D] += mixed
+            partial_ref[at, D:] += dq
         sum_ref[...] = running
         for u in range(UNROLL):
             pos = t * UNROLL + u
 
-            @pl.when(lax.rem(mark_ref[pos], 2) > 0)
+            @pl.when(last_ref[pos] > 0)
             def _():
-                stage_copy(lax.rem(order_ref[pos], STAGES), cell_ref[pos]).start()
+                stage_copy(stage_pos_ref[pos], cell_ref[pos]).start()
 
         start(t + DEPTH)
         return carry
@@ -430,8 +427,8 @@
         slope = final_ref[2, pl.ds(first + i, 1), :S]
 
         def both(scores, slopes):
-            prob = jnp.exp(scores - top) * inverse
-            dscore = (prob * ((slopes - slope) * SCALE)).astype(jnp.bfloat16)
+            prob = jnp.exp2(scores * LOG2E - top) * inverse
+            dscore = (prob * (slopes * SCALE - slope)).astype(jnp.bfloat16)
             return prob.astype(jnp.bfloat16), dscore
 
         prob, dscore = both(scores, slopes)
@@ -551,7 +548,14 @@
     slot_list = jnp.where(real, slot_list, entries + group)
     item_list = slot_list % group
     item_list = (y_place - item_list // block_count) % y_count * block_count + item_list % block_count
-    mark_list = last_list.astype(jnp.int32) + 2 * (fresh & (order_list >= STAGES))
+    row_list = jnp.where(real, slot_list % group, group)
+    grad_lists = (
+        row_list,
+        order_list % STAGES,
+        fresh.astype(jnp.int32),
+        last_list.astype(jnp.int32),
+        (fresh & (order_list >= STAGES)).astype(jnp.int32),
+    )
     meta = jnp.stack(
         [(edge_count + UNROLL - 1) // UNROLL, y_place, jnp.sum(fresh.astype(jnp.int32))]
     ).astype(jnp.int32)
@@ -577,9 +581,10 @@
     )(bias, qd, kv, shared)
 
     stat_rows = (SLOTS + 1) * group + 8
+    own, grad_lists = lax.optimization_barrier((own, grad_lists))
     fetch_scratch = [
-        pltpu.VMEM((DEPTH * UNROLL, S, 2 * D), jnp.bfloat16),
-        pltpu.SemaphoreType.DMA((DEPTH * UNROLL,)),
+        pltpu.VMEM((DEPTH, UNROLL * S, 2 * D), jnp.bfloat16),
+        pltpu.SemaphoreType.DMA((DEPTH,)),
     ]
     stats, cleared = pl.pallas_call(
         edge_stats_kernel,
@@ -602,11 +607,11 @@
         edge_grads_kernel,
         out_shape=(
             jax.ShapeDtypeStruct((cells * S, 2 * D), jnp.bfloat16),
-            jax.ShapeDtypeStruct((3, group, 2 * S), f32),
+            jax.ShapeDtypeStruct((3, group + 8, 2 * S), f32),
             jax.ShapeDtypeStruct((tokens, 2 * D), f32),
         )
         + (jax.ShapeDtypeStruct((tokens, 2 * D), jnp.bfloat16),) * (y_count - 1),
-        in_specs=[SMEM] * 6 + [VMEM, ANY, VMEM, ANY],
+        in_specs=[SMEM] * 8 + [VMEM, ANY, VMEM, ANY],
         out_specs=(ANY,) + (VMEM,) * (y_count + 1),
         scratch_shapes=[
             pltpu.VMEM((group * S, 2 * D), f32),
@@ -615,10 +620,10 @@
         ]
         + fetch_scratch
         + [pltpu.SemaphoreType.DMA((STAGES,))],
-        input_output_aliases={9: 0},
+        input_output_aliases={11: 0},
         compiler_params=PARAMS,
         name="edge_grads",
-    )(*lists, order_list, mark_list, qd_group, kv_all, parts, cleared)
+    )(meta, grad_lists[0], item_list, cell_list, *grad_lists[1:], qd_group, kv_all, parts, cleared)
     returned = lax.psum_scatter(table, Z_AXIS, scatter_dimension=0, tiled=True)
     halves = [lax.ppermute(half, Y_AXIS, pairs) for half, pairs in zip(halves, backward)]
     rows_all = to_all(to_all(rows, Z_AXIS), Y_AXIS).reshape(ctx_count, 3, G)
@@ -646,14 +651,19 @@
     shared_sums = summed.reshape(2, WORLDWIDE_COUNT, 1, S, 2 * D).astype(f32)
 
     mixed = sum([half.astype(f32) for half in halves], mixed).reshape(block_count, S, 2 * D)
-    pairs = (returned.astype(f32) + pairs).reshape(block_count, S, 2 * D)
     for g in range(WORLDWIDE_COUNT):
         mask = hits[:, g][:, None, None]
         mixed = jnp.where(mask, shared_sums[1, g], mixed)
-        pairs = pairs + jnp.where(mask, shared_sums[0, g], 0.0)
     mixed = mixed.reshape(tokens, 2 * D).astype(jnp.bfloat16)
-    pairs = pairs.reshape(tokens, 2 * D).astype(jnp.bfloat16)
-    return mixed[:, :D], mixed[:, D:], pairs[:, :D], pairs[:, D:]
+    pairs = pairs.reshape(block_count, S, 2 * D)
+    for g in range(WORLDWIDE_COUNT):
+        pairs = pairs + jnp.where(hits[:, g][:, None, None], shared_sums[0, g], 0.0)
+    pairs = lax.optimization_barrier((pairs.reshape(tokens, 2 * D), mixed))[0]
+    grads = [
+        (returned[:, half].astype(f32) + pairs[:, half]).astype(jnp.bfloat16)
+        for half in (slice(0, D), slice(D, 2 * D))
+    ]
+    return mixed[:, :D], mixed[:, D:], grads[0], grads[1]
 
 
 def solution(mesh):

time: 289 us -> 284 us (0.983)
  waiting for transfers between devices: 85.3 us -> 73.6 us
  blocking collectives: 41 us -> 51 us
  starting transfers between devices: 70.5 us -> 67.3 us
    all_to_all x3 -> x4, blocking collectives: 41 us -> 51 us  [exchange(): return lax.all_to_all(array, axes, split_axis=0, concat_axis=0, tiled=True)]
    all_gather x1, waiting for transfers between devices: 12.1 us -> 6.42 us  [body(): kv_all = lax.all_gather(kv, Z_AXIS, axis=0, tiled=True)]
    all_to_all x10 -> x9, starting transfers between devices: 53.7 us -> 50.3 us  [exchange(): return lax.all_to_all(array, axes, split_axis=0, concat_axis=0, tiled=True)]
    convert_element_type x1 -> x3, other arithmetic: 1.74 us -> 5.09 us  [the longest x1 2.58 us: body(): fresh.astype(jnp.int32)]
    reduce_scatter x1, waiting for transfers between devices: 6.88 us -> 3.53 us  [body(): returned = lax.psum_scatter(table, Z_AXIS, scatter_dimension=0, tiled=True)]
    all_to_all x10 -> x9, waiting for transfers between devices: 66.3 us -> 63.6 us  [exchange(): return lax.all_to_all(array, axes, split_axis=0, concat_axis=0, tiled=True)]
  transfers between devices with their start and end apart: 18 -> 17, of which waited for: 12 -> 11; matrix products, arithmetic and copies ran while one was open for 10% -> 12% of each run, Pallas kernels for 5% -> 5%
where the time goes in v5:
time: 284 us; the launch traced here: 282 us
  waiting for transfers between devices  73.6 us (26%)
  starting transfers between devices  67.3 us (24%)
  blocking collectives  51 us (18%)
  Pallas kernels  35.3 us (12%)
  other arithmetic  22.9 us (8%)
  between operations  17.1 us (6%)
  local copies, waits for them, and re-layouts  15.1 us (5%)
    all_to_all x9, waiting for transfers between devices, exchange(): return lax.all_to_all(array, axes, split_axis=0, concat_axis=0, tiled=True)  63.6 us
    all_to_all x4, blocking collectives, exchange(): return lax.all_to_all(array, axes, split_axis=0, concat_axis=0, tiled=True)  51 us
    all_to_all x9, starting transfers between devices, exchange(): return lax.all_to_all(array, axes, split_axis=0, concat_axis=0, tiled=True)  50.3 us
    pallas_call x1, Pallas kernels, body(): pl.pallas_call(edge_grads_kernel, out_shape=(jax.ShapeDtypeStruct((cells...  11.5 us
    pallas_call x1, Pallas kernels, body(): pl.pallas_call(own_grads_kernel, out_shape=(jax.ShapeDtypeStruct((tokens,...  9.36 us
    ppermute x3, starting transfers between devices, body(): lax.ppermute(qd_sent, Y_AXIS, pairs)  8.76 us
    pallas_call x1, Pallas kernels, body(): pl.pallas_call(edge_stats_kernel, out_shape=(jax.ShapeDtypeStruct((y_coun...  8.66 us
    ppermute x3, starting transfers between devices, body(): lax.ppermute(half, Y_AXIS, pairs)  8.22 us
  transfers between devices with their start and end apart: 17, of which 11 were waited for; matrix products, arithmetic and copies ran while one was open for 12% of the time, Pallas kernels for 5%

profile of v5, /device:TPU:1, one launch (start us, length us, event | category | flops | bytes accessed | tf_op | source)
XLA Modules:
  0.0 282.4 jit_solution(5678793314375872212)
XLA Ops:
  7.3 1.0 copy-done
  8.2 1.1 copy_bitcast_fusion.2
  9.4 19.2 %all_to_all.65 = bf16[8,128,256]{2,1,0:T(8,128)(2,1)} all-to-all(bf16[8,128,256]{2,1,0:T(8,128)(2,1)S(1)} %maximum_bitcast_fusion), channel_id=1, replica_groups=mesh['ctx_0'=16,'ctx_1'=4,'head'=8] {'head'}, dimensions={0} | all-to-all | bytes 1048576 | tf_op jit(solution)/shard_map/all_to_all | solution.py:60
  28.7 1.3 fusion.40
  30.7 1.0 copy_bitcast_fusion
  32.7 4.4 %all-to-all-start.1 = ((bf16[8,128,256]{2,1,0:T(8,128)(2,1)}), bf16[8,128,256]{2,1,0:T(8,128)(2,1)S(1)}, u32[]{:S(2)}, u32[]{:S(2)}) async-start(bf16[8,128,256]{2,1,0:T(8,128)(2,1)} %maximum_bitcast_fusion.1), calls=%async_computation.1 | async-start | bytes 1048576 | tf_op jit(solution)/shard_map/all_to_all | solution.py:60
  38.1 8.4 %all-to-all-done.1 = bf16[8,128,256]{2,1,0:T(8,128)(2,1)S(1)} async-done(((bf16[8,128,256]{2,1,0:T(8,128)(2,1)}), bf16[8,128,256]{2,1,0:T(8,128)(2,1)S(1)}, u32[]{:S(2)}, u32[]{:S(2)}) %all-to-all-start.1) | async-done | bytes 524320 | tf_op jit(solution)/shard_map/all_to_all | solution.py:60
  47.3 2.3 pick.1
  49.6 3.4 %all-to-all-start.2 = ((bf16[4,48,512]{2,1,0:T(8,128)(2,1)}), bf16[4,48,512]{2,1,0:T(8,128)(2,1)S(1)}, u32[]{:S(2)}, u32[]{:S(2)}) async-start(bf16[4,48,512]{2,1,0:T(8,128)(2,1)} %pick.1), calls=%async_computation.2 | async-start | bytes 393216 | tf_op jit(solution)/shard_map/all_to_all | solution.py:60
  54.3 3.9 %all-to-all-done.2 = bf16[4,48,512]{2,1,0:T(8,128)(2,1)S(1)} async-done(((bf16[4,48,512]{2,1,0:T(8,128)(2,1)}), bf16[4,48,512]{2,1,0:T(8,128)(2,1)S(1)}, u32[]{:S(2)}, u32[]{:S(2)}) %all-to-all-start.2) | async-done | bytes 196640 | tf_op jit(solution)/shard_map/all_to_all | solution.py:60
  58.2 2.5 collective-permute-start
  60.7 3.3 %collective-permute-start.1 = (bf16[1024,256]{1,0:T(8,128)(2,1)}, bf16[1024,256]{1,0:T(8,128)(2,1)S(1)}, u32[]{:S(2)}, u32[]{:S(2)}) collective-permute-start(bf16[1024,256]{1,0:T(8,128)(2,1)} %bitcast.96), channel_id=1, source_target_pairs={{0,16},{8,24},{16,0},{24,8},{1,17},{9,25},{17,1},{25,9},{2,18},{10... | collective-permute-start | bytes 1572872 | tf_op jit(solution)/shard_map/ppermute | solution.py:515
  64.1 2.9 %collective-permute-start.2 = (bf16[1024,256]{1,0:T(8,128)(2,1)}, bf16[1024,256]{1,0:T(8,128)(2,1)S(1)}, u32[]{:S(2)}, u32[]{:S(2)}) collective-permute-start(bf16[1024,256]{1,0:T(8,128)(2,1)} %bitcast.97), channel_id=1, source_target_pairs={{0,24},{8,0},{16,8},{24,16},{1,25},{9,1},{17,9},{25,17},{2,26},{10... | collective-permute-start | bytes 1572872 | tf_op jit(solution)/shard_map/ppermute | solution.py:515
  70.3 11.5 %all-to-all-start.3 = ((bf16[16,2,1,512]{3,1,2,0:T(2,128)(2,1)}), bf16[16,2,1,512]{3,1,2,0:T(2,128)(2,1)S(1)}, u32[]{:S(2)}, u32[]{:S(2)}) async-start(bf16[16,2,1,512]{3,1,2,0:T(2,128)(2,1)} %copy.178), calls=%async_computation.3 | async-start | bytes 65536 | tf_op jit(solution)/shard_map/all_to_all | solution.py:60
  83.6 2.6 fusion.34
  87.5 1.2 fusion.24
  88.7 1.2 fusion.28.row_ref
  90.0 3.8 %all-to-all-done.3 = bf16[16,2,1,512]{3,1,2,0:T(2,128)(2,1)S(1)} async-done(((bf16[16,2,1,512]{3,1,2,0:T(2,128)(2,1)}), bf16[16,2,1,512]{3,1,2,0:T(2,128)(2,1)S(1)}, u32[]{:S(2)}, u32[]{:S(2)}) %all-to-all-start.3) | async-done | bytes 32800 | tf_op jit(solution)/shard_map/all_to_all | solution.py:60
  94.5 7.7 %all-to-all-start.4 = ((bf16[16,2,1,512]{3,1,2,0:T(2,128)(2,1)}), bf16[16,2,1,512]{3,1,2,0:T(2,128)(2,1)S(1)}, u32[]{:S(2)}, u32[]{:S(2)}) async-start(bf16[16,2,1,512]{3,1,2,0:T(2,128)(2,1)} %broadcast_in_dim.237), calls=%async_computation.4 | async-start | bytes 65536 | tf_op jit(solution)/shard_map/all_to_all | solution.py:60
  104.2 9.9 %all-to-all-done.4 = bf16[16,2,1,512]{3,1,2,0:T(2,128)(2,1)S(1)} async-done(((bf16[16,2,1,512]{3,1,2,0:T(2,128)(2,1)}), bf16[16,2,1,512]{3,1,2,0:T(2,128)(2,1)S(1)}, u32[]{:S(2)}, u32[]{:S(2)}) %all-to-all-start.4) | async-done | bytes 32800 | tf_op jit(solution)/shard_map/all_to_all | solution.py:60
  114.8 3.3 %all-to-all-start.5 = ((bf16[4,2,16,512]{3,2,1,0:T(8,128)(2,1)}), bf16[4,2,16,512]{3,2,1,0:T(8,128)(2,1)S(1)}, u32[]{:S(2)}, u32[]{:S(2)}) async-start(bf16[4,2,16,512]{3,2,1,0:T(8,128)(2,1)} %broadcast_in_dim.239), calls=%async_computation.5 | async-start | bytes 262144 | tf_op jit(solution)/shard_map/all_to_all | solution.py:60
  118.2 1.3 pad_add_fusion.1.meta_ref
  119.4 3.5 %all-to-all-done.5 = bf16[4,2,16,512]{3,2,1,0:T(8,128)(2,1)S(1)} async-done(((bf16[4,2,16,512]{3,2,1,0:T(8,128)(2,1)}), bf16[4,2,16,512]{3,2,1,0:T(8,128)(2,1)S(1)}, u32[]{:S(2)}, u32[]{:S(2)}) %all-to-all-start.5) | async-done | bytes 131104 | tf_op jit(solution)/shard_map/all_to_all | solution.py:60
  123.6 3.5 %own_stats.1 = (f32[3,16,64]{2,1,0:T(8,128)}, f32[3,128]{1,0:T(4,128)}) custom-call(f32[32]{0:T(128)} %reshape.387.bias_ref, bf16[1024,256]{1,0:T(8,128)(2,1)} %bitcast.98, bf16[1024,256]{1,0:T(8,128)(2,1)} %bitcast.92, bf16[128,512]{1,0:T(8,128)(2,1)} %bitcast.101), custom_call_target="tpu_custom_call" | custom-call | tf_op jit(solution)/shard_map/own_stats/pallas_call | solution.py:571
  127.1 2.5 pad_maximum_fusion.qd_ref
  129.7 6.4 %all-gather.2.cloned.1.call-done.kv_ref = bf16[16384,256]{1,0:T(8,128)(2,1)} async-done(((bf16[1024,256]{1,0:T(8,128)(2,1)}), bf16[16384,256]{1,0:T(8,128)(2,1)}) %all-gather.2.cloned.1.call-update) | async-done | bytes 8388624 | tf_op jit(solution)/shard_map/all_gather | solution.py:468
  136.1 8.7 %edge_stats.1 = (f32[4,128,128]{2,1,0:T(8,128)}, bf16[16384,256]{1,0:T(8,128)(2,1)}) custom-call(s32[3]{0:T(128)} %pad_add_fusion.1.meta_ref, s32[256]{0:T(256)} %get-tuple-element.62.slot_ref, s32[256]{0:T(256)} %get-tuple-element.60.item_ref, s32[256]{0:T(256)} %copy-done.4, bf16[4096,256]{1,0:T(8,128)(2,1)} %pad_maximum_fusion.qd_ref, ...), custom_call_target="tpu_custom_call" | custom-call | tf_op jit(solution)/shard_map/edge_stats/pallas_call | solution.py:589
  144.7 10.2 %all_to_all.66.parts_ref = f32[4,128,128]{2,1,0:T(8,128)} all-to-all(f32[4,128,128]{2,1,0:T(8,128)} %get-tuple-element.43), channel_id=1, replica_groups=mesh['ctx_0'=16,'ctx_1'=4,'head'=8] {'ctx_1'}, dimensions={0} | all-to-all | bytes 524288 | tf_op jit(solution)/shard_map/all_to_all | solution.py:60
  154.9 11.5 %edge_grads.1 = (bf16[16384,256]{1,0:T(8,128)(2,1)}, f32[3,72,128]{2,1,0:T(8,128)}, f32[1024,256]{1,0:T(8,128)}, bf16[1024,256]{1,0:T(8,128)(2,1)}, bf16[1024,25...) custom-call(s32[3]{0:T(128)} %pad_add_fusion.1.meta_ref, s32[256]{0:T(256)} %fusion.28.row_ref, ...), custom_call_target="tpu_custom_call", output_to_operand_aliasing={{0}: (11, {})} | custom-call | tf_op jit(solution)/shard_map/edge_grads/pallas_call | solution.py:606
  167.7 9.8 %all-to-all-start.7 = ((f32[16,3,128]{2,1,0:T(4,128)}), f32[16,3,128]{2,1,0:T(4,128)S(1)}, u32[]{:S(2)}, u32[]{:S(2)}) async-start(f32[16,3,128]{2,1,0:T(4,128)} %broadcast_in_dim.243), calls=%async_computation.7 | async-start | bytes 65536 | tf_op jit(solution)/shard_map/all_to_all | solution.py:60
  177.6 11.5 %all-to-all-done.7 = f32[16,3,128]{2,1,0:T(4,128)S(1)} async-done(((f32[16,3,128]{2,1,0:T(4,128)}), f32[16,3,128]{2,1,0:T(4,128)S(1)}, u32[]{:S(2)}, u32[]{:S(2)}) %all-to-all-start.7) | async-done | bytes 24608 | tf_op jit(solution)/shard_map/all_to_all | solution.py:60
  189.8 3.3 %all-to-all-start.8 = ((f32[4,16,3,128]{3,1,2,0:T(8,128)}), f32[4,16,3,128]{3,1,2,0:T(8,128)S(1)}, u32[]{:S(2)}, u32[]{:S(2)}) async-start(f32[4,16,3,128]{3,1,2,0:T(8,128)} %broadcast_in_dim.244), calls=%async_computation.8 | async-start | bytes 196608 | tf_op jit(solution)/shard_map/all_to_all | solution.py:60
  193.7 4.1 %all-to-all-done.8 = f32[4,16,3,128]{3,1,2,0:T(8,128)S(1)} async-done(((f32[4,16,3,128]{3,1,2,0:T(8,128)}), f32[4,16,3,128]{3,1,2,0:T(8,128)S(1)}, u32[]{:S(2)}, u32[]{:S(2)}) %all-to-all-start.8) | async-done | bytes 98336 | tf_op jit(solution)/shard_map/all_to_all | solution.py:60
  198.4 9.4 %own_grads.1 = (f32[1024,256]{1,0:T(8,128)}, f32[1024,256]{1,0:T(8,128)}, f32[256,256]{1,0:T(8,128)}) custom-call(s32[3]{0:T(128)} %pad_add_fusion.1.meta_ref, f32[32]{0:T(128)} %reshape.387.bias_ref, f32[16]{0:T(128)} %broadcast_select_fusion.1.flag_ref, bf16[1024,256]{1,0:T(8,128)(2,1)} %bitcast.100, bf16[1024,256]{1,0:T(8,128)(2,1)} %bitcast.93, ...), custom_call_target="tpu_custom_call" | custom-call | tf_op jit(solution)/shard_map/own_grads/pallas_call | solution.py:631
  207.8 1.1 convert_element_type.99
  208.9 7.2 %all_to_all.67 = bf16[4,64,256]{2,1,0:T(8,128)(2,1)S(1)} all-to-all(bf16[4,64,256]{2,1,0:T(8,128)(2,1)S(1)} %bitcast.105), channel_id=1, replica_groups=mesh['ctx_0'=16,'ctx_1'=4,'head'=8] {'ctx_1'}, dimensions={0} | all-to-all | bytes 262144 | tf_op jit(solution)/shard_map/all_to_all | solution.py:60
  216.1 14.4 %all_to_all.68 = bf16[16,4,256]{2,1,0:T(4,128)(2,1)S(1)} all-to-all(bf16[16,4,256]{2,1,0:T(4,128)(2,1)S(1)} %reshape.393), channel_id=1, replica_groups=mesh['ctx_0'=16,'ctx_1'=4,'head'=8] {'ctx_0'}, dimensions={0} | all-to-all | bytes 65536 | tf_op jit(solution)/shard_map/all_to_all | solution.py:60
  231.2 3.5 %all-to-all-start.11 = ((bf16[16,4,256]{2,1,0:T(4,128)(2,1)}), bf16[16,4,256]{2,1,0:T(4,128)(2,1)S(1)}, u32[]{:S(2)}, u32[]{:S(2)}) async-start(bf16[16,4,256]{2,1,0:T(4,128)(2,1)} %broadcast_in_dim.245), calls=%async_computation.11 | async-start | bytes 65536 | tf_op jit(solution)/shard_map/all_to_all | solution.py:60
  234.7 2.8 collective-permute-start.3
  237.5 3.5 %collective-permute-start.4 = (bf16[1024,256]{1,0:T(8,128)(2,1)}, bf16[1024,256]{1,0:T(8,128)(2,1)S(1)}, u32[]{:S(2)}, u32[]{:S(2)}) collective-permute-start(bf16[1024,256]{1,0:T(8,128)(2,1)} %get-tuple-element.51), channel_id=1, source_target_pairs={{0,16},{8,24},{16,0},{24,8},{1,17},{9,25},{17,1},{25,9},{2,18},{10... | collective-permute-start | bytes 1572872 | tf_op jit(solution)/shard_map/ppermute | solution.py:628
  241.0 1.9 collective-permute-start.5
  243.0 3.6 %all-to-all-done.11 = bf16[16,4,256]{2,1,0:T(4,128)(2,1)S(1)} async-done(((bf16[16,4,256]{2,1,0:T(4,128)(2,1)}), bf16[16,4,256]{2,1,0:T(4,128)(2,1)S(1)}, u32[]{:S(2)}, u32[]{:S(2)}) %all-to-all-start.11) | async-done | bytes 32800 | tf_op jit(solution)/shard_map/all_to_all | solution.py:60
  247.2 3.3 %all-to-all-start.12 = ((bf16[4,64,256]{2,1,0:T(8,128)(2,1)}), bf16[4,64,256]{2,1,0:T(8,128)(2,1)S(1)}, u32[]{:S(2)}, u32[]{:S(2)}) async-start(bf16[4,64,256]{2,1,0:T(8,128)(2,1)} %broadcast_in_dim.247), calls=%async_computation.12 | async-start | bytes 262144 | tf_op jit(solution)/shard_map/all_to_all | solution.py:60
  250.9 14.9 %all-to-all-done.12 = bf16[4,64,256]{2,1,0:T(8,128)(2,1)S(1)} async-done(((bf16[4,64,256]{2,1,0:T(8,128)(2,1)}), bf16[4,64,256]{2,1,0:T(8,128)(2,1)S(1)}, u32[]{:S(2)}, u32[]{:S(2)}) %all-to-all-start.12) | async-done | bytes 131104 | tf_op jit(solution)/shard_map/all_to_all | solution.py:60
  265.9 1.6 fusion
  267.5 1.8 fusion.3
  270.1 3.5 %reduce-scatter.2.cloned.1.call-done = bf16[1024,256]{1,0:T(8,128)(2,1)} async-done(((bf16[16384,256]{1,0:T(8,128)(2,1)}), bf16[1024,256]{1,0:T(8,128)(2,1)}) %reduce-scatter.2.cloned.1.call-update) | async-done | bytes 524304 | tf_op jit(solution)/shard_map/reduce_scatter | solution.py:627
  273.6 1.9 add_convert_fusion
  (104 shorter events, 18.7 us)
Async XLA Ops:
  7.2 1.1 copy-start
  7.2 30.0 %copy-start.8 = (s32[16,1,3]{0,1,2:T(1,128)S(1)}, s32[16,1,3]{0,1,2:T(1,128)}, u32[]{:S(2)}) copy-start(s32[16,1,3]{0,1,2:T(1,128)} %param.10) | copy-start | bytes 580
  7.2 24.5 %copy-start.3 = (bf16[128,1024]{1,0:T(8,128)(2,1)S(1)}, bf16[128,1024]{1,0:T(8,128)(2,1)}, u32[]{:S(2)}) copy-start(bf16[128,1024]{1,0:T(8,128)(2,1)} %param.6) | copy-start | bytes 786436
  7.2 29.9 %copy-start.5 = (s32[2]{0:T(128)S(1)}, s32[2]{0:T(128)}, u32[]{:S(2)}) copy-start(s32[2]{0:T(128)} %index_ref.1) | copy-start | bytes 28
  7.2 128.9 %all-gather.2.cloned.1.call-start = ((), (), s32[]{:S(2)}) async-start(), calls=%async_computation.14 | async-start | bytes 8912896 | tf_op jit(solution)/shard_map/all_gather | solution.py:468
  9.3 58.0 %copy-start.6 = (s32[2]{0:T(128)S(1)}, s32[2]{0:T(128)}, u32[]{:S(2)}) copy-start(s32[2]{0:T(128)} %index_ref.1) | copy-start | bytes 28
  32.7 13.8 %all-to-all-start.1 = ((bf16[8,128,256]{2,1,0:T(8,128)(2,1)}), bf16[8,128,256]{2,1,0:T(8,128)(2,1)S(1)}, u32[]{:S(2)}, u32[]{:S(2)}) async-start(bf16[8,128,256]{2,1,0:T(8,128)(2,1)} %maximum_bitcast_fusion.1), calls=%async_computation.1 | async-start | bytes 1048576 | tf_op jit(solution)/shard_map/all_to_all | solution.py:60
  46.5 0.8 copy-start.1
  49.6 8.6 %all-to-all-start.2 = ((bf16[4,48,512]{2,1,0:T(8,128)(2,1)}), bf16[4,48,512]{2,1,0:T(8,128)(2,1)S(1)}, u32[]{:S(2)}, u32[]{:S(2)}) async-start(bf16[4,48,512]{2,1,0:T(8,128)(2,1)} %pick.1), calls=%async_computation.2 | async-start | bytes 393216 | tf_op jit(solution)/shard_map/all_to_all | solution.py:60
  58.2 69.0 %collective-permute-start = (bf16[1024,256]{1,0:T(8,128)(2,1)}, bf16[1024,256]{1,0:T(8,128)(2,1)S(1)}, u32[]{:S(2)}, u32[]{:S(2)}) collective-permute-start(bf16[1024,256]{1,0:T(8,128)(2,1)} %bitcast.95), channel_id=1, source_target_pairs={{0,8},{8,16},{16,24},{24,0},{1,9},{9,17},{17,25},{25,1},{2,10},{10... | collective-permute-start | bytes 1572872 | tf_op jit(solution)/shard_map/ppermute | solution.py:515
  60.7 66.4 %collective-permute-start.1 = (bf16[1024,256]{1,0:T(8,128)(2,1)}, bf16[1024,256]{1,0:T(8,128)(2,1)S(1)}, u32[]{:S(2)}, u32[]{:S(2)}) collective-permute-start(bf16[1024,256]{1,0:T(8,128)(2,1)} %bitcast.96), channel_id=1, source_target_pairs={{0,16},{8,24},{16,0},{24,8},{1,17},{9,25},{17,1},{25,9},{2,18},{10... | collective-permute-start | bytes 1572872 | tf_op jit(solution)/shard_map/ppermute | solution.py:515
  64.1 63.1 %collective-permute-start.2 = (bf16[1024,256]{1,0:T(8,128)(2,1)}, bf16[1024,256]{1,0:T(8,128)(2,1)S(1)}, u32[]{:S(2)}, u32[]{:S(2)}) collective-permute-start(bf16[1024,256]{1,0:T(8,128)(2,1)} %bitcast.97), channel_id=1, source_target_pairs={{0,24},{8,0},{16,8},{24,16},{1,25},{9,1},{17,9},{25,17},{2,26},{10... | collective-permute-start | bytes 1572872 | tf_op jit(solution)/shard_map/ppermute | solution.py:515
  70.3 23.5 %all-to-all-start.3 = ((bf16[16,2,1,512]{3,1,2,0:T(2,128)(2,1)}), bf16[16,2,1,512]{3,1,2,0:T(2,128)(2,1)S(1)}, u32[]{:S(2)}, u32[]{:S(2)}) async-start(bf16[16,2,1,512]{3,1,2,0:T(2,128)(2,1)} %copy.178), calls=%async_computation.3 | async-start | bytes 65536 | tf_op jit(solution)/shard_map/all_to_all | solution.py:60
  82.9 53.2 %copy-start.4 = (s32[256]{0:T(256)}, s32[256]{0:T(256)S(1)}, u32[]{:S(2)}) copy-start(s32[256]{0:T(256)S(1)} %get-tuple-element.57.cell_ref) | copy-start | bytes 3076
  94.5 19.6 %all-to-all-start.4 = ((bf16[16,2,1,512]{3,1,2,0:T(2,128)(2,1)}), bf16[16,2,1,512]{3,1,2,0:T(2,128)(2,1)S(1)}, u32[]{:S(2)}, u32[]{:S(2)}) async-start(bf16[16,2,1,512]{3,1,2,0:T(2,128)(2,1)} %broadcast_in_dim.237), calls=%async_computation.4 | async-start | bytes 65536 | tf_op jit(solution)/shard_map/all_to_all | solution.py:60
  114.8 8.2 %all-to-all-start.5 = ((bf16[4,2,16,512]{3,2,1,0:T(8,128)(2,1)}), bf16[4,2,16,512]{3,2,1,0:T(8,128)(2,1)S(1)}, u32[]{:S(2)}, u32[]{:S(2)}) async-start(bf16[4,2,16,512]{3,2,1,0:T(8,128)(2,1)} %broadcast_in_dim.239), calls=%async_computation.5 | async-start | bytes 262144 | tf_op jit(solution)/shard_map/all_to_all | solution.py:60
  118.1 155.5 %reduce-scatter.2.cloned.1.call-start = ((), (), s32[]{:S(2)}) async-start(), calls=%async_computation.15 | async-start | bytes 8912896 | tf_op jit(solution)/shard_map/reduce_scatter | solution.py:627
  166.4 0.7 copy-start.7
  167.7 21.4 %all-to-all-start.7 = ((f32[16,3,128]{2,1,0:T(4,128)}), f32[16,3,128]{2,1,0:T(4,128)S(1)}, u32[]{:S(2)}, u32[]{:S(2)}) async-start(f32[16,3,128]{2,1,0:T(4,128)} %broadcast_in_dim.243), calls=%async_computation.7 | async-start | bytes 65536 | tf_op jit(solution)/shard_map/all_to_all | solution.py:60
  189.8 7.9 %all-to-all-start.8 = ((f32[4,16,3,128]{3,1,2,0:T(8,128)}), f32[4,16,3,128]{3,1,2,0:T(8,128)S(1)}, u32[]{:S(2)}, u32[]{:S(2)}) async-start(f32[4,16,3,128]{3,1,2,0:T(8,128)} %broadcast_in_dim.244), calls=%async_computation.8 | async-start | bytes 196608 | tf_op jit(solution)/shard_map/all_to_all | solution.py:60
  207.8 59.7 %copy-start.2 = (f32[1024,256]{1,0:T(8,128)S(1)}, f32[1024,256]{1,0:T(8,128)}, u32[]{:S(2)}) copy-start(f32[1024,256]{1,0:T(8,128)} %get-tuple-element.49) | copy-start | bytes 3145732
  231.2 15.3 %all-to-all-start.11 = ((bf16[16,4,256]{2,1,0:T(4,128)(2,1)}), bf16[16,4,256]{2,1,0:T(4,128)(2,1)S(1)}, u32[]{:S(2)}, u32[]{:S(2)}) async-start(bf16[16,4,256]{2,1,0:T(4,128)(2,1)} %broadcast_in_dim.245), calls=%async_computation.11 | async-start | bytes 65536 | tf_op jit(solution)/shard_map/all_to_all | solution.py:60
  234.7 32.8 %collective-permute-start.3 = (bf16[1024,256]{1,0:T(8,128)(2,1)}, bf16[1024,256]{1,0:T(8,128)(2,1)S(1)}, u32[]{:S(2)}, u32[]{:S(2)}) collective-permute-start(bf16[1024,256]{1,0:T(8,128)(2,1)} %get-tuple-element.50), channel_id=1, source_target_pairs={{0,24},{8,0},{16,8},{24,16},{1,25},{9,1},{17,9},{25,17},{2,26},{10... | collective-permute-start | bytes 1572872 | tf_op jit(solution)/shard_map/ppermute | solution.py:628
  237.5 30.0 %collective-permute-start.4 = (bf16[1024,256]{1,0:T(8,128)(2,1)}, bf16[1024,256]{1,0:T(8,128)(2,1)S(1)}, u32[]{:S(2)}, u32[]{:S(2)}) collective-permute-start(bf16[1024,256]{1,0:T(8,128)(2,1)} %get-tuple-element.51), channel_id=1, source_target_pairs={{0,16},{8,24},{16,0},{24,8},{1,17},{9,25},{17,1},{25,9},{2,18},{10... | collective-permute-start | bytes 1572872 | tf_op jit(solution)/shard_map/ppermute | solution.py:628
  241.0 26.5 %collective-permute-start.5 = (bf16[1024,256]{1,0:T(8,128)(2,1)}, bf16[1024,256]{1,0:T(8,128)(2,1)}, u32[]{:S(2)}, u32[]{:S(2)}) collective-permute-start(bf16[1024,256]{1,0:T(8,128)(2,1)} %get-tuple-element.52), channel_id=1, source_target_pairs={{0,8},{8,16},{16,24},{24,0},{1,9},{9,17},{17,25},{25,1},{2,10},{10... | collective-permute-start | bytes 1572872 | tf_op jit(solution)/shard_map/ppermute | solution.py:628
  247.2 18.6 %all-to-all-start.12 = ((bf16[4,64,256]{2,1,0:T(8,128)(2,1)}), bf16[4,64,256]{2,1,0:T(8,128)(2,1)S(1)}, u32[]{:S(2)}, u32[]{:S(2)}) async-start(bf16[4,64,256]{2,1,0:T(8,128)(2,1)} %broadcast_in_dim.247), calls=%async_computation.12 | async-start | bytes 262144 | tf_op jit(solution)/shard_map/all_to_all | solution.py:60
Sparse Core Ops, SparseCore 0:
  28.8 107.2 all-gather.1
  166.6 107.0 reduce-scatter.1

commit v6 on v5

--- a/solution.py
+++ b/solution.py
@@ -136,7 +136,17 @@
             out_ref[lane, g * part : (g + 1) * part, :] = rows_ref[low : low + part, :]
 
 
-def own_stats_kernel(bias_ref, qd_ref, kv_ref, shared_ref, own_ref, rows_ref):
+def own_stats_kernel(
+    bias_ref, qd_ref, kv_ref, shared_ref, own_ref, rows_ref, table_ref, zero_ref, zero_sems
+):
+    size = zero_ref.shape[0]
+    zero_ref[...] = jnp.zeros(zero_ref.shape, jnp.bfloat16)
+    clears = [
+        pltpu.make_async_copy(zero_ref, table_ref.at[pl.ds(i * size, size), :], zero_sems.at[i])
+        for i in range(table_ref.shape[0] // size)
+    ]
+    for clear in clears:
+        clear.start()
     tokens = qd_ref.shape[0]
     blocks = tokens // S
     for i in range(blocks):
@@ -158,6 +168,8 @@
     rows_ref[0:1, :] = top
     rows_ref[1:2, :] = total
     rows_ref[2:3, :] = slope
+    for clear in clears:
+        clear.wait()
 
 
 def cell_fetcher(meta_ref, cell_ref, kv_ref, fetch_ref, fetch_sems):
@@ -202,28 +214,17 @@
     kv_ref,
     own_ref,
     out_ref,
-    table_ref,
     top_ref,
     total_ref,
     slope_ref,
-    zero_ref,
     fetch_ref,
     fetch_sems,
-    zero_sems,
 ):
     group = qd_ref.shape[0] // S
     blocks = own_ref.shape[1]
     start, wait = cell_fetcher(meta_ref, cell_ref, kv_ref, fetch_ref, fetch_sems)
     for t in range(DEPTH):
         start(t)
-    rows = zero_ref.shape[0]
-    zero_ref[...] = jnp.zeros(zero_ref.shape, jnp.bfloat16)
-    clears = [
-        pltpu.make_async_copy(zero_ref, table_ref.at[pl.ds(i * rows, rows), :], zero_sems.at[i])
-        for i in range(table_ref.shape[0] // rows)
-    ]
-    for clear in clears:
-        clear.start()
     top_ref[...] = jnp.full(top_ref.shape, NEG, jnp.float32)
     total_ref[...] = jnp.zeros(total_ref.shape, jnp.float32)
     slope_ref[...] = jnp.zeros(slope_ref.shape, jnp.float32)
@@ -269,8 +270,6 @@
     for lane in range(out_ref.shape[0]):
         out_ref[lane, :group, :] = first
         out_ref[lane, group:, :] = second
-    for clear in clears:
-        clear.wait()
 
 
 def edge_grads_kernel(
@@ -505,15 +504,15 @@
     picked = chosen(arrived, owners % y_count)
     sent = picked.reshape(WORLDWIDE_COUNT, z_count, -1, 4 * D).transpose(1, 0, 2, 3)
     picked = chosen(exchange(sent, Z_AXIS), owners // y_count)
-    shared = to_all(picked, Z_AXIS).transpose(1, 0, 2, 3).reshape(WORLDWIDE_COUNT, part, 4 * D)
-    shared = to_all(shared, Y_AXIS).transpose(1, 0, 2, 3).reshape(G, 4 * D)
-
     shifts = range(1, y_count)
     forward = [[(i, (i + shift) % y_count) for i in range(y_count)] for shift in shifts]
     backward = [[(i, (i - shift) % y_count) for i in range(y_count)] for shift in shifts]
     qd_group = jnp.concatenate(
         [qd] + [lax.ppermute(qd_sent, Y_AXIS, pairs) for pairs in forward], 0
     )
+    gathered, qd_group = lax.optimization_barrier((to_all(picked, Z_AXIS), qd_group))
+    shared = gathered.transpose(1, 0, 2, 3).reshape(WORLDWIDE_COUNT, part, 4 * D)
+    shared = to_all(shared, Y_AXIS).transpose(1, 0, 2, 3).reshape(G, 4 * D)
 
     ids = z_place * group + jnp.arange(group, dtype=jnp.int32)
     local = jnp.arange(group, dtype=jnp.int32) % block_count
@@ -568,14 +567,19 @@
     hits = own_ids[:, None] == universal_segment_indices[None]
     flags = jnp.where(jnp.any(hits, 1), 0.0, 1.0).astype(f32)
 
-    own, rows = pl.pallas_call(
+    own, rows, cleared = pl.pallas_call(
         own_stats_kernel,
         out_shape=(
             jax.ShapeDtypeStruct((3, block_count, S), f32),
             jax.ShapeDtypeStruct((3, G), f32),
+            jax.ShapeDtypeStruct((cells * S, 2 * D), jnp.bfloat16),
         ),
         in_specs=[SMEM, VMEM, VMEM, VMEM],
-        out_specs=(VMEM, VMEM),
+        out_specs=(VMEM, VMEM, ANY),
+        scratch_shapes=[
+            pltpu.VMEM((tokens, 2 * D), jnp.bfloat16),
+            pltpu.SemaphoreType.DMA((z_count,)),
+        ],
         compiler_params=PARAMS,
         name="own_stats",
     )(bias, qd, kv, shared)
@@ -586,18 +590,12 @@
         pltpu.VMEM((DEPTH, UNROLL * S, 2 * D), jnp.bfloat16),
         pltpu.SemaphoreType.DMA((DEPTH,)),
     ]
-    stats, cleared = pl.pallas_call(
+    stats = pl.pallas_call(
         edge_stats_kernel,
-        out_shape=(
-            jax.ShapeDtypeStruct((y_count, 2 * group, 2 * S), f32),
-            jax.ShapeDtypeStruct((cells * S, 2 * D), jnp.bfloat16),
-        ),
+        out_shape=jax.ShapeDtypeStruct((y_count, 2 * group, 2 * S), f32),
         in_specs=[SMEM] * 4 + [VMEM, ANY, VMEM],
-        out_specs=(VMEM, ANY),
-        scratch_shapes=[pltpu.VMEM((stat_rows, 2 * S), f32)] * 3
-        + [pltpu.VMEM((tokens, 2 * D), jnp.bfloat16)]
-        + fetch_scratch
-        + [pltpu.SemaphoreType.DMA((z_count,))],
+        out_specs=VMEM,
+        scratch_shapes=[pltpu.VMEM((stat_rows, 2 * S), f32)] * 3 + fetch_scratch,
         compiler_params=PARAMS,
         name="edge_stats",
     )(*lists, qd_group, kv_all, own)

time: 284 us -> 283 us (level)
  waiting for transfers between devices: 73.6 us -> 66.6 us
  starting transfers between devices: 67.3 us -> 71.7 us
    all_to_all x9, waiting for transfers between devices: 63.6 us -> 58.7 us  [exchange(): return lax.all_to_all(array, axes, split_axis=0, concat_axis=0, tiled=True)]
    all_to_all x9, starting transfers between devices: 50.3 us -> 54.5 us  [exchange(): return lax.all_to_all(array, axes, split_axis=0, concat_axis=0, tiled=True)]
    pallas_call x1, Pallas kernels: 3.47 us -> 6.88 us  [body(): pl.pallas_call(own_stats_kernel, out_shape=(jax.ShapeDtypeStruct((3, bloc...]
    all_gather x1, waiting for transfers between devices: 6.42 us -> 3.55 us  [body(): kv_all = lax.all_gather(kv, Z_AXIS, axis=0, tiled=True)]
  transfers between devices with their start and end apart: 17 -> 17, of which waited for: 11 -> 10; matrix products, arithmetic and copies ran while one was open for 12% -> 12% of each run, Pallas kernels for 5% -> 7%
where the time goes in v6:
time: 283 us; the launch traced here: 280 us
  starting transfers between devices  71.7 us (25%)
  waiting for transfers between devices  66.6 us (24%)
  blocking collectives  50.8 us (18%)
  Pallas kernels  36.2 us (13%)
  other arithmetic  22.9 us (8%)
  between operations  17.2 us (6%)
  local copies, waits for them, and re-layouts  15.1 us (5%)
    all_to_all x9, waiting for transfers between devices, exchange(): return lax.all_to_all(array, axes, split_axis=0, concat_axis=0, tiled=True)  58.7 us
    all_to_all x9, starting transfers between devices, exchange(): return lax.all_to_all(array, axes, split_axis=0, concat_axis=0, tiled=True)  54.5 us
    all_to_all x4, blocking collectives, exchange(): return lax.all_to_all(array, axes, split_axis=0, concat_axis=0, tiled=True)  50.8 us
    pallas_call x1, Pallas kernels, body(): pl.pallas_call(edge_grads_kernel, out_shape=(jax.ShapeDtypeStruct((cells...  11.5 us
    pallas_call x1, Pallas kernels, body(): pl.pallas_call(own_grads_kernel, out_shape=(jax.ShapeDtypeStruct((tokens,...  9.34 us
    ppermute x3, starting transfers between devices, body(): lax.ppermute(qd_sent, Y_AXIS, pairs)  8.76 us
    ppermute x3, starting transfers between devices, body(): lax.ppermute(half, Y_AXIS, pairs)  8.37 us
    pallas_call x1, Pallas kernels, body(): pl.pallas_call(own_stats_kernel, out_shape=(jax.ShapeDtypeStruct((3, bloc...  6.88 us
  transfers between devices with their start and end apart: 17, of which 10 were waited for; matrix products, arithmetic and copies ran while one was open for 12% of the time, Pallas kernels for 7%

profile of v6, /device:TPU:1, one launch (start us, length us, event | category | flops | bytes accessed | tf_op | source)
XLA Modules:
  0.0 280.5 jit_solution(11695554289849007975)
XLA Ops:
  7.3 1.0 copy-done
  8.2 1.1 copy_bitcast_fusion.2
  9.4 19.2 %all_to_all.65 = bf16[8,128,256]{2,1,0:T(8,128)(2,1)} all-to-all(bf16[8,128,256]{2,1,0:T(8,128)(2,1)S(1)} %maximum_bitcast_fusion), channel_id=1, replica_groups=mesh['ctx_0'=16,'ctx_1'=4,'head'=8] {'head'}, dimensions={0} | all-to-all | bytes 1048576 | tf_op jit(solution)/shard_map/all_to_all | solution.py:60
  28.7 1.3 fusion.40
  30.7 1.0 copy_bitcast_fusion
  31.8 0.9 maximum_bitcast_fusion.1
  32.7 4.4 %all-to-all-start.1 = ((bf16[8,128,256]{2,1,0:T(8,128)(2,1)}), bf16[8,128,256]{2,1,0:T(8,128)(2,1)S(1)}, u32[]{:S(2)}, u32[]{:S(2)}) async-start(bf16[8,128,256]{2,1,0:T(8,128)(2,1)} %maximum_bitcast_fusion.1), calls=%async_computation.1 | async-start | bytes 1048576 | tf_op jit(solution)/shard_map/all_to_all | solution.py:60
  38.1 8.4 %all-to-all-done.1 = bf16[8,128,256]{2,1,0:T(8,128)(2,1)S(1)} async-done(((bf16[8,128,256]{2,1,0:T(8,128)(2,1)}), bf16[8,128,256]{2,1,0:T(8,128)(2,1)S(1)}, u32[]{:S(2)}, u32[]{:S(2)}) %all-to-all-start.1) | async-done | bytes 524320 | tf_op jit(solution)/shard_map/all_to_all | solution.py:60
  47.3 2.3 pick.1
  49.6 3.4 %all-to-all-start.2 = ((bf16[4,48,512]{2,1,0:T(8,128)(2,1)}), bf16[4,48,512]{2,1,0:T(8,128)(2,1)S(1)}, u32[]{:S(2)}, u32[]{:S(2)}) async-start(bf16[4,48,512]{2,1,0:T(8,128)(2,1)} %pick.1), calls=%async_computation.2 | async-start | bytes 393216 | tf_op jit(solution)/shard_map/all_to_all | solution.py:60
  54.3 3.9 %all-to-all-done.2 = bf16[4,48,512]{2,1,0:T(8,128)(2,1)S(1)} async-done(((bf16[4,48,512]{2,1,0:T(8,128)(2,1)}), bf16[4,48,512]{2,1,0:T(8,128)(2,1)S(1)}, u32[]{:S(2)}, u32[]{:S(2)}) %all-to-all-start.2) | async-done | bytes 196640 | tf_op jit(solution)/shard_map/all_to_all | solution.py:60
  58.2 2.5 collective-permute-start
  60.7 3.3 %collective-permute-start.1 = (bf16[1024,256]{1,0:T(8,128)(2,1)}, bf16[1024,256]{1,0:T(8,128)(2,1)S(1)}, u32[]{:S(2)}, u32[]{:S(2)}) collective-permute-start(bf16[1024,256]{1,0:T(8,128)(2,1)} %bitcast.96), channel_id=1, source_target_pairs={{0,16},{8,24},{16,0},{24,8},{1,17},{9,25},{17,1},{25,9},{2,18},{10... | collective-permute-start | bytes 1572872 | tf_op jit(solution)/shard_map/ppermute | solution.py:511
  64.1 2.9 %collective-permute-start.2 = (bf16[1024,256]{1,0:T(8,128)(2,1)}, bf16[1024,256]{1,0:T(8,128)(2,1)S(1)}, u32[]{:S(2)}, u32[]{:S(2)}) collective-permute-start(bf16[1024,256]{1,0:T(8,128)(2,1)} %bitcast.97), channel_id=1, source_target_pairs={{0,24},{8,0},{16,8},{24,16},{1,25},{9,1},{17,9},{25,17},{2,26},{10... | collective-permute-start | bytes 1572872 | tf_op jit(solution)/shard_map/ppermute | solution.py:511
  68.0 11.5 %all-to-all-start.3 = ((bf16[16,2,1,512]{3,1,2,0:T(2,128)(2,1)}), bf16[16,2,1,512]{3,1,2,0:T(2,128)(2,1)S(1)}, u32[]{:S(2)}, u32[]{:S(2)}) async-start(bf16[16,2,1,512]{3,1,2,0:T(2,128)(2,1)} %copy.178), calls=%async_computation.3 | async-start | bytes 65536 | tf_op jit(solution)/shard_map/all_to_all | solution.py:60
  83.7 2.6 fusion.34
  87.6 1.2 fusion.24
  88.8 1.2 fusion.28.row_ref
  92.8 11.5 %all-to-all-start.4 = ((bf16[16,2,1,512]{3,1,2,0:T(2,128)(2,1)}), bf16[16,2,1,512]{3,1,2,0:T(2,128)(2,1)S(1)}, u32[]{:S(2)}, u32[]{:S(2)}) async-start(bf16[16,2,1,512]{3,1,2,0:T(2,128)(2,1)} %broadcast_in_dim.237), calls=%async_computation.4 | async-start | bytes 65536 | tf_op jit(solution)/shard_map/all_to_all | solution.py:60
  104.3 2.5 pad_maximum_fusion.qd_ref
  106.8 9.4 %all-to-all-done.4 = bf16[16,2,1,512]{3,1,2,0:T(2,128)(2,1)S(1)} async-done(((bf16[16,2,1,512]{3,1,2,0:T(2,128)(2,1)}), bf16[16,2,1,512]{3,1,2,0:T(2,128)(2,1)S(1)}, u32[]{:S(2)}, u32[]{:S(2)}) %all-to-all-start.4) | async-done | bytes 32800 | tf_op jit(solution)/shard_map/all_to_all | solution.py:60
  116.8 3.3 %all-to-all-start.5 = ((bf16[4,2,16,512]{3,2,1,0:T(8,128)(2,1)}), bf16[4,2,16,512]{3,2,1,0:T(8,128)(2,1)S(1)}, u32[]{:S(2)}, u32[]{:S(2)}) async-start(bf16[4,2,16,512]{3,2,1,0:T(8,128)(2,1)} %broadcast_in_dim.239), calls=%async_computation.5 | async-start | bytes 262144 | tf_op jit(solution)/shard_map/all_to_all | solution.py:60
  120.2 1.3 pad_add_fusion.1.meta_ref
  121.4 3.5 %all-to-all-done.5 = bf16[4,2,16,512]{3,2,1,0:T(8,128)(2,1)S(1)} async-done(((bf16[4,2,16,512]{3,2,1,0:T(8,128)(2,1)}), bf16[4,2,16,512]{3,2,1,0:T(8,128)(2,1)S(1)}, u32[]{:S(2)}, u32[]{:S(2)}) %all-to-all-start.5) | async-done | bytes 131104 | tf_op jit(solution)/shard_map/all_to_all | solution.py:60
  125.6 6.9 %own_stats.1 = (f32[3,16,64]{2,1,0:T(8,128)}, f32[3,128]{1,0:T(4,128)}, bf16[16384,256]{1,0:T(8,128)(2,1)}) custom-call(f32[32]{0:T(128)} %reshape.387.bias_ref, bf16[1024,256]{1,0:T(8,128)(2,1)} %bitcast.99, bf16[1024,256]{1,0:T(8,128)(2,1)} %bitcast.92, bf16[128,512]{1,0:T(8,128)(2,1)} %bitcast.101), custom_call_target="tpu_custom_call" | custom-call | tf_op jit(solution)/shard_map/own_stats/pallas_call | solution.py:570
  132.5 3.5 %all-gather.2.cloned.1.call-done.kv_ref = bf16[16384,256]{1,0:T(8,128)(2,1)} async-done(((bf16[1024,256]{1,0:T(8,128)(2,1)}), bf16[16384,256]{1,0:T(8,128)(2,1)}) %all-gather.2.cloned.1.call-update) | async-done | bytes 8388624 | tf_op jit(solution)/shard_map/all_gather | solution.py:467
  136.1 6.2 %edge_stats.1 = f32[4,128,128]{2,1,0:T(8,128)} custom-call(s32[3]{0:T(128)} %pad_add_fusion.1.meta_ref, s32[256]{0:T(256)} %get-tuple-element.64.slot_ref, s32[256]{0:T(256)} %get-tuple-element.62.item_ref, s32[256]{0:T(256)} %copy-done.4, bf16[4096,256]{1,0:T(8,128)(2,1)} %pad_maximum_fusion.qd_ref, bf16[16384,256]{1,0:T(8,128)(2,1)} %all-gather.2.cloned.1.call-done.kv_ref, ...), custom_call_target="tpu_custom_call" | custom-call | tf_op jit(solution)/shard_map/edge_stats/pallas_call | solution.py:593
  142.3 10.0 %all_to_all.66.parts_ref = f32[4,128,128]{2,1,0:T(8,128)} all-to-all(f32[4,128,128]{2,1,0:T(8,128)} %edge_stats.1), channel_id=1, replica_groups=mesh['ctx_0'=16,'ctx_1'=4,'head'=8] {'ctx_1'}, dimensions={0} | all-to-all | bytes 524288 | tf_op jit(solution)/shard_map/all_to_all | solution.py:60
  152.2 11.5 %edge_grads.1 = (bf16[16384,256]{1,0:T(8,128)(2,1)}, f32[3,72,128]{2,1,0:T(8,128)}, f32[1024,256]{1,0:T(8,128)}, bf16[1024,256]{1,0:T(8,128)(2,1)}, bf16[1024,25...) custom-call(s32[3]{0:T(128)} %pad_add_fusion.1.meta_ref, s32[256]{0:T(256)} %fusion.28.row_ref, ...), custom_call_target="tpu_custom_call", output_to_operand_aliasing={{0}: (11, {})} | custom-call | tf_op jit(solution)/shard_map/edge_grads/pallas_call | solution.py:604
  165.1 10.2 %all-to-all-start.7 = ((f32[16,3,128]{2,1,0:T(4,128)}), f32[16,3,128]{2,1,0:T(4,128)S(1)}, u32[]{:S(2)}, u32[]{:S(2)}) async-start(f32[16,3,128]{2,1,0:T(4,128)} %broadcast_in_dim.243), calls=%async_computation.7 | async-start | bytes 65536 | tf_op jit(solution)/shard_map/all_to_all | solution.py:60
  175.4 11.6 %all-to-all-done.7 = f32[16,3,128]{2,1,0:T(4,128)S(1)} async-done(((f32[16,3,128]{2,1,0:T(4,128)}), f32[16,3,128]{2,1,0:T(4,128)S(1)}, u32[]{:S(2)}, u32[]{:S(2)}) %all-to-all-start.7) | async-done | bytes 24608 | tf_op jit(solution)/shard_map/all_to_all | solution.py:60
  187.6 3.3 %all-to-all-start.8 = ((f32[4,16,3,128]{3,1,2,0:T(8,128)}), f32[4,16,3,128]{3,1,2,0:T(8,128)S(1)}, u32[]{:S(2)}, u32[]{:S(2)}) async-start(f32[4,16,3,128]{3,1,2,0:T(8,128)} %broadcast_in_dim.244), calls=%async_computation.8 | async-start | bytes 196608 | tf_op jit(solution)/shard_map/all_to_all | solution.py:60
  191.6 4.0 %all-to-all-done.8 = f32[4,16,3,128]{3,1,2,0:T(8,128)S(1)} async-done(((f32[4,16,3,128]{3,1,2,0:T(8,128)}), f32[4,16,3,128]{3,1,2,0:T(8,128)S(1)}, u32[]{:S(2)}, u32[]{:S(2)}) %all-to-all-start.8) | async-done | bytes 98336 | tf_op jit(solution)/shard_map/all_to_all | solution.py:60
  196.3 9.3 %own_grads.1 = (f32[1024,256]{1,0:T(8,128)}, f32[1024,256]{1,0:T(8,128)}, f32[256,256]{1,0:T(8,128)}) custom-call(s32[3]{0:T(128)} %pad_add_fusion.1.meta_ref, f32[32]{0:T(128)} %reshape.387.bias_ref, f32[16]{0:T(128)} %broadcast_select_fusion.1.flag_ref, bf16[1024,256]{1,0:T(8,128)(2,1)} %bitcast.100, bf16[1024,256]{1,0:T(8,128)(2,1)} %bitcast.93, ...), custom_call_target="tpu_custom_call" | custom-call | tf_op jit(solution)/shard_map/own_grads/pallas_call | solution.py:629
  205.6 1.1 convert_element_type.99
  206.7 7.2 %all_to_all.67 = bf16[4,64,256]{2,1,0:T(8,128)(2,1)S(1)} all-to-all(bf16[4,64,256]{2,1,0:T(8,128)(2,1)S(1)} %bitcast.105), channel_id=1, replica_groups=mesh['ctx_0'=16,'ctx_1'=4,'head'=8] {'ctx_1'}, dimensions={0} | all-to-all | bytes 262144 | tf_op jit(solution)/shard_map/all_to_all | solution.py:60
  213.9 14.3 %all_to_all.68 = bf16[16,4,256]{2,1,0:T(4,128)(2,1)S(1)} all-to-all(bf16[16,4,256]{2,1,0:T(4,128)(2,1)S(1)} %reshape.393), channel_id=1, replica_groups=mesh['ctx_0'=16,'ctx_1'=4,'head'=8] {'ctx_0'}, dimensions={0} | all-to-all | bytes 65536 | tf_op jit(solution)/shard_map/all_to_all | solution.py:60
  229.0 3.5 %all-to-all-start.11 = ((bf16[16,4,256]{2,1,0:T(4,128)(2,1)}), bf16[16,4,256]{2,1,0:T(4,128)(2,1)S(1)}, u32[]{:S(2)}, u32[]{:S(2)}) async-start(bf16[16,4,256]{2,1,0:T(4,128)(2,1)} %broadcast_in_dim.245), calls=%async_computation.11 | async-start | bytes 65536 | tf_op jit(solution)/shard_map/all_to_all | solution.py:60
  232.5 2.9 %collective-permute-start.3 = (bf16[1024,256]{1,0:T(8,128)(2,1)}, bf16[1024,256]{1,0:T(8,128)(2,1)S(1)}, u32[]{:S(2)}, u32[]{:S(2)}) collective-permute-start(bf16[1024,256]{1,0:T(8,128)(2,1)} %get-tuple-element.52), channel_id=1, source_target_pairs={{0,24},{8,0},{16,8},{24,16},{1,25},{9,1},{17,9},{25,17},{2,26},{10... | collective-permute-start | bytes 1572872 | tf_op jit(solution)/shard_map/ppermute | solution.py:626
  235.4 3.6 %collective-permute-start.4 = (bf16[1024,256]{1,0:T(8,128)(2,1)}, bf16[1024,256]{1,0:T(8,128)(2,1)S(1)}, u32[]{:S(2)}, u32[]{:S(2)}) collective-permute-start(bf16[1024,256]{1,0:T(8,128)(2,1)} %get-tuple-element.53), channel_id=1, source_target_pairs={{0,16},{8,24},{16,0},{24,8},{1,17},{9,25},{17,1},{25,9},{2,18},{10... | collective-permute-start | bytes 1572872 | tf_op jit(solution)/shard_map/ppermute | solution.py:626
  238.9 1.9 collective-permute-start.5
  240.9 3.5 %all-to-all-done.11 = bf16[16,4,256]{2,1,0:T(4,128)(2,1)S(1)} async-done(((bf16[16,4,256]{2,1,0:T(4,128)(2,1)}), bf16[16,4,256]{2,1,0:T(4,128)(2,1)S(1)}, u32[]{:S(2)}, u32[]{:S(2)}) %all-to-all-start.11) | async-done | bytes 32800 | tf_op jit(solution)/shard_map/all_to_all | solution.py:60
  245.1 3.3 %all-to-all-start.12 = ((bf16[4,64,256]{2,1,0:T(8,128)(2,1)}), bf16[4,64,256]{2,1,0:T(8,128)(2,1)S(1)}, u32[]{:S(2)}, u32[]{:S(2)}) async-start(bf16[4,64,256]{2,1,0:T(8,128)(2,1)} %broadcast_in_dim.247), calls=%async_computation.12 | async-start | bytes 262144 | tf_op jit(solution)/shard_map/all_to_all | solution.py:60
  248.7 14.4 %all-to-all-done.12 = bf16[4,64,256]{2,1,0:T(8,128)(2,1)S(1)} async-done(((bf16[4,64,256]{2,1,0:T(8,128)(2,1)}), bf16[4,64,256]{2,1,0:T(8,128)(2,1)S(1)}, u32[]{:S(2)}, u32[]{:S(2)}) %all-to-all-start.12) | async-done | bytes 131104 | tf_op jit(solution)/shard_map/all_to_all | solution.py:60
  263.1 1.6 fusion
  264.8 1.8 fusion.3
  267.4 4.3 %reduce-scatter.2.cloned.1.call-done = bf16[1024,256]{1,0:T(8,128)(2,1)} async-done(((bf16[16384,256]{1,0:T(8,128)(2,1)}), bf16[1024,256]{1,0:T(8,128)(2,1)}) %reduce-scatter.2.cloned.1.call-update) | async-done | bytes 524304 | tf_op jit(solution)/shard_map/reduce_scatter | solution.py:625
  271.7 1.9 add_convert_fusion
  (104 shorter events, 17.8 us)
Async XLA Ops:
  7.2 1.1 copy-start
  7.2 30.0 %copy-start.8 = (s32[16,1,3]{0,1,2:T(1,128)S(1)}, s32[16,1,3]{0,1,2:T(1,128)}, u32[]{:S(2)}) copy-start(s32[16,1,3]{0,1,2:T(1,128)} %param.10) | copy-start | bytes 580
  7.2 24.5 %copy-start.3 = (bf16[128,1024]{1,0:T(8,128)(2,1)S(1)}, bf16[128,1024]{1,0:T(8,128)(2,1)}, u32[]{:S(2)}) copy-start(bf16[128,1024]{1,0:T(8,128)(2,1)} %param.6) | copy-start | bytes 786436
  7.2 29.9 %copy-start.5 = (s32[2]{0:T(128)S(1)}, s32[2]{0:T(128)}, u32[]{:S(2)}) copy-start(s32[2]{0:T(128)} %index_ref.1) | copy-start | bytes 28
  7.2 128.9 %all-gather.2.cloned.1.call-start = ((), (), s32[]{:S(2)}) async-start(), calls=%async_computation.14 | async-start | bytes 8912896 | tf_op jit(solution)/shard_map/all_gather | solution.py:467
  9.3 70.2 %copy-start.6 = (s32[2]{0:T(128)S(1)}, s32[2]{0:T(128)}, u32[]{:S(2)}) copy-start(s32[2]{0:T(128)} %index_ref.1) | copy-start | bytes 28
  32.7 13.8 %all-to-all-start.1 = ((bf16[8,128,256]{2,1,0:T(8,128)(2,1)}), bf16[8,128,256]{2,1,0:T(8,128)(2,1)S(1)}, u32[]{:S(2)}, u32[]{:S(2)}) async-start(bf16[8,128,256]{2,1,0:T(8,128)(2,1)} %maximum_bitcast_fusion.1), calls=%async_computation.1 | async-start | bytes 1048576 | tf_op jit(solution)/shard_map/all_to_all | solution.py:60
  46.5 0.8 copy-start.1
  49.6 8.6 %all-to-all-start.2 = ((bf16[4,48,512]{2,1,0:T(8,128)(2,1)}), bf16[4,48,512]{2,1,0:T(8,128)(2,1)S(1)}, u32[]{:S(2)}, u32[]{:S(2)}) async-start(bf16[4,48,512]{2,1,0:T(8,128)(2,1)} %pick.1), calls=%async_computation.2 | async-start | bytes 393216 | tf_op jit(solution)/shard_map/all_to_all | solution.py:60
  58.2 46.1 %collective-permute-start = (bf16[1024,256]{1,0:T(8,128)(2,1)}, bf16[1024,256]{1,0:T(8,128)(2,1)S(1)}, u32[]{:S(2)}, u32[]{:S(2)}) collective-permute-start(bf16[1024,256]{1,0:T(8,128)(2,1)} %bitcast.95), channel_id=1, source_target_pairs={{0,8},{8,16},{16,24},{24,0},{1,9},{9,17},{17,25},{25,1},{2,10},{10... | collective-permute-start | bytes 1572872 | tf_op jit(solution)/shard_map/ppermute | solution.py:511
  60.7 43.5 %collective-permute-start.1 = (bf16[1024,256]{1,0:T(8,128)(2,1)}, bf16[1024,256]{1,0:T(8,128)(2,1)S(1)}, u32[]{:S(2)}, u32[]{:S(2)}) collective-permute-start(bf16[1024,256]{1,0:T(8,128)(2,1)} %bitcast.96), channel_id=1, source_target_pairs={{0,16},{8,24},{16,0},{24,8},{1,17},{9,25},{17,1},{25,9},{2,18},{10... | collective-permute-start | bytes 1572872 | tf_op jit(solution)/shard_map/ppermute | solution.py:511
  64.1 40.2 %collective-permute-start.2 = (bf16[1024,256]{1,0:T(8,128)(2,1)}, bf16[1024,256]{1,0:T(8,128)(2,1)S(1)}, u32[]{:S(2)}, u32[]{:S(2)}) collective-permute-start(bf16[1024,256]{1,0:T(8,128)(2,1)} %bitcast.97), channel_id=1, source_target_pairs={{0,24},{8,0},{16,8},{24,16},{1,25},{9,1},{17,9},{25,17},{2,26},{10... | collective-permute-start | bytes 1572872 | tf_op jit(solution)/shard_map/ppermute | solution.py:511
  68.0 24.0 %all-to-all-start.3 = ((bf16[16,2,1,512]{3,1,2,0:T(2,128)(2,1)}), bf16[16,2,1,512]{3,1,2,0:T(2,128)(2,1)S(1)}, u32[]{:S(2)}, u32[]{:S(2)}) async-start(bf16[16,2,1,512]{3,1,2,0:T(2,128)(2,1)} %copy.178), calls=%async_computation.3 | async-start | bytes 65536 | tf_op jit(solution)/shard_map/all_to_all | solution.py:60
  83.0 53.1 %copy-start.4 = (s32[256]{0:T(256)}, s32[256]{0:T(256)S(1)}, u32[]{:S(2)}) copy-start(s32[256]{0:T(256)S(1)} %get-tuple-element.59.cell_ref) | copy-start | bytes 3076
  92.8 23.4 %all-to-all-start.4 = ((bf16[16,2,1,512]{3,1,2,0:T(2,128)(2,1)}), bf16[16,2,1,512]{3,1,2,0:T(2,128)(2,1)S(1)}, u32[]{:S(2)}, u32[]{:S(2)}) async-start(bf16[16,2,1,512]{3,1,2,0:T(2,128)(2,1)} %broadcast_in_dim.237), calls=%async_computation.4 | async-start | bytes 65536 | tf_op jit(solution)/shard_map/all_to_all | solution.py:60
  116.8 8.2 %all-to-all-start.5 = ((bf16[4,2,16,512]{3,2,1,0:T(8,128)(2,1)}), bf16[4,2,16,512]{3,2,1,0:T(8,128)(2,1)S(1)}, u32[]{:S(2)}, u32[]{:S(2)}) async-start(bf16[4,2,16,512]{3,2,1,0:T(8,128)(2,1)} %broadcast_in_dim.239), calls=%async_computation.5 | async-start | bytes 262144 | tf_op jit(solution)/shard_map/all_to_all | solution.py:60
  120.1 151.6 %reduce-scatter.2.cloned.1.call-start = ((), (), s32[]{:S(2)}) async-start(), calls=%async_computation.15 | async-start | bytes 8912896 | tf_op jit(solution)/shard_map/reduce_scatter | solution.py:625
  163.8 0.7 copy-start.7
  165.1 21.9 %all-to-all-start.7 = ((f32[16,3,128]{2,1,0:T(4,128)}), f32[16,3,128]{2,1,0:T(4,128)S(1)}, u32[]{:S(2)}, u32[]{:S(2)}) async-start(f32[16,3,128]{2,1,0:T(4,128)} %broadcast_in_dim.243), calls=%async_computation.7 | async-start | bytes 65536 | tf_op jit(solution)/shard_map/all_to_all | solution.py:60
  187.6 7.9 %all-to-all-start.8 = ((f32[4,16,3,128]{3,1,2,0:T(8,128)}), f32[4,16,3,128]{3,1,2,0:T(8,128)S(1)}, u32[]{:S(2)}, u32[]{:S(2)}) async-start(f32[4,16,3,128]{3,1,2,0:T(8,128)} %broadcast_in_dim.244), calls=%async_computation.8 | async-start | bytes 196608 | tf_op jit(solution)/shard_map/all_to_all | solution.py:60
  205.6 59.2 %copy-start.2 = (f32[1024,256]{1,0:T(8,128)S(1)}, f32[1024,256]{1,0:T(8,128)}, u32[]{:S(2)}) copy-start(f32[1024,256]{1,0:T(8,128)} %get-tuple-element.51) | copy-start | bytes 3145732
  229.0 15.4 %all-to-all-start.11 = ((bf16[16,4,256]{2,1,0:T(4,128)(2,1)}), bf16[16,4,256]{2,1,0:T(4,128)(2,1)S(1)}, u32[]{:S(2)}, u32[]{:S(2)}) async-start(bf16[16,4,256]{2,1,0:T(4,128)(2,1)} %broadcast_in_dim.245), calls=%async_computation.11 | async-start | bytes 65536 | tf_op jit(solution)/shard_map/all_to_all | solution.py:60
  232.5 32.3 %collective-permute-start.3 = (bf16[1024,256]{1,0:T(8,128)(2,1)}, bf16[1024,256]{1,0:T(8,128)(2,1)S(1)}, u32[]{:S(2)}, u32[]{:S(2)}) collective-permute-start(bf16[1024,256]{1,0:T(8,128)(2,1)} %get-tuple-element.52), channel_id=1, source_target_pairs={{0,24},{8,0},{16,8},{24,16},{1,25},{9,1},{17,9},{25,17},{2,26},{10... | collective-permute-start | bytes 1572872 | tf_op jit(solution)/shard_map/ppermute | solution.py:626
  235.4 29.4 %collective-permute-start.4 = (bf16[1024,256]{1,0:T(8,128)(2,1)}, bf16[1024,256]{1,0:T(8,128)(2,1)S(1)}, u32[]{:S(2)}, u32[]{:S(2)}) collective-permute-start(bf16[1024,256]{1,0:T(8,128)(2,1)} %get-tuple-element.53), channel_id=1, source_target_pairs={{0,16},{8,24},{16,0},{24,8},{1,17},{9,25},{17,1},{25,9},{2,18},{10... | collective-permute-start | bytes 1572872 | tf_op jit(solution)/shard_map/ppermute | solution.py:626
  238.9 25.8 %collective-permute-start.5 = (bf16[1024,256]{1,0:T(8,128)(2,1)}, bf16[1024,256]{1,0:T(8,128)(2,1)}, u32[]{:S(2)}, u32[]{:S(2)}) collective-permute-start(bf16[1024,256]{1,0:T(8,128)(2,1)} %get-tuple-element.54), channel_id=1, source_target_pairs={{0,8},{8,16},{16,24},{24,0},{1,9},{9,17},{17,25},{25,1},{2,10},{10... | collective-permute-start | bytes 1572872 | tf_op jit(solution)/shard_map/ppermute | solution.py:626
  245.1 18.0 %all-to-all-start.12 = ((bf16[4,64,256]{2,1,0:T(8,128)(2,1)}), bf16[4,64,256]{2,1,0:T(8,128)(2,1)S(1)}, u32[]{:S(2)}, u32[]{:S(2)}) async-start(bf16[4,64,256]{2,1,0:T(8,128)(2,1)} %broadcast_in_dim.247), calls=%async_computation.12 | async-start | bytes 262144 | tf_op jit(solution)/shard_map/all_to_all | solution.py:60
Sparse Core Ops, SparseCore 0:
  28.8 107.2 all-gather.1
  163.9 107.7 reduce-scatter.1

commit v7 on v6

--- a/solution.py
+++ b/solution.py
@@ -136,9 +136,7 @@
             out_ref[lane, g * part : (g + 1) * part, :] = rows_ref[low : low + part, :]
 
 
-def own_stats_kernel(
-    bias_ref, qd_ref, kv_ref, shared_ref, own_ref, rows_ref, table_ref, zero_ref, zero_sems
-):
+def clear_kernel(after_ref, table_ref, zero_ref, zero_sems):
     size = zero_ref.shape[0]
     zero_ref[...] = jnp.zeros(zero_ref.shape, jnp.bfloat16)
     clears = [
@@ -147,6 +145,11 @@
     ]
     for clear in clears:
         clear.start()
+    for clear in clears:
+        clear.wait()
+
+
+def own_stats_kernel(bias_ref, qd_ref, kv_ref, shared_ref, own_ref, rows_ref):
     tokens = qd_ref.shape[0]
     blocks = tokens // S
     for i in range(blocks):
@@ -168,8 +171,6 @@
     rows_ref[0:1, :] = top
     rows_ref[1:2, :] = total
     rows_ref[2:3, :] = slope
-    for clear in clears:
-        clear.wait()
 
 
 def cell_fetcher(meta_ref, cell_ref, kv_ref, fetch_ref, fetch_sems):
@@ -510,7 +511,21 @@
     qd_group = jnp.concatenate(
         [qd] + [lax.ppermute(qd_sent, Y_AXIS, pairs) for pairs in forward], 0
     )
-    gathered, qd_group = lax.optimization_barrier((to_all(picked, Z_AXIS), qd_group))
+    cleared = pl.pallas_call(
+        clear_kernel,
+        out_shape=jax.ShapeDtypeStruct((cells * S, 2 * D), jnp.bfloat16),
+        in_specs=[ANY],
+        out_specs=ANY,
+        scratch_shapes=[
+            pltpu.VMEM((tokens, 2 * D), jnp.bfloat16),
+            pltpu.SemaphoreType.DMA((z_count,)),
+        ],
+        compiler_params=PARAMS,
+        name="clear",
+    )(qd_group)
+    gathered, qd_group, cleared = lax.optimization_barrier(
+        (to_all(picked, Z_AXIS), qd_group, cleared)
+    )
     shared = gathered.transpose(1, 0, 2, 3).reshape(WORLDWIDE_COUNT, part, 4 * D)
     shared = to_all(shared, Y_AXIS).transpose(1, 0, 2, 3).reshape(G, 4 * D)
 
@@ -567,19 +582,14 @@
     hits = own_ids[:, None] == universal_segment_indices[None]
     flags = jnp.where(jnp.any(hits, 1), 0.0, 1.0).astype(f32)
 
-    own, rows, cleared = pl.pallas_call(
+    own, rows = pl.pallas_call(
         own_stats_kernel,
         out_shape=(
             jax.ShapeDtypeStruct((3, block_count, S), f32),
             jax.ShapeDtypeStruct((3, G), f32),
-            jax.ShapeDtypeStruct((cells * S, 2 * D), jnp.bfloat16),
         ),
         in_specs=[SMEM, VMEM, VMEM, VMEM],
-        out_specs=(VMEM, VMEM, ANY),
-        scratch_shapes=[
-            pltpu.VMEM((tokens, 2 * D), jnp.bfloat16),
-            pltpu.SemaphoreType.DMA((z_count,)),
-        ],
+        out_specs=(VMEM, VMEM),
         compiler_params=PARAMS,
         name="own_stats",
     )(bias, qd, kv, shared)

time: 283 us -> 283 us (level)
    all_to_all x9, waiting for transfers between devices: 58.7 us -> 52.2 us  [exchange(): return lax.all_to_all(array, axes, split_axis=0, concat_axis=0, tiled=True)]
    reduce_scatter x1, waiting for transfers between devices: 4.34 us -> 10.2 us  [body(): returned = lax.psum_scatter(table, Z_AXIS, scatter_dimension=0, tiled=True)]
    pallas_call x0 -> x1, Pallas kernels: none -> 3.45 us  [body(): pl.pallas_call(clear_kernel, out_shape=jax.ShapeDtypeStruct((cells * S, 2...]
    pallas_call x1, Pallas kernels: 6.88 us -> 3.47 us  [body(): pl.pallas_call(own_stats_kernel, out_shape=(jax.ShapeDtypeStruct((3, bloc...]
    all_gather x1, waiting for transfers between devices: 3.55 us -> 6.92 us  [body(): kv_all = lax.all_gather(kv, Z_AXIS, axis=0, tiled=True)]
where the time goes in v7:
time: 283 us; the launch traced here: 281 us
  starting transfers between devices  69.8 us (25%)
  waiting for transfers between devices  69.3 us (24%)
  blocking collectives  50.5 us (18%)
  Pallas kernels  36.3 us (13%)
  other arithmetic  22.9 us (8%)
  between operations  17.2 us (6%)
  local copies, waits for them, and re-layouts  15.2 us (5%)
    all_to_all x9, starting transfers between devices, exchange(): return lax.all_to_all(array, axes, split_axis=0, concat_axis=0, tiled=True)  52.7 us
    all_to_all x9, waiting for transfers between devices, exchange(): return lax.all_to_all(array, axes, split_axis=0, concat_axis=0, tiled=True)  52.2 us
    all_to_all x4, blocking collectives, exchange(): return lax.all_to_all(array, axes, split_axis=0, concat_axis=0, tiled=True)  50.5 us
    pallas_call x1, Pallas kernels, body(): pl.pallas_call(edge_grads_kernel, out_shape=(jax.ShapeDtypeStruct((cells...  11.6 us
    reduce_scatter x1, waiting for transfers between devices, body(): returned = lax.psum_scatter(table, Z_AXIS, scatter_dimension=0, tiled=True)  10.2 us
    pallas_call x1, Pallas kernels, body(): pl.pallas_call(own_grads_kernel, out_shape=(jax.ShapeDtypeStruct((tokens,...  9.34 us
    ppermute x3, starting transfers between devices, body(): lax.ppermute(qd_sent, Y_AXIS, pairs)  8.76 us
    ppermute x3, starting transfers between devices, body(): lax.ppermute(half, Y_AXIS, pairs)  8.24 us
  transfers between devices with their start and end apart: 17, of which 10 were waited for; matrix products, arithmetic and copies ran while one was open for 12% of the time, Pallas kernels for 7%

profile of v7, /device:TPU:1, one launch (start us, length us, event | category | flops | bytes accessed | tf_op | source)
XLA Modules:
  0.0 281.2 jit_solution(625102667658992006)
XLA Ops:
  7.3 1.0 copy-done
  8.2 1.1 copy_bitcast_fusion.2
  9.4 19.2 %all_to_all.65 = bf16[8,128,256]{2,1,0:T(8,128)(2,1)} all-to-all(bf16[8,128,256]{2,1,0:T(8,128)(2,1)S(1)} %maximum_bitcast_fusion), channel_id=1, replica_groups=mesh['ctx_0'=16,'ctx_1'=4,'head'=8] {'head'}, dimensions={0} | all-to-all | bytes 1048576 | tf_op jit(solution)/shard_map/all_to_all | solution.py:60
  28.7 1.3 fusion.40
  30.7 1.0 copy_bitcast_fusion
  32.7 4.4 %all-to-all-start.1 = ((bf16[8,128,256]{2,1,0:T(8,128)(2,1)}), bf16[8,128,256]{2,1,0:T(8,128)(2,1)S(1)}, u32[]{:S(2)}, u32[]{:S(2)}) async-start(bf16[8,128,256]{2,1,0:T(8,128)(2,1)} %maximum_bitcast_fusion.1), calls=%async_computation.1 | async-start | bytes 1048576 | tf_op jit(solution)/shard_map/all_to_all | solution.py:60
  38.1 8.4 %all-to-all-done.1 = bf16[8,128,256]{2,1,0:T(8,128)(2,1)S(1)} async-done(((bf16[8,128,256]{2,1,0:T(8,128)(2,1)}), bf16[8,128,256]{2,1,0:T(8,128)(2,1)S(1)}, u32[]{:S(2)}, u32[]{:S(2)}) %all-to-all-start.1) | async-done | bytes 524320 | tf_op jit(solution)/shard_map/all_to_all | solution.py:60
  47.3 2.3 pick.1
  49.6 3.4 %all-to-all-start.2 = ((bf16[4,48,512]{2,1,0:T(8,128)(2,1)}), bf16[4,48,512]{2,1,0:T(8,128)(2,1)S(1)}, u32[]{:S(2)}, u32[]{:S(2)}) async-start(bf16[4,48,512]{2,1,0:T(8,128)(2,1)} %pick.1), calls=%async_computation.2 | async-start | bytes 393216 | tf_op jit(solution)/shard_map/all_to_all | solution.py:60
  54.3 3.9 %all-to-all-done.2 = bf16[4,48,512]{2,1,0:T(8,128)(2,1)S(1)} async-done(((bf16[4,48,512]{2,1,0:T(8,128)(2,1)}), bf16[4,48,512]{2,1,0:T(8,128)(2,1)S(1)}, u32[]{:S(2)}, u32[]{:S(2)}) %all-to-all-start.2) | async-done | bytes 196640 | tf_op jit(solution)/shard_map/all_to_all | solution.py:60
  58.2 2.5 collective-permute-start
  60.7 3.3 %collective-permute-start.1 = (bf16[1024,256]{1,0:T(8,128)(2,1)}, bf16[1024,256]{1,0:T(8,128)(2,1)S(1)}, u32[]{:S(2)}, u32[]{:S(2)}) collective-permute-start(bf16[1024,256]{1,0:T(8,128)(2,1)} %bitcast.96), channel_id=1, source_target_pairs={{0,16},{8,24},{16,0},{24,8},{1,17},{9,25},{17,1},{25,9},{2,18},{10... | collective-permute-start | bytes 1572872 | tf_op jit(solution)/shard_map/ppermute | solution.py:512
  64.1 2.9 %collective-permute-start.2 = (bf16[1024,256]{1,0:T(8,128)(2,1)}, bf16[1024,256]{1,0:T(8,128)(2,1)S(1)}, u32[]{:S(2)}, u32[]{:S(2)}) collective-permute-start(bf16[1024,256]{1,0:T(8,128)(2,1)} %bitcast.97), channel_id=1, source_target_pairs={{0,24},{8,0},{16,8},{24,16},{1,25},{9,1},{17,9},{25,17},{2,26},{10... | collective-permute-start | bytes 1572872 | tf_op jit(solution)/shard_map/ppermute | solution.py:512
  67.7 11.5 %all-to-all-start.3 = ((bf16[16,2,1,512]{3,1,2,0:T(2,128)(2,1)}), bf16[16,2,1,512]{3,1,2,0:T(2,128)(2,1)S(1)}, u32[]{:S(2)}, u32[]{:S(2)}) async-start(bf16[16,2,1,512]{3,1,2,0:T(2,128)(2,1)} %copy.178), calls=%async_computation.3 | async-start | bytes 65536 | tf_op jit(solution)/shard_map/all_to_all | solution.py:60
  83.7 2.6 fusion.34
  87.5 1.2 fusion.24
  88.8 1.2 fusion.28.row_ref
  92.8 11.5 %all-to-all-start.4 = ((bf16[16,2,1,512]{3,1,2,0:T(2,128)(2,1)}), bf16[16,2,1,512]{3,1,2,0:T(2,128)(2,1)S(1)}, u32[]{:S(2)}, u32[]{:S(2)}) async-start(bf16[16,2,1,512]{3,1,2,0:T(2,128)(2,1)} %broadcast_in_dim.237), calls=%async_computation.4 | async-start | bytes 65536 | tf_op jit(solution)/shard_map/all_to_all | solution.py:60
  104.3 2.5 pad_maximum_fusion.after_ref.qd_ref
  106.8 3.4 %clear.1.cleared_ref = bf16[16384,256]{1,0:T(8,128)(2,1)} custom-call(bf16[4096,256]{1,0:T(8,128)(2,1)} %pad_maximum_fusion.after_ref.qd_ref), custom_call_target="tpu_custom_call" | custom-call | tf_op jit(solution)/shard_map/clear/pallas_call | solution.py:514
  110.2 5.9 %all-to-all-done.4 = bf16[16,2,1,512]{3,1,2,0:T(2,128)(2,1)S(1)} async-done(((bf16[16,2,1,512]{3,1,2,0:T(2,128)(2,1)}), bf16[16,2,1,512]{3,1,2,0:T(2,128)(2,1)S(1)}, u32[]{:S(2)}, u32[]{:S(2)}) %all-to-all-start.4) | async-done | bytes 32800 | tf_op jit(solution)/shard_map/all_to_all | solution.py:60
  116.8 3.3 %all-to-all-start.5 = ((bf16[4,2,16,512]{3,2,1,0:T(8,128)(2,1)}), bf16[4,2,16,512]{3,2,1,0:T(8,128)(2,1)S(1)}, u32[]{:S(2)}, u32[]{:S(2)}) async-start(bf16[4,2,16,512]{3,2,1,0:T(8,128)(2,1)} %broadcast_in_dim.239), calls=%async_computation.5 | async-start | bytes 262144 | tf_op jit(solution)/shard_map/all_to_all | solution.py:60
  120.2 1.3 pad_add_fusion.1.meta_ref
  121.5 3.5 %all-to-all-done.5 = bf16[4,2,16,512]{3,2,1,0:T(8,128)(2,1)S(1)} async-done(((bf16[4,2,16,512]{3,2,1,0:T(8,128)(2,1)}), bf16[4,2,16,512]{3,2,1,0:T(8,128)(2,1)S(1)}, u32[]{:S(2)}, u32[]{:S(2)}) %all-to-all-start.5) | async-done | bytes 131104 | tf_op jit(solution)/shard_map/all_to_all | solution.py:60
  125.7 3.5 %own_stats.1 = (f32[3,16,64]{2,1,0:T(8,128)}, f32[3,128]{1,0:T(4,128)}) custom-call(f32[32]{0:T(128)} %reshape.387.bias_ref, bf16[1024,256]{1,0:T(8,128)(2,1)} %bitcast.99, bf16[1024,256]{1,0:T(8,128)(2,1)} %bitcast.92, bf16[128,512]{1,0:T(8,128)(2,1)} %bitcast.101), custom_call_target="tpu_custom_call" | custom-call | tf_op jit(solution)/shard_map/own_stats/pallas_call | solution.py:585
  129.1 6.9 %all-gather.2.cloned.1.call-done.kv_ref = bf16[16384,256]{1,0:T(8,128)(2,1)} async-done(((bf16[1024,256]{1,0:T(8,128)(2,1)}), bf16[16384,256]{1,0:T(8,128)(2,1)}) %all-gather.2.cloned.1.call-update) | async-done | bytes 8388624 | tf_op jit(solution)/shard_map/all_gather | solution.py:468
  136.1 6.2 %edge_stats.1 = f32[4,128,128]{2,1,0:T(8,128)} custom-call(s32[3]{0:T(128)} %pad_add_fusion.1.meta_ref, s32[256]{0:T(256)} %get-tuple-element.64.slot_ref, s32[256]{0:T(256)} %get-tuple-element.62.item_ref, s32[256]{0:T(256)} %copy-done.4, bf16[4096,256]{1,0:T(8,128)(2,1)} %pad_maximum_fusion.after_ref.qd_ref, ...), custom_call_target="tpu_custom_call" | custom-call | tf_op jit(solution)/shard_map/edge_stats/pallas_call | solution.py:603
  142.3 9.7 %all_to_all.66.parts_ref = f32[4,128,128]{2,1,0:T(8,128)} all-to-all(f32[4,128,128]{2,1,0:T(8,128)} %edge_stats.1), channel_id=1, replica_groups=mesh['ctx_0'=16,'ctx_1'=4,'head'=8] {'ctx_1'}, dimensions={0} | all-to-all | bytes 524288 | tf_op jit(solution)/shard_map/all_to_all | solution.py:60
  151.9 11.6 %edge_grads.1 = (bf16[16384,256]{1,0:T(8,128)(2,1)}, f32[3,72,128]{2,1,0:T(8,128)}, f32[1024,256]{1,0:T(8,128)}, bf16[1024,256]{1,0:T(8,128)(2,1)}, bf16[1024,25...) custom-call(s32[3]{0:T(128)} %pad_add_fusion.1.meta_ref, s32[256]{0:T(256)} %fusion.28.row_ref, ...), custom_call_target="tpu_custom_call", output_to_operand_aliasing={{0}: (11, {})} | custom-call | tf_op jit(solution)/shard_map/edge_grads/pallas_call | solution.py:614
  164.8 8.4 %all-to-all-start.7 = ((f32[16,3,128]{2,1,0:T(4,128)}), f32[16,3,128]{2,1,0:T(4,128)S(1)}, u32[]{:S(2)}, u32[]{:S(2)}) async-start(f32[16,3,128]{2,1,0:T(4,128)} %broadcast_in_dim.243), calls=%async_computation.7 | async-start | bytes 65536 | tf_op jit(solution)/shard_map/all_to_all | solution.py:60
  173.3 11.5 %all-to-all-done.7 = f32[16,3,128]{2,1,0:T(4,128)S(1)} async-done(((f32[16,3,128]{2,1,0:T(4,128)}), f32[16,3,128]{2,1,0:T(4,128)S(1)}, u32[]{:S(2)}, u32[]{:S(2)}) %all-to-all-start.7) | async-done | bytes 24608 | tf_op jit(solution)/shard_map/all_to_all | solution.py:60
  185.5 3.3 %all-to-all-start.8 = ((f32[4,16,3,128]{3,1,2,0:T(8,128)}), f32[4,16,3,128]{3,1,2,0:T(8,128)S(1)}, u32[]{:S(2)}, u32[]{:S(2)}) async-start(f32[4,16,3,128]{3,1,2,0:T(8,128)} %broadcast_in_dim.244), calls=%async_computation.8 | async-start | bytes 196608 | tf_op jit(solution)/shard_map/all_to_all | solution.py:60
  189.4 4.0 %all-to-all-done.8 = f32[4,16,3,128]{3,1,2,0:T(8,128)S(1)} async-done(((f32[4,16,3,128]{3,1,2,0:T(8,128)}), f32[4,16,3,128]{3,1,2,0:T(8,128)S(1)}, u32[]{:S(2)}, u32[]{:S(2)}) %all-to-all-start.8) | async-done | bytes 98336 | tf_op jit(solution)/shard_map/all_to_all | solution.py:60
  194.1 9.3 %own_grads.1 = (f32[1024,256]{1,0:T(8,128)}, f32[1024,256]{1,0:T(8,128)}, f32[256,256]{1,0:T(8,128)}) custom-call(s32[3]{0:T(128)} %pad_add_fusion.1.meta_ref, f32[32]{0:T(128)} %reshape.387.bias_ref, f32[16]{0:T(128)} %broadcast_select_fusion.1.flag_ref, bf16[1024,256]{1,0:T(8,128)(2,1)} %bitcast.100, bf16[1024,256]{1,0:T(8,128)(2,1)} %bitcast.93, ...), custom_call_target="tpu_custom_call" | custom-call | tf_op jit(solution)/shard_map/own_grads/pallas_call | solution.py:639
  203.4 1.1 convert_element_type.99
  204.5 7.2 %all_to_all.67 = bf16[4,64,256]{2,1,0:T(8,128)(2,1)S(1)} all-to-all(bf16[4,64,256]{2,1,0:T(8,128)(2,1)S(1)} %bitcast.105), channel_id=1, replica_groups=mesh['ctx_0'=16,'ctx_1'=4,'head'=8] {'ctx_1'}, dimensions={0} | all-to-all | bytes 262144 | tf_op jit(solution)/shard_map/all_to_all | solution.py:60
  211.8 14.4 %all_to_all.68 = bf16[16,4,256]{2,1,0:T(4,128)(2,1)S(1)} all-to-all(bf16[16,4,256]{2,1,0:T(4,128)(2,1)S(1)} %reshape.393), channel_id=1, replica_groups=mesh['ctx_0'=16,'ctx_1'=4,'head'=8] {'ctx_0'}, dimensions={0} | all-to-all | bytes 65536 | tf_op jit(solution)/shard_map/all_to_all | solution.py:60
  226.9 3.5 %all-to-all-start.11 = ((bf16[16,4,256]{2,1,0:T(4,128)(2,1)}), bf16[16,4,256]{2,1,0:T(4,128)(2,1)S(1)}, u32[]{:S(2)}, u32[]{:S(2)}) async-start(bf16[16,4,256]{2,1,0:T(4,128)(2,1)} %broadcast_in_dim.245), calls=%async_computation.11 | async-start | bytes 65536 | tf_op jit(solution)/shard_map/all_to_all | solution.py:60
  230.4 2.8 %collective-permute-start.3 = (bf16[1024,256]{1,0:T(8,128)(2,1)}, bf16[1024,256]{1,0:T(8,128)(2,1)S(1)}, u32[]{:S(2)}, u32[]{:S(2)}) collective-permute-start(bf16[1024,256]{1,0:T(8,128)(2,1)} %get-tuple-element.52), channel_id=1, source_target_pairs={{0,24},{8,0},{16,8},{24,16},{1,25},{9,1},{17,9},{25,17},{2,26},{10... | collective-permute-start | bytes 1572872 | tf_op jit(solution)/shard_map/ppermute | solution.py:636
  233.2 3.5 %collective-permute-start.4 = (bf16[1024,256]{1,0:T(8,128)(2,1)}, bf16[1024,256]{1,0:T(8,128)(2,1)S(1)}, u32[]{:S(2)}, u32[]{:S(2)}) collective-permute-start(bf16[1024,256]{1,0:T(8,128)(2,1)} %get-tuple-element.53), channel_id=1, source_target_pairs={{0,16},{8,24},{16,0},{24,8},{1,17},{9,25},{17,1},{25,9},{2,18},{10... | collective-permute-start | bytes 1572872 | tf_op jit(solution)/shard_map/ppermute | solution.py:636
  236.7 1.9 collective-permute-start.5
  238.6 3.6 %all-to-all-done.11 = bf16[16,4,256]{2,1,0:T(4,128)(2,1)S(1)} async-done(((bf16[16,4,256]{2,1,0:T(4,128)(2,1)}), bf16[16,4,256]{2,1,0:T(4,128)(2,1)S(1)}, u32[]{:S(2)}, u32[]{:S(2)}) %all-to-all-start.11) | async-done | bytes 32800 | tf_op jit(solution)/shard_map/all_to_all | solution.py:60
  242.9 3.3 %all-to-all-start.12 = ((bf16[4,64,256]{2,1,0:T(8,128)(2,1)}), bf16[4,64,256]{2,1,0:T(8,128)(2,1)S(1)}, u32[]{:S(2)}, u32[]{:S(2)}) async-start(bf16[4,64,256]{2,1,0:T(8,128)(2,1)} %broadcast_in_dim.247), calls=%async_computation.12 | async-start | bytes 262144 | tf_op jit(solution)/shard_map/all_to_all | solution.py:60
  246.6 11.3 %all-to-all-done.12 = bf16[4,64,256]{2,1,0:T(8,128)(2,1)S(1)} async-done(((bf16[4,64,256]{2,1,0:T(8,128)(2,1)}), bf16[4,64,256]{2,1,0:T(8,128)(2,1)S(1)}, u32[]{:S(2)}, u32[]{:S(2)}) %all-to-all-start.12) | async-done | bytes 131104 | tf_op jit(solution)/shard_map/all_to_all | solution.py:60
  258.0 1.6 fusion
  259.6 1.8 fusion.3
  262.2 10.2 %reduce-scatter.2.cloned.1.call-done = bf16[1024,256]{1,0:T(8,128)(2,1)} async-done(((bf16[16384,256]{1,0:T(8,128)(2,1)}), bf16[1024,256]{1,0:T(8,128)(2,1)}) %reduce-scatter.2.cloned.1.call-update) | async-done | bytes 524304 | tf_op jit(solution)/shard_map/reduce_scatter | solution.py:635
  272.4 1.9 add_convert_fusion
  (105 shorter events, 18.7 us)
Async XLA Ops:
  7.2 1.1 copy-start
  7.2 30.0 %copy-start.8 = (s32[16,1,3]{0,1,2:T(1,128)S(1)}, s32[16,1,3]{0,1,2:T(1,128)}, u32[]{:S(2)}) copy-start(s32[16,1,3]{0,1,2:T(1,128)} %param.10) | copy-start | bytes 580
  7.2 24.5 %copy-start.3 = (bf16[128,1024]{1,0:T(8,128)(2,1)S(1)}, bf16[128,1024]{1,0:T(8,128)(2,1)}, u32[]{:S(2)}) copy-start(bf16[128,1024]{1,0:T(8,128)(2,1)} %param.6) | copy-start | bytes 786436
  7.2 29.9 %copy-start.5 = (s32[2]{0:T(128)S(1)}, s32[2]{0:T(128)}, u32[]{:S(2)}) copy-start(s32[2]{0:T(128)} %index_ref.1) | copy-start | bytes 28
  7.2 128.9 %all-gather.2.cloned.1.call-start = ((), (), s32[]{:S(2)}) async-start(), calls=%async_computation.14 | async-start | bytes 8912896 | tf_op jit(solution)/shard_map/all_gather | solution.py:468
  9.3 70.2 %copy-start.6 = (s32[2]{0:T(128)S(1)}, s32[2]{0:T(128)}, u32[]{:S(2)}) copy-start(s32[2]{0:T(128)} %index_ref.1) | copy-start | bytes 28
  32.7 13.8 %all-to-all-start.1 = ((bf16[8,128,256]{2,1,0:T(8,128)(2,1)}), bf16[8,128,256]{2,1,0:T(8,128)(2,1)S(1)}, u32[]{:S(2)}, u32[]{:S(2)}) async-start(bf16[8,128,256]{2,1,0:T(8,128)(2,1)} %maximum_bitcast_fusion.1), calls=%async_computation.1 | async-start | bytes 1048576 | tf_op jit(solution)/shard_map/all_to_all | solution.py:60
  46.5 0.8 copy-start.1
  49.6 8.6 %all-to-all-start.2 = ((bf16[4,48,512]{2,1,0:T(8,128)(2,1)}), bf16[4,48,512]{2,1,0:T(8,128)(2,1)S(1)}, u32[]{:S(2)}, u32[]{:S(2)}) async-start(bf16[4,48,512]{2,1,0:T(8,128)(2,1)} %pick.1), calls=%async_computation.2 | async-start | bytes 393216 | tf_op jit(solution)/shard_map/all_to_all | solution.py:60
  58.2 46.1 %collective-permute-start = (bf16[1024,256]{1,0:T(8,128)(2,1)}, bf16[1024,256]{1,0:T(8,128)(2,1)S(1)}, u32[]{:S(2)}, u32[]{:S(2)}) collective-permute-start(bf16[1024,256]{1,0:T(8,128)(2,1)} %bitcast.95), channel_id=1, source_target_pairs={{0,8},{8,16},{16,24},{24,0},{1,9},{9,17},{17,25},{25,1},{2,10},{10... | collective-permute-start | bytes 1572872 | tf_op jit(solution)/shard_map/ppermute | solution.py:512
  60.7 43.5 %collective-permute-start.1 = (bf16[1024,256]{1,0:T(8,128)(2,1)}, bf16[1024,256]{1,0:T(8,128)(2,1)S(1)}, u32[]{:S(2)}, u32[]{:S(2)}) collective-permute-start(bf16[1024,256]{1,0:T(8,128)(2,1)} %bitcast.96), channel_id=1, source_target_pairs={{0,16},{8,24},{16,0},{24,8},{1,17},{9,25},{17,1},{25,9},{2,18},{10... | collective-permute-start | bytes 1572872 | tf_op jit(solution)/shard_map/ppermute | solution.py:512
  64.1 40.2 %collective-permute-start.2 = (bf16[1024,256]{1,0:T(8,128)(2,1)}, bf16[1024,256]{1,0:T(8,128)(2,1)S(1)}, u32[]{:S(2)}, u32[]{:S(2)}) collective-permute-start(bf16[1024,256]{1,0:T(8,128)(2,1)} %bitcast.97), channel_id=1, source_target_pairs={{0,24},{8,0},{16,8},{24,16},{1,25},{9,1},{17,9},{25,17},{2,26},{10... | collective-permute-start | bytes 1572872 | tf_op jit(solution)/shard_map/ppermute | solution.py:512
  67.7 24.3 %all-to-all-start.3 = ((bf16[16,2,1,512]{3,1,2,0:T(2,128)(2,1)}), bf16[16,2,1,512]{3,1,2,0:T(2,128)(2,1)S(1)}, u32[]{:S(2)}, u32[]{:S(2)}) async-start(bf16[16,2,1,512]{3,1,2,0:T(2,128)(2,1)} %copy.178), calls=%async_computation.3 | async-start | bytes 65536 | tf_op jit(solution)/shard_map/all_to_all | solution.py:60
  83.0 27.2 %copy-start.4 = (s32[256]{0:T(256)}, s32[256]{0:T(256)S(1)}, u32[]{:S(2)}) copy-start(s32[256]{0:T(256)S(1)} %get-tuple-element.59.cell_ref) | copy-start | bytes 3076
  92.8 23.4 %all-to-all-start.4 = ((bf16[16,2,1,512]{3,1,2,0:T(2,128)(2,1)}), bf16[16,2,1,512]{3,1,2,0:T(2,128)(2,1)S(1)}, u32[]{:S(2)}, u32[]{:S(2)}) async-start(bf16[16,2,1,512]{3,1,2,0:T(2,128)(2,1)} %broadcast_in_dim.237), calls=%async_computation.4 | async-start | bytes 65536 | tf_op jit(solution)/shard_map/all_to_all | solution.py:60
  116.8 8.2 %all-to-all-start.5 = ((bf16[4,2,16,512]{3,2,1,0:T(8,128)(2,1)}), bf16[4,2,16,512]{3,2,1,0:T(8,128)(2,1)S(1)}, u32[]{:S(2)}, u32[]{:S(2)}) async-start(bf16[4,2,16,512]{3,2,1,0:T(8,128)(2,1)} %broadcast_in_dim.239), calls=%async_computation.5 | async-start | bytes 262144 | tf_op jit(solution)/shard_map/all_to_all | solution.py:60
  120.2 152.2 %reduce-scatter.2.cloned.1.call-start = ((), (), s32[]{:S(2)}) async-start(), calls=%async_computation.15 | async-start | bytes 8912896 | tf_op jit(solution)/shard_map/reduce_scatter | solution.py:635
  163.5 0.7 copy-start.7
  164.8 20.0 %all-to-all-start.7 = ((f32[16,3,128]{2,1,0:T(4,128)}), f32[16,3,128]{2,1,0:T(4,128)S(1)}, u32[]{:S(2)}, u32[]{:S(2)}) async-start(f32[16,3,128]{2,1,0:T(4,128)} %broadcast_in_dim.243), calls=%async_computation.7 | async-start | bytes 65536 | tf_op jit(solution)/shard_map/all_to_all | solution.py:60
  185.5 7.9 %all-to-all-start.8 = ((f32[4,16,3,128]{3,1,2,0:T(8,128)}), f32[4,16,3,128]{3,1,2,0:T(8,128)S(1)}, u32[]{:S(2)}, u32[]{:S(2)}) async-start(f32[4,16,3,128]{3,1,2,0:T(8,128)} %broadcast_in_dim.244), calls=%async_computation.8 | async-start | bytes 196608 | tf_op jit(solution)/shard_map/all_to_all | solution.py:60
  203.4 56.2 %copy-start.2 = (f32[1024,256]{1,0:T(8,128)S(1)}, f32[1024,256]{1,0:T(8,128)}, u32[]{:S(2)}) copy-start(f32[1024,256]{1,0:T(8,128)} %get-tuple-element.51) | copy-start | bytes 3145732
  226.9 15.4 %all-to-all-start.11 = ((bf16[16,4,256]{2,1,0:T(4,128)(2,1)}), bf16[16,4,256]{2,1,0:T(4,128)(2,1)S(1)}, u32[]{:S(2)}, u32[]{:S(2)}) async-start(bf16[16,4,256]{2,1,0:T(4,128)(2,1)} %broadcast_in_dim.245), calls=%async_computation.11 | async-start | bytes 65536 | tf_op jit(solution)/shard_map/all_to_all | solution.py:60
  230.4 29.2 %collective-permute-start.3 = (bf16[1024,256]{1,0:T(8,128)(2,1)}, bf16[1024,256]{1,0:T(8,128)(2,1)S(1)}, u32[]{:S(2)}, u32[]{:S(2)}) collective-permute-start(bf16[1024,256]{1,0:T(8,128)(2,1)} %get-tuple-element.52), channel_id=1, source_target_pairs={{0,24},{8,0},{16,8},{24,16},{1,25},{9,1},{17,9},{25,17},{2,26},{10... | collective-permute-start | bytes 1572872 | tf_op jit(solution)/shard_map/ppermute | solution.py:636
  233.2 26.4 %collective-permute-start.4 = (bf16[1024,256]{1,0:T(8,128)(2,1)}, bf16[1024,256]{1,0:T(8,128)(2,1)S(1)}, u32[]{:S(2)}, u32[]{:S(2)}) collective-permute-start(bf16[1024,256]{1,0:T(8,128)(2,1)} %get-tuple-element.53), channel_id=1, source_target_pairs={{0,16},{8,24},{16,0},{24,8},{1,17},{9,25},{17,1},{25,9},{2,18},{10... | collective-permute-start | bytes 1572872 | tf_op jit(solution)/shard_map/ppermute | solution.py:636
  236.7 22.9 %collective-permute-start.5 = (bf16[1024,256]{1,0:T(8,128)(2,1)}, bf16[1024,256]{1,0:T(8,128)(2,1)}, u32[]{:S(2)}, u32[]{:S(2)}) collective-permute-start(bf16[1024,256]{1,0:T(8,128)(2,1)} %get-tuple-element.54), channel_id=1, source_target_pairs={{0,8},{8,16},{16,24},{24,0},{1,9},{9,17},{17,25},{25,1},{2,10},{10... | collective-permute-start | bytes 1572872 | tf_op jit(solution)/shard_map/ppermute | solution.py:636
  242.9 15.0 %all-to-all-start.12 = ((bf16[4,64,256]{2,1,0:T(8,128)(2,1)}), bf16[4,64,256]{2,1,0:T(8,128)(2,1)S(1)}, u32[]{:S(2)}, u32[]{:S(2)}) async-start(bf16[4,64,256]{2,1,0:T(8,128)(2,1)} %broadcast_in_dim.247), calls=%async_computation.12 | async-start | bytes 262144 | tf_op jit(solution)/shard_map/all_to_all | solution.py:60
Sparse Core Ops, SparseCore 0:
  28.8 107.2 all-gather.1
  163.7 108.6 reduce-scatter.1
